TPU v7x, 32 devices: a whole 2x2x4 slice. The times are simulated.
32 devices in a mesh: rep: 8 (over z, core), shard: 4 (over y, x).
Axes of the slice: x: 2, y: 2, z: 4, core: 2. Of those that a mesh axis runs over, the one named last changes fastest.
Arguments:
- tokens: bfloat16 [4096, 1536], P(('rep', 'shard')), may hold values from -6 to 6
- cotangent: bfloat16 [4096, 1536], P(('rep', 'shard')), may hold values from -6 to 6
- lengths: int32 [8], P('rep'), may hold values from 128 to 512, as said below
- gain_one: bfloat16 [1536], P('shard'), may hold values from 0.5 to 1.5
- w_query: bfloat16 [1536, 1536], P('shard'), may hold values from -0.15625 to 0.15625
- w_key: bfloat16 [1536, 1536], P('shard'), may hold values from -0.15625 to 0.15625
- w_value: bfloat16 [1536, 1536], P('shard'), may hold values from -0.15625 to 0.15625
- w_path: bfloat16 [1536, 1536], P('shard'), may hold values from -0.15625 to 0.15625
- w_beta: bfloat16 [1536, 12], P('shard'), may hold values from -0.15625 to 0.15625
- w_out: bfloat16 [1536, 1536], P('shard'), may hold values from -0.625 to 0.625
- gain_two: bfloat16 [1536], P('shard'), may hold values from 0.5 to 1.5
- w_gate: bfloat16 [1536, 4096], P('shard'), may hold values from -0.15625 to 0.15625
- w_up: bfloat16 [1536, 4096], P('shard'), may hold values from -0.15625 to 0.15625
- w_down: bfloat16 [4096, 1536], P('shard'), may hold values from -0.09375 to 0.09375
Outputs:
- output: bfloat16 [4096, 1536], P(('rep', 'shard'))
- input_grad: bfloat16 [4096, 1536], P(('rep', 'shard'))
- grad_gain_one: float32 [1536], P('shard')
- grad_w_query: float32 [1536, 1536], P('shard')
- grad_w_key: float32 [1536, 1536], P('shard')
- grad_w_value: float32 [1536, 1536], P('shard')
- grad_w_path: float32 [1536, 1536], P('shard')
- grad_w_beta: float32 [1536, 12], P('shard')
- grad_w_out: float32 [1536, 1536], P('shard')
- grad_gain_two: float32 [1536], P('shard')
- grad_w_gate: float32 [1536, 4096], P('shard')
- grad_w_up: float32 [1536, 4096], P('shard')
- grad_w_down: float32 [4096, 1536], P('shard')
- rms_input: float32 [], replicated
- rms_attn: float32 [], replicated
- rms_feed: float32 [], replicated
Inputs may be any that keep to these rules, and one draw needn't show every extreme that they name: Sequence r fills the first lengths[r] of its 512 slots; at least one sequence fills all of them.
All inputs are finite; a program needn't handle non-finite values.
Results may differ from a plain program's by a relative error of at most 0.02.
Values may be sent and summed in bfloat16 or wider, within the bound.
No kernel may reach another device: no remote copies, remote signals or barrier semaphores. Data moves between devices by JAX's collectives and lax.ppermute only.
A program may use at most 320 MiB of HBM per device.

v0:
```python
import jax
import jax.numpy as jnp
from jax import lax
from jax.sharding import PartitionSpec as P

eps = 1e-06
highest = lax.Precision.HIGHEST


def rms_norm(value, gain_vec):
    factor = lax.rsqrt(jnp.mean(value * value, axis=-1, keepdims=True) + eps)
    return value * factor * gain_vec


def unit_rows(raw):
    return raw * lax.rsqrt(jnp.sum(raw * raw, axis=-1, keepdims=True) + eps)


def rounded(value):
    return lax.optimization_barrier(value.astype(jnp.bfloat16)).astype(jnp.float32)


def round_pass(value):
    return value + lax.stop_gradient(rounded(value) - value)


def split_heads(matrix, head_count):
    return matrix.reshape(matrix.shape[0], head_count, -1).transpose(1, 0, 2)


def join_heads(matrix):
    return matrix.transpose(1, 0, 2).reshape(matrix.shape[1], -1)


def mul_low(left, right):
    return jnp.dot(left, right, preferred_element_type=jnp.float32)


def back_mul(grad_rows, weight):
    return jnp.einsum("tg,fg->tf", grad_rows, weight, preferred_element_type=jnp.float32)


def weight_grad(left, right):
    return jnp.einsum("tf,tg->fg", left, right, preferred_element_type=jnp.float32)


def masks(block_len):
    row_ids = jnp.arange(block_len)[:, None]
    col_ids = jnp.arange(block_len)[None, :]
    return (col_ids < row_ids, col_ids <= row_ids)


def block_system(direction, beta_rate):
    block_len = direction.shape[1]
    strictly, up_to = masks(block_len)
    gram = jnp.einsum("htd,hsd->hts", direction, direction, precision=highest)
    return jnp.eye(block_len, dtype=jnp.float32)[None] + jnp.where(
        strictly[None], gram * beta_rate[:, None, :], 0.0
    )


def own_context(keyset, values, direction, beta_rate):
    system = block_system(direction, beta_rate)
    strictly, up_to = masks(keyset.shape[1])
    coupled = jnp.where(
        strictly[None], jnp.einsum("htd,hjd->htj", direction, keyset, precision=highest), 0.0
    )
    solved = jax.scipy.linalg.solve_triangular(system, coupled, lower=True, unit_diagonal=True)
    scaled_dir = direction * beta_rate[:, :, None]
    key_end = keyset - jnp.einsum("htj,htd->hjd", solved, scaled_dir, precision=highest)
    through = jax.scipy.linalg.solve_triangular(system, direction, lower=True, unit_diagonal=True)
    block_map = jnp.eye(direction.shape[2], dtype=jnp.float32)[None] - jnp.einsum(
        "htm,htn->hmn", scaled_dir, through, precision=highest
    )
    return (join_heads(key_end), join_heads(values), block_map[None])


def attend(
    queries, keyset, values, direction, beta_rate, key_far, value_far, maps_far, my_block, length
):
    head_count, block_len, head_width = queries.shape
    blocks = maps_far.shape[0]
    score_scale = head_width ** (-0.5)
    strictly, up_to = masks(block_len)
    system = block_system(direction, beta_rate)
    coupled = jnp.where(
        strictly[None], jnp.einsum("htd,hjd->htj", direction, keyset, precision=highest), 0.0
    )
    solved = jax.scipy.linalg.solve_triangular(system, coupled, lower=True, unit_diagonal=True)
    crossing = (
        jnp.where(
            up_to[None], jnp.einsum("hid,htd->hit", queries, direction, precision=highest), 0.0
        )
        * beta_rate[:, None, :]
    )
    near_scores = (
        jnp.einsum("hid,hjd->hij", queries, keyset, precision=highest)
        - jnp.einsum("hit,htj->hij", crossing, solved, precision=highest)
    ) * score_scale
    back_solved = jax.scipy.linalg.solve_triangular(
        system, crossing.transpose(0, 2, 1), lower=True, trans=1, unit_diagonal=True
    )
    moved = queries - jnp.einsum("hti,htd->hid", back_solved, direction, precision=highest)

    def advance(carried, item_pair):
        block_map, index = item_pair
        updated = jnp.einsum("hid,hde->hie", carried, block_map, precision=highest)
        return (jnp.where(index < my_block, updated, carried), carried)

    unused, reached = lax.scan(advance, moved, (maps_far, jnp.arange(blocks)), reverse=True)
    far_keys = key_far.reshape(blocks, block_len, head_count, head_width)
    far_values = value_far.reshape(blocks, block_len, head_count, head_width)
    far_scores = jnp.einsum("ehid,ejhd->ehij", reached, far_keys, precision=highest) * score_scale
    positions = jnp.arange(block_len)
    near_ok = up_to[None] & ((my_block * block_len + positions)[None, None, :] < length)
    block_ids = jnp.arange(blocks)
    far_ok = (block_ids[:, None, None, None] < my_block) & (
        (block_ids[:, None] * block_len + positions[None, :])[:, None, None, :] < length
    )
    near_masked = jnp.where(near_ok, near_scores, -1e30)
    far_masked = jnp.where(far_ok, far_scores, -1e30)
    row_max = jnp.maximum(jnp.max(near_masked, axis=2), jnp.max(far_masked, axis=(0, 3)))[
        :, :, None
    ]
    row_total = jnp.sum(jnp.where(near_ok, jnp.exp(near_masked - row_max), 0.0), axis=2) + jnp.sum(
        jnp.where(far_ok, jnp.exp(far_masked - row_max[None]), 0.0), axis=(0, 3)
    )
    log_total = row_max + jnp.log(row_total)[:, :, None]
    near_probs = round_pass(jnp.where(near_ok, jnp.exp(near_masked - log_total), 0.0))
    far_probs = round_pass(jnp.where(far_ok, jnp.exp(far_masked - log_total[None]), 0.0))
    return jnp.einsum("hij,hjd->hid", near_probs, values, precision=highest) + jnp.einsum(
        "ehij,ejhd->hid", far_probs, far_values, precision=highest
    )


def per_device(
    tokens,
    cotangent,
    lengths,
    gain_one,
    w_query,
    w_key,
    w_value,
    w_path,
    w_beta,
    w_out,
    gain_two,
    w_gate,
    w_up,
    w_down,
):
    gain_a, query_w, key_w, value_w, path_w, beta_w, out_w, gain_b, gate_w, up_w, down_w = (
        lax.all_gather(gain_one, "shard", axis=0, tiled=True),
        lax.all_gather(w_query, "shard", axis=0, tiled=True),
        lax.all_gather(w_key, "shard", axis=0, tiled=True),
        lax.all_gather(w_value, "shard", axis=0, tiled=True),
        lax.all_gather(w_path, "shard", axis=0, tiled=True),
        lax.all_gather(w_beta, "shard", axis=0, tiled=True),
        lax.all_gather(w_out, "shard", axis=0, tiled=True),
        lax.all_gather(gain_two, "shard", axis=0, tiled=True),
        lax.all_gather(w_gate, "shard", axis=0, tiled=True),
        lax.all_gather(w_up, "shard", axis=0, tiled=True),
        lax.all_gather(w_down, "shard", axis=0, tiled=True),
    )
    block_len = tokens.shape[0]
    width = tokens.shape[1]
    head_count = beta_w.shape[1]
    my_block = lax.axis_index("shard")
    length = lengths[0]
    live_mask = (my_block * block_len + jnp.arange(block_len) < length).astype(jnp.float32)[:, None]
    stream_in = tokens.astype(jnp.float32)
    normed_f, norm_pull = jax.vjp(rms_norm, stream_in, gain_a.astype(jnp.float32))
    normed = normed_f.astype(jnp.bfloat16)
    queries = split_heads(rounded(mul_low(normed, query_w)), head_count)
    keyset = split_heads(rounded(mul_low(normed, key_w)), head_count)
    values_h = split_heads(rounded(mul_low(normed, value_w)), head_count)
    raw = mul_low(normed, path_w).reshape(block_len, head_count, -1)
    direction_f, unit_pull = jax.vjp(unit_rows, raw)
    direction = rounded(direction_f).transpose(1, 0, 2)
    beta_rate = 2.0 * jax.nn.sigmoid(mul_low(normed, beta_w))
    (key_end, value_own, map_own), context_pull = jax.vjp(
        own_context, keyset, values_h, direction, beta_rate.T
    )
    key_far, value_far, maps_far = (
        lax.all_gather(key_end.astype(jnp.bfloat16), "shard", axis=0, tiled=True).astype(
            key_end.dtype
        ),
        lax.all_gather(value_own.astype(jnp.bfloat16), "shard", axis=0, tiled=True).astype(
            value_own.dtype
        ),
        lax.all_gather(map_own.astype(jnp.bfloat16), "shard", axis=0, tiled=True).astype(
            map_own.dtype
        ),
    )

    def local_attend(
        queries, keyset, values_h, direction, beta_heads, key_far, value_far, maps_far
    ):
        return attend(
            queries,
            keyset,
            values_h,
            direction,
            beta_heads,
            key_far,
            value_far,
            maps_far,
            my_block,
            length,
        )

    heads_out, attend_pull = jax.vjp(
        local_attend,
        queries,
        keyset,
        values_h,
        direction,
        beta_rate.T,
        key_far,
        value_far,
        maps_far,
    )
    mixed = join_heads(heads_out).astype(jnp.bfloat16)
    attn_out = mul_low(mixed, out_w)
    stream = stream_in + live_mask * attn_out
    normed_two_f, norm_two_pull = jax.vjp(rms_norm, stream, gain_b.astype(jnp.float32))
    normed_two = normed_two_f.astype(jnp.bfloat16)
    gate_pre = mul_low(normed_two, gate_w)
    up_pre = mul_low(normed_two, up_w)
    gate_sig = jax.nn.sigmoid(gate_pre)
    hidden = (gate_pre * gate_sig * up_pre).astype(jnp.bfloat16)
    feed_out = mul_low(hidden, down_w)
    output = (live_mask * (stream + feed_out)).astype(jnp.bfloat16)
    cot_rows = cotangent.astype(jnp.float32) * live_mask
    d_feed = cot_rows.astype(jnp.bfloat16)
    d_hidden = back_mul(d_feed, down_w)
    d_gate = (d_hidden * up_pre * gate_sig * (1.0 + gate_pre * (1.0 - gate_sig))).astype(
        jnp.bfloat16
    )
    d_up = (d_hidden * gate_pre * gate_sig).astype(jnp.bfloat16)
    d_normed_two = back_mul(d_gate, gate_w) + back_mul(d_up, up_w)
    d_stream_norm, grad_gain_b = norm_two_pull(d_normed_two)
    d_stream = cot_rows + d_stream_norm
    d_attn = (live_mask * d_stream).astype(jnp.bfloat16)
    d_mixed = split_heads(rounded(back_mul(d_attn, out_w)), head_count)
    (
        d_queries,
        d_keys_near,
        d_values_near,
        d_dir_near,
        d_beta_near,
        d_key_far,
        d_value_far,
        d_maps_far,
    ) = attend_pull(d_mixed)
    d_key_end, d_value_own, d_map_own = (
        lax.psum_scatter(
            d_key_far.astype(jnp.bfloat16), "shard", scatter_dimension=0, tiled=True
        ).astype(jnp.float32),
        lax.psum_scatter(
            d_value_far.astype(jnp.bfloat16), "shard", scatter_dimension=0, tiled=True
        ).astype(jnp.float32),
        lax.psum_scatter(
            d_maps_far.astype(jnp.bfloat16), "shard", scatter_dimension=0, tiled=True
        ).astype(jnp.float32),
    )
    d_keys_ctx, d_values_ctx, d_dir_ctx, d_beta_ctx = context_pull(
        (d_key_end, d_value_own, d_map_own)
    )
    d_query_b = join_heads(d_queries).astype(jnp.bfloat16)
    d_key_b = join_heads(d_keys_near + d_keys_ctx).astype(jnp.bfloat16)
    d_value_b = join_heads(d_values_near + d_values_ctx).astype(jnp.bfloat16)
    (d_raw,) = unit_pull((d_dir_near + d_dir_ctx).transpose(1, 0, 2))
    d_raw_b = d_raw.reshape(block_len, -1).astype(jnp.bfloat16)
    d_beta_total = (d_beta_near + d_beta_ctx).T
    d_logit_b = (d_beta_total * beta_rate * (1.0 - 0.5 * beta_rate)).astype(jnp.bfloat16)
    d_normed = (
        back_mul(d_query_b, query_w)
        + back_mul(d_key_b, key_w)
        + back_mul(d_value_b, value_w)
        + back_mul(d_raw_b, path_w)
        + back_mul(d_logit_b, beta_w)
    )
    d_stream_in, grad_gain_a = norm_pull(d_normed)
    input_grad = (d_stream_in + d_stream).astype(jnp.bfloat16)
    g_query = weight_grad(normed, d_query_b)
    g_key = weight_grad(normed, d_key_b)
    g_value = weight_grad(normed, d_value_b)
    g_path = weight_grad(normed, d_raw_b)
    g_beta = weight_grad(normed, d_logit_b)
    g_out = weight_grad(mixed, d_attn)
    g_gate = weight_grad(normed_two, d_gate)
    g_up = weight_grad(normed_two, d_up)
    g_down = weight_grad(hidden, d_feed)
    part_sums = (
        lax.psum_scatter(
            grad_gain_a.astype(jnp.bfloat16), "shard", scatter_dimension=0, tiled=True
        ).astype(jnp.float32),
        lax.psum_scatter(
            g_query.astype(jnp.bfloat16), "shard", scatter_dimension=0, tiled=True
        ).astype(jnp.float32),
        lax.psum_scatter(
            g_key.astype(jnp.bfloat16), "shard", scatter_dimension=0, tiled=True
        ).astype(jnp.float32),
        lax.psum_scatter(
            g_value.astype(jnp.bfloat16), "shard", scatter_dimension=0, tiled=True
        ).astype(jnp.float32),
        lax.psum_scatter(
            g_path.astype(jnp.bfloat16), "shard", scatter_dimension=0, tiled=True
        ).astype(jnp.float32),
        lax.psum_scatter(
            g_beta.astype(jnp.bfloat16), "shard", scatter_dimension=0, tiled=True
        ).astype(jnp.float32),
        lax.psum_scatter(
            g_out.astype(jnp.bfloat16), "shard", scatter_dimension=0, tiled=True
        ).astype(jnp.float32),
        lax.psum_scatter(
            grad_gain_b.astype(jnp.bfloat16), "shard", scatter_dimension=0, tiled=True
        ).astype(jnp.float32),
        lax.psum_scatter(
            g_gate.astype(jnp.bfloat16), "shard", scatter_dimension=0, tiled=True
        ).astype(jnp.float32),
        lax.psum_scatter(
            g_up.astype(jnp.bfloat16), "shard", scatter_dimension=0, tiled=True
        ).astype(jnp.float32),
        lax.psum_scatter(
            g_down.astype(jnp.bfloat16), "shard", scatter_dimension=0, tiled=True
        ).astype(jnp.float32),
    )
    owned = (
        lax.psum(part_sums[0].astype(jnp.bfloat16), "rep").astype(jnp.float32),
        lax.psum(part_sums[1].astype(jnp.bfloat16), "rep").astype(jnp.float32),
        lax.psum(part_sums[2].astype(jnp.bfloat16), "rep").astype(jnp.float32),
        lax.psum(part_sums[3].astype(jnp.bfloat16), "rep").astype(jnp.float32),
        lax.psum(part_sums[4].astype(jnp.bfloat16), "rep").astype(jnp.float32),
        lax.psum(part_sums[5].astype(jnp.bfloat16), "rep").astype(jnp.float32),
        lax.psum(part_sums[6].astype(jnp.bfloat16), "rep").astype(jnp.float32),
        lax.psum(part_sums[7].astype(jnp.bfloat16), "rep").astype(jnp.float32),
        lax.psum(part_sums[8].astype(jnp.bfloat16), "rep").astype(jnp.float32),
        lax.psum(part_sums[9].astype(jnp.bfloat16), "rep").astype(jnp.float32),
        lax.psum(part_sums[10].astype(jnp.bfloat16), "rep").astype(jnp.float32),
    )
    sq_input, sq_attn, sq_feed, live_total = lax.psum(
        (
            jnp.sum(live_mask * stream_in * stream_in),
            jnp.sum(live_mask * attn_out * attn_out),
            jnp.sum(live_mask * feed_out * feed_out),
            jnp.sum(live_mask),
        ),
        ("rep", "shard"),
    )
    denom = live_total * width
    return (
        output,
        input_grad,
        owned[0],
        owned[1],
        owned[2],
        owned[3],
        owned[4],
        owned[5],
        owned[6],
        owned[7],
        owned[8],
        owned[9],
        owned[10],
        jnp.sqrt(sq_input / denom),
        jnp.sqrt(sq_attn / denom),
        jnp.sqrt(sq_feed / denom),
    )


def solution(mesh):
    return jax.shard_map(
        per_device,
        mesh=mesh,
        in_specs=(
            P(("rep", "shard"), None),
            P(("rep", "shard"), None),
            P("rep"),
            P("shard"),
            P("shard", None),
            P("shard", None),
            P("shard", None),
            P("shard", None),
            P("shard", None),
            P("shard", None),
            P("shard"),
            P("shard", None),
            P("shard", None),
            P("shard", None),
        ),
        out_specs=(
            P(("rep", "shard"), None),
            P(("rep", "shard"), None),
            P("shard"),
            P("shard", None),
            P("shard", None),
            P("shard", None),
            P("shard", None),
            P("shard", None),
            P("shard", None),
            P("shard"),
            P("shard", None),
            P("shard", None),
            P("shard", None),
            P(),
            P(),
            P(),
        ),
        check_vma=False,
    )
```

profile of v0, /device:TPU:0, one launch (start us, length us, event | category | flops | bytes accessed | tf_op | source)
XLA Modules:
  0.0 1988.5 jit_solution(15971856994298718647)
XLA Ops:
  10.1 9.5 all-gather.1
  19.6 8.5 all_gather.46
  29.4 40.5 %all-gather.19.cloned.1.call-done = bf16[1536,1536]{1,0:T(8,128)(2,1)} async-done(((bf16[384,1536]{1,0:T(8,128)(2,1)}), bf16[1536,1536]{1,0:T(8,128)(2,1)}) %all-gather.19.cloned.1.call-update) | async-done | bytes 4718608 | tf_op jit(solution)/shard_map/all_gather | solution.py:157
  69.9 4.3 fusion.196
  76.4 117.9 %custom-call.16 = f32[12,1,128,128]{2,3,1,0:T(8,128)S(1)} custom-call(f32[12,1,128,128]{3,2,1,0:T(8,128)S(1)} %add_bitcast_fusion), custom_call_target="InvertDiagBlocksLowerTriangular" | custom-call | tf_op jit(solution)/shard_map/jvp(jit(_solve_triangular))/vmap()/triangular_solve/custom-call.1 | solution.py:89
  199.4 3.6 convolution_convert_fusion.10
  207.4 3.9 convolution_convert_fusion.9
  216.0 8.1 all-gather.2
  228.1 20.2 %all-gather.15.cloned.1.call-done = bf16[1536,1536]{1,0:T(8,128)(2,1)} async-done(((bf16[384,1536]{1,0:T(8,128)(2,1)}), bf16[1536,1536]{1,0:T(8,128)(2,1)}) %all-gather.15.cloned.1.call-update) | async-done | bytes 4718608 | tf_op jit(solution)/shard_map/all_gather | solution.py:154
  263.0 18.5 all-gather.35.cloned.1.call-done
  285.0 29.7 %all-gather.21.cloned.1.call-done = bf16[512,1536]{0,1:T(8,128)(2,1)} async-done(((bf16[128,1536]{0,1:T(8,128)(2,1)}), bf16[512,1536]{0,1:T(8,128)(2,1)}) %all-gather.21.cloned.1.call-update) | async-done | bytes 1572880 | tf_op jit(solution)/shard_map/all_gather | solution.py:185
  321.8 19.7 while.31
  342.1 4.6 fusion.201
  353.4 3.5 reshape.355
  359.3 3.9 copy.212
  371.0 36.0 %all-gather.27.cloned.1.call-done = bf16[1536,1536]{1,0:T(8,128)(2,1)} async-done(((bf16[384,1536]{1,0:T(8,128)(2,1)}), bf16[1536,1536]{1,0:T(8,128)(2,1)}) %all-gather.27.cloned.1.call-update) | async-done | bytes 4718608 | tf_op jit(solution)/shard_map/all_gather | solution.py:159
  407.0 4.3 multiply_reduce_fusion.6
  413.2 118.2 %all-gather.29.cloned.1.call-done = bf16[1536,4096]{1,0:T(8,128)(2,1)} async-done(((bf16[384,4096]{1,0:T(8,128)(2,1)}), bf16[1536,4096]{1,0:T(8,128)(2,1)}) %all-gather.29.cloned.1.call-update) | async-done | bytes 12582928 | tf_op jit(solution)/shard_map/all_gather | solution.py:161
  531.4 7.8 fusion.203
  539.3 116.4 %all-gather.31.cloned.1.call-done = bf16[1536,4096]{1,0:T(8,128)(2,1)} async-done(((bf16[384,4096]{1,0:T(8,128)(2,1)}), bf16[1536,4096]{1,0:T(8,128)(2,1)}) %all-gather.31.cloned.1.call-update) | async-done | bytes 12582928 | tf_op jit(solution)/shard_map/all_gather | solution.py:162
  655.7 7.8 fusion.204
  663.5 116.5 %all-gather.33.cloned.1.call-done = bf16[4096,1536]{1,0:T(8,128)(2,1)} async-done(((bf16[1024,1536]{1,0:T(8,128)(2,1)}), bf16[4096,1536]{1,0:T(8,128)(2,1)}) %all-gather.33.cloned.1.call-update) | async-done | bytes 12582928 | tf_op jit(solution)/shard_map/all_gather | solution.py:163
  780.1 10.2 multiply_convert_fusion
  790.4 10.2 fusion.205
  800.7 9.7 multiply_reduce_fusion
  810.4 8.0 fusion.81
  832.8 8.0 fusion.31
  843.5 4.9 fusion.28
  848.4 4.4 copy.337
  856.2 8.4 fusion.188
  864.6 41.8 %while.32 = (s32[]{:T(128)}, f32[12,128,128]{2,1,0:T(8,128)}, bf16[4,12,128,128]{3,2,1,0:T(8,128)(2,1)}, f32[4,12,128,128]{3,2,1,0:T(8,128)}, pred[4]{0:T(512)(1...) while((s32[]{:T(128)}, f32[12,128,128]{2,1,0:T(8,128)}, ...), condition=%wide.region_16.19_spmd.clone, body=%wide.region_15.18_spmd.clone.sunk | while | flops 605552640 | bytes 7869556 | solution.py:110
  866.9 3.5 fusion.311
  870.3 4.7 convolution_add_fusion.20
  877.4 3.4 fusion.311
  880.8 4.6 convolution_add_fusion.20
  887.8 3.5 fusion.311
  891.3 4.7 convolution_add_fusion.20
  898.3 3.5 fusion.311
  901.8 4.6 convolution_add_fusion.20
  919.8 3.7 convolution_convert_fusion.7
  923.6 4.8 convolution_convert_fusion.3
  948.0 3.7 convolution_convert_fusion.6
  956.6 4.3 convolution_convert_fusion.5
  993.1 3.6 convolution_convert_fusion.4
  998.1 6.5 convolution_convert_fusion.2
  1005.8 6.4 convolution_convert_fusion.1
  1013.6 6.7 convolution_convert_fusion
  1022.4 41.7 %reduce-scatter.29.cloned.1.call-done = bf16[384,1536]{1,0:T(8,128)(2,1)} async-done(((bf16[1536,1536]{1,0:T(8,128)(2,1)}), bf16[384,1536]{1,0:T(8,128)(2,1)}) %reduce-scatter.29.cloned.1.call-update) | async-done | bytes 1179664 | tf_op jit(solution)/shard_map/reduce_scatter | solution.py:314
  1064.0 60.5 %reduce-scatter.23.cloned.1.call-done = bf16[384,1536]{1,0:T(8,128)(2,1)} async-done(((bf16[1536,1536]{1,0:T(8,128)(2,1)}), bf16[384,1536]{1,0:T(8,128)(2,1)}) %reduce-scatter.23.cloned.1.call-update) | async-done | bytes 1179664 | tf_op jit(solution)/shard_map/reduce_scatter | solution.py:302
  1124.6 60.6 %reduce-scatter.25.cloned.1.call-done = bf16[384,1536]{1,0:T(8,128)(2,1)} async-done(((bf16[1536,1536]{1,0:T(8,128)(2,1)}), bf16[384,1536]{1,0:T(8,128)(2,1)}) %reduce-scatter.25.cloned.1.call-update) | async-done | bytes 1179664 | tf_op jit(solution)/shard_map/reduce_scatter | solution.py:305
  1185.1 60.1 %reduce-scatter.27.cloned.1.call-done = bf16[384,1536]{1,0:T(8,128)(2,1)} async-done(((bf16[1536,1536]{1,0:T(8,128)(2,1)}), bf16[384,1536]{1,0:T(8,128)(2,1)}) %reduce-scatter.27.cloned.1.call-update) | async-done | bytes 1179664 | tf_op jit(solution)/shard_map/reduce_scatter | solution.py:308
  1245.2 123.7 %reduce-scatter.31.cloned.1.call-done = bf16[384,4096]{1,0:T(8,128)(2,1)} async-done(((bf16[1536,4096]{1,0:T(8,128)(2,1)}), bf16[384,4096]{1,0:T(8,128)(2,1)}) %reduce-scatter.31.cloned.1.call-update) | async-done | bytes 3145744 | tf_op jit(solution)/shard_map/reduce_scatter | solution.py:320
  1368.9 123.9 %reduce-scatter.33.cloned.1.call-done = bf16[384,4096]{1,0:T(8,128)(2,1)} async-done(((bf16[1536,4096]{1,0:T(8,128)(2,1)}), bf16[384,4096]{1,0:T(8,128)(2,1)}) %reduce-scatter.33.cloned.1.call-update) | async-done | bytes 3145744 | tf_op jit(solution)/shard_map/reduce_scatter | solution.py:323
  1492.8 123.9 %reduce-scatter.35.cloned.1.call-done = bf16[1024,1536]{1,0:T(8,128)(2,1)} async-done(((bf16[4096,1536]{1,0:T(8,128)(2,1)}), bf16[1024,1536]{1,0:T(8,128)(2,1)}) %reduce-scatter.35.cloned.1.call-update) | async-done | bytes 3145744 | tf_op jit(solution)/shard_map/reduce_scatter | solution.py:326
  1618.6 4.2 fusion.206
  1622.8 4.1 convolution_add_fusion.4
  1626.9 4.0 convolution_add_fusion.3
  1633.7 40.3 %all-reduce.3 = (f32[]{:T(128)}, f32[]{:T(128)}, f32[]{:T(128)}, f32[]{:T(128)}) all-reduce(f32[]{:T(128)} %get-tuple-element.278, f32[]{:T(128)} %get-tuple-element.326, f32[]{:T(128)} %get-tuple-element.280, f32[]{:T(128)} %get-tuple-element.279), channel_id=1, replica_groups=mesh['rep'=8,'shard'=4] {'rep','shard'}, use_global_device_ids=true, to_apply=%region_52.55 | all-reduce | flops 4 | bytes 32 | tf_op jit(solution)/shard_map/psum | solution.py:343
  1674.0 10.8 all-reduce.6
  1689.7 28.2 %all-reduce.4 = (bf16[384]{0:T(512)(128)(2,1)S(1)}, bf16[384,12]{0,1:T(8,128)(2,1)S(1)}, bf16[384]{0:T(512)(128)(2,1)S(1)}) all-reduce(bf16[384]{0:T(512)(128)(2,1)S(1)} %dynamic-slice.3, bf16[384,12]{0,1:T(8,128)(2,1)S(1)} %copy.335, bf16[384]{0:T(512)(128)(2,1)S(1)} %dynamic-slice.5), channel_id=1, replica_groups=mesh['rep'=8,'shard'=4] {'rep'}, use_global_device_ids=true, to_apply=%region_29.32 | all-reduce | flops 5376 | bytes 21504 | tf_op jit(solution)/shard_map/psum | solution.py:331
  1719.6 238.0 %all-reduce.9.cloned.1.call-done = (bf16[384,1536]{1,0:T(8,128)(2,1)}, bf16[384,1536]{1,0:T(8,128)(2,1)}, bf16[384,1536]{1,0:T(8,128)(2,1)}, bf16[384,1536]{1,0:...) async-done(((bf16[384,1536]{1,0:T(8,128)(2,1)}, bf16[384,1536]{1,0:T(8,128)(2,1)}, ...) | async-done | bytes 15335440 | tf_op jit(solution)/shard_map/psum | solution.py:332
  1967.6 3.5 convert_element_type.336
  1971.0 3.5 convert_element_type.338
  1974.5 3.6 convert_element_type.340
  (513 shorter events, 207.9 us)
Async XLA Ops:
  7.2 12.4 copy-start.129
  7.2 21.0 %copy-start.2 = (bf16[128,1536]{1,0:T(8,128)(2,1)S(1)}, bf16[128,1536]{1,0:T(8,128)(2,1)}, u32[]{:S(2)}) copy-start(bf16[128,1536]{1,0:T(8,128)(2,1)} %param.22) | copy-start | bytes 1179652
  7.2 62.7 %all-gather.19.cloned.1.call-start = ((), (), s32[]{:S(2)}) async-start(), calls=%async_computation.14 | async-start | bytes 5898240 | tf_op jit(solution)/shard_map/all_gather | solution.py:157
  7.9 191.4 %all-gather.17.cloned.1.call-start = ((), (), s32[]{:S(2)}) async-start(), calls=%async_computation.13 | async-start | bytes 5898240 | tf_op jit(solution)/shard_map/all_gather | solution.py:155
  8.7 198.7 %all-gather.23.cloned.1.call-start = ((), (), s32[]{:S(2)}) async-start(), calls=%async_computation.16 | async-start | bytes 5898240 | tf_op jit(solution)/shard_map/all_gather | solution.py:156
  9.4 238.9 %all-gather.15.cloned.1.call-start = ((), (), s32[]{:S(2)}) async-start(), calls=%async_computation.12 | async-start | bytes 5898240 | tf_op jit(solution)/shard_map/all_gather | solution.py:154
  10.0 271.5 %all-gather.35.cloned.1.call-start = ((), (), s32[]{:S(2)}) async-start(), calls=%async_computation.30 | async-start | bytes 1966080 | tf_op jit(solution)/shard_map/all_gather | solution.py:191
  28.2 46.1 %copy-start.116 = (bf16[1536,12]{0,1:T(8,128)(2,1)}, bf16[1536,12]{0,1:T(8,128)(2,1)S(1)}, u32[]{:S(2)}) copy-start(bf16[1536,12]{0,1:T(8,128)(2,1)S(1)} %all_gather.46) | copy-start | bytes 110596
  29.0 170.4 %copy-start.108 = (f32[128]{0:T(128)}, f32[128]{0:T(128)S(1)}, u32[]{:S(2)}) copy-start(f32[128]{0:T(128)S(1)} %fusion.179) | copy-start | bytes 1540
  29.3 45.3 %copy-start.122 = (f32[128,12]{0,1:T(8,128)}, f32[128,12]{0,1:T(8,128)S(1)}, u32[]{:S(2)}) copy-start(f32[128,12]{0,1:T(8,128)S(1)} %fusion.67) | copy-start | bytes 18436
  29.4 46.0 %copy-start.84 = (pred[128,128]{1,0:T(8,128)(4,1)}, pred[128,128]{1,0:T(8,128)(4,1)S(1)}, u32[]{:S(2)}) copy-start(pred[128,128]{1,0:T(8,128)(4,1)S(1)} %get-tuple-element.356) | copy-start | bytes 49156
  29.4 46.0 %copy-start.88 = (pred[128,128]{1,0:T(8,128)(4,1)}, pred[128,128]{1,0:T(8,128)(4,1)S(1)}, u32[]{:S(2)}) copy-start(pred[128,128]{1,0:T(8,128)(4,1)S(1)} %get-tuple-element.355) | copy-start | bytes 49156
  74.6 124.3 %copy-start.114 = (f32[128,12]{0,1:T(8,128)}, f32[128,12]{0,1:T(8,128)S(1)}, u32[]{:S(2)}) copy-start(f32[128,12]{0,1:T(8,128)S(1)} %multiply_reduce_fusion.7) | copy-start | bytes 18436
  194.3 60.0 %copy-start = (f32[12,1,128,128]{2,3,1,0:T(8,128)}, f32[12,1,128,128]{2,3,1,0:T(8,128)S(1)}, u32[]{:S(2)}) copy-start(f32[12,1,128,128]{2,3,1,0:T(8,128)S(1)} %custom-call.16) | copy-start | bytes 2359300
  199.0 115.6 %all-gather.21.cloned.1.call-start = ((), (), s32[]{:S(2)}) async-start(), calls=%async_computation.15 | async-start | bytes 1966080 | tf_op jit(solution)/shard_map/all_gather | solution.py:185
  203.2 57.3 %copy-start.16 = (bf16[128,1536]{0,1:T(8,128)(2,1)}, bf16[128,1536]{0,1:T(8,128)(2,1)S(1)}, u32[]{:S(2)}) copy-start(bf16[128,1536]{0,1:T(8,128)(2,1)S(1)} %copy.185) | copy-start | bytes 1179652
  204.9 53.4 %copy-start.9 = (f32[12,128,128]{2,1,0:T(8,128)}, f32[12,128,128]{2,1,0:T(8,128)S(1)}, u32[]{:S(2)}) copy-start(f32[12,128,128]{2,1,0:T(8,128)S(1)} %fusion.105) | copy-start | bytes 2359300
  207.4 143.5 %all-gather.25.cloned.1.call-start = ((), (), s32[]{:S(2)}) async-start(), calls=%async_computation.17 | async-start | bytes 1966080 | tf_op jit(solution)/shard_map/all_gather | solution.py:188
  211.4 195.7 %all-gather.27.cloned.1.call-start = ((), (), s32[]{:S(2)}) async-start(), calls=%async_computation.18 | async-start | bytes 5898240 | tf_op jit(solution)/shard_map/all_gather | solution.py:159
  212.1 319.3 %all-gather.29.cloned.1.call-start = ((), (), s32[]{:S(2)}) async-start(), calls=%async_computation.19 | async-start | bytes 15728640 | tf_op jit(solution)/shard_map/all_gather | solution.py:161
  212.9 14.3 copy-start.61
  212.9 442.8 %all-gather.31.cloned.1.call-start = ((), (), s32[]{:S(2)}) async-start(), calls=%async_computation.20 | async-start | bytes 15728640 | tf_op jit(solution)/shard_map/all_gather | solution.py:162
  213.5 566.6 %all-gather.33.cloned.1.call-start = ((), (), s32[]{:S(2)}) async-start(), calls=%async_computation.21 | async-start | bytes 15728640 | tf_op jit(solution)/shard_map/all_gather | solution.py:163
  214.2 724.2 %reduce-scatter.37.cloned.1.call-start = ((), (), s32[]{:S(2)}) async-start(), calls=%async_computation.31 | async-start | bytes 1966080
  790.3 10.2 copy-start.53
  790.3 10.2 copy-start.51
  790.3 20.0 %copy-start.31 = (bf16[128,4096]{1,0:T(8,128)(2,1)}, bf16[128,4096]{1,0:T(8,128)(2,1)S(1)}, u32[]{:S(2)}) copy-start(bf16[128,4096]{1,0:T(8,128)(2,1)S(1)} %get-tuple-element.336) | copy-start | bytes 3145732
  790.3 10.2 copy-start.21
  790.4 10.2 copy-start.105
  790.4 10.2 copy-start.132
  800.6 9.8 copy-start.138
  800.6 9.8 copy-start.64
  800.6 9.8 copy-start.74
  800.6 9.8 copy-start.127
  800.6 18.8 slice-start.2
  810.4 9.0 slice-start.3
  829.2 11.6 copy-start.106
  832.8 8.0 copy-start.130
  843.5 108.3 %reduce-scatter.39.cloned.1.call-start = ((), (), s32[]{:S(2)}) async-start(), calls=%async_computation.32 | async-start | bytes 1966080
  856.0 116.3 %reduce-scatter.43.cloned.1.call-start = ((), (), s32[]{:S(2)}) async-start(), calls=%async_computation.34 | async-start | bytes 1966080
  906.5 115.9 %reduce-scatter.21.cloned.1.call-start = ((), (), s32[]{:S(2)}) async-start(), calls=%async_computation.22 | async-start | bytes 5898240 | tf_op jit(solution)/shard_map/reduce_scatter | solution.py:299
  923.5 140.5 %reduce-scatter.29.cloned.1.call-start = ((), (), s32[]{:S(2)}) async-start(), calls=%async_computation.26 | async-start | bytes 5898240 | tf_op jit(solution)/shard_map/reduce_scatter | solution.py:314
  928.4 196.2 %reduce-scatter.23.cloned.1.call-start = ((), (), s32[]{:S(2)}) async-start(), calls=%async_computation.23 | async-start | bytes 5898240 | tf_op jit(solution)/shard_map/reduce_scatter | solution.py:302
  940.4 6.3 copy-start.47
  940.4 6.3 copy-start.73
  940.4 7.7 copy-start.110
  951.7 233.4 %reduce-scatter.25.cloned.1.call-start = ((), (), s32[]{:S(2)}) async-start(), calls=%async_computation.24 | async-start | bytes 5898240 | tf_op jit(solution)/shard_map/reduce_scatter | solution.py:305
  960.9 284.3 %reduce-scatter.27.cloned.1.call-start = ((), (), s32[]{:S(2)}) async-start(), calls=%async_computation.25 | async-start | bytes 5898240 | tf_op jit(solution)/shard_map/reduce_scatter | solution.py:308
  961.2 6.7 copy-start.89
  963.3 6.3 copy-start.45
  963.4 6.3 copy-start.50
  963.4 6.3 copy-start.92
  975.1 5.6 copy-start.90
  996.8 372.2 %reduce-scatter.31.cloned.1.call-start = ((), (), s32[]{:S(2)}) async-start(), calls=%async_computation.27 | async-start | bytes 15728640 | tf_op jit(solution)/shard_map/reduce_scatter | solution.py:320
  1004.6 488.2 %reduce-scatter.33.cloned.1.call-start = ((), (), s32[]{:S(2)}) async-start(), calls=%async_computation.28 | async-start | bytes 15728640 | tf_op jit(solution)/shard_map/reduce_scatter | solution.py:323
  1012.2 604.5 %reduce-scatter.35.cloned.1.call-start = ((), (), s32[]{:S(2)}) async-start(), calls=%async_computation.29 | async-start | bytes 15728640 | tf_op jit(solution)/shard_map/reduce_scatter | solution.py:326
  1020.3 668.4 %reduce-scatter.41.cloned.1.call-start = ((), (), s32[]{:S(2)}) async-start(), calls=%async_computation.33 | async-start | bytes 491520
  1022.3 935.4 %all-reduce.9.cloned.1.call-start = ((), (), s32[]{:S(2)}) async-start(), calls=%async_computation.35 | async-start | bytes 30670848 | tf_op jit(solution)/shard_map/psum | solution.py:332
  1616.7 6.0 copy-start.60
  1618.6 12.3 slice-start
  1622.8 8.1 slice-start.1
  1630.9 43.0 %copy-start.126 = (bf16[1536]{0:T(1024)(128)(2,1)S(1)}, bf16[1536]{0:T(1024)(128)(2,1)}, u32[]{:S(2)}) copy-start(bf16[1536]{0:T(1024)(128)(2,1)} %get-tuple-element.270) | copy-start | bytes 9220
  1630.9 56.8 %copy-start.136 = (f32[128]{0:T(128)S(1)}, f32[128]{0:T(128)}, u32[]{:S(2)}) copy-start(f32[128]{0:T(128)} %copy-done.135) | copy-start | bytes 1540
  1630.9 56.8 %copy-start.23 = (f32[128,1536]{1,0:T(8,128)S(1)}, f32[128,1536]{1,0:T(8,128)}, u32[]{:S(2)}) copy-start(f32[128,1536]{1,0:T(8,128)} %copy-done.22) | copy-start | bytes 2359300
  (105 other events, 266.7 us)
Sparse Core Ops, SparseCore 0:
  9.9 60.0 all-gather.18
  71.8 58.0 all-gather.16
  131.7 57.6 all-gather.22
  191.1 57.1 all-gather.14
  250.5 30.9 all-gather.34
  283.8 30.8 all-gather.20
  317.1 30.9 all-gather.24
  349.9 57.0 all-gather.26
  408.9 122.5 all-gather.28
  533.1 122.5 all-gather.30
  657.5 122.5 all-gather.32
  843.6 30.9 reduce-scatter.36
  878.1 30.9 reduce-scatter.38
  912.5 30.9 reduce-scatter.42
  946.9 57.0 reduce-scatter.20
  1006.9 57.0 reduce-scatter.28
  1067.4 57.0 reduce-scatter.22
  1128.0 57.0 reduce-scatter.24
  1188.1 57.0 reduce-scatter.26
  1248.2 120.7 reduce-scatter.30
  1372.0 120.7 reduce-scatter.32
  1495.9 120.7 reduce-scatter.34
  1620.0 24.5 reduce-scatter.40
  1647.4 310.1 all-reduce.8
where the time goes:
time: 2000 us; the launch traced here: 1990 us
  waiting for transfers between devices  1330 us (66%)
  matrix products  278 us (14%)
  other arithmetic  163 us (8%)
  blocking collectives  105 us (5%)
  local copies, waits for them, and re-layouts  78.5 us (4%)
  between operations  24 us (1%)
    psum x1, waiting for transfers between devices, per_device(): lax.psum(part_sums[1].astype(jnp.bfloat16), 'rep').astype(jnp.float32)  238 us
    reduce_scatter x1, waiting for transfers between devices, per_device(): lax.psum_scatter(g_up.astype(jnp.bfloat16), 'shard', scatter_dimension=0,...  124 us
    reduce_scatter x1, waiting for transfers between devices, per_device(): lax.psum_scatter(g_down.astype(jnp.bfloat16), 'shard', scatter_dimension=...  124 us
    reduce_scatter x1, waiting for transfers between devices, per_device(): lax.psum_scatter(g_gate.astype(jnp.bfloat16), 'shard', scatter_dimension=...  124 us
    all_gather x1, waiting for transfers between devices, per_device(): lax.all_gather(w_gate, 'shard', axis=0, tiled=True)  118 us
    another operation x4, other arithmetic, attend(): jax.scipy.linalg.solve_triangular(system, coupled, lower=True, unit_diago...  118 us
    all_gather x1, waiting for transfers between devices, per_device(): lax.all_gather(w_down, 'shard', axis=0, tiled=True)  117 us
    all_gather x1, waiting for transfers between devices, per_device(): lax.all_gather(w_up, 'shard', axis=0, tiled=True)  116 us
  transfers between devices with their start and end apart: 24, of which 16 were waited for; matrix products, arithmetic and copies ran while one was open for 21% of the time, Pallas kernels for 0%

commit v1 on v0

--- a/solution.py
+++ b/solution.py
@@ -1,7 +1,14 @@
+import functools
+
 import jax
 import jax.numpy as jnp
 from jax import lax
+from jax.experimental import pallas as pl
+from jax.experimental.pallas import tpu as pltpu
 from jax.sharding import PartitionSpec as P
+
+f32 = jnp.float32
+bf16 = jnp.bfloat16
 
 eps = 1e-06
 highest = lax.Precision.HIGHEST
@@ -133,7 +140,7 @@
     )
 
 
-def per_device(
+def gathered_layer(
     tokens,
     cotangent,
     lengths,
@@ -370,9 +377,503 @@
     )
 
 
+def dot_nn(a,b): return lax.dot_general(a,b,(((1,),(0,)),((),())),preferred_element_type=f32)
+def dot_nt(a,b): return lax.dot_general(a,b,(((1,),(1,)),((),())),preferred_element_type=f32)
+def dot_tn(a,b): return lax.dot_general(a,b,(((0,),(0,)),((),())),preferred_element_type=f32)
+
+def halves(a):
+    hi=a.astype(bf16)
+    return hi,(a-hi.astype(f32)).astype(bf16)
+
+def mul3(dot,a,b):
+    return dot(a[0],b[0])+(dot(a[0],b[1])+dot(a[1],b[0]))
+
+def mul2(dot,a,b):
+    return dot(a[0],b)+dot(a[1],b)
+
+def iota2(n,ax): return lax.broadcasted_iota(jnp.int32,(n,n),ax)
+
+def tri_inverse(system, blk):
+    n=system.shape[0]
+    r=iota2(blk,0); c=iota2(blk,1)
+    eye=jnp.where(r==c,1.0,0.0)
+    outs=[]
+    tiles=[system[i*blk:(i+1)*blk,i*blk:(i+1)*blk] for i in range(n//blk)]
+    invs=[eye-jnp.where(((r>>1)==(c>>1))&((r&1)==1)&((c&1)==0),t,0.0) for t in tiles]
+    b=2
+    while b<blk:
+        m=((r//(2*b))==(c//(2*b)))&(((r//b)&1)==1)&(((c//b)&1)==0)
+        new=[]
+        for t,v in zip(tiles,invs):
+            vs=halves(v)
+            low=mul3(dot_nn,halves(jnp.where(m,t,0.0)),vs)
+            new.append(v-mul3(dot_nn,vs,halves(low)))
+        invs=new; b*=2
+    size=blk
+    while size<n:
+        new=[]
+        for i in range(0,len(invs),2):
+            a,d=invs[i],invs[i+1]
+            off=system[(i+1)*size:(i+2)*size,i*size:(i+1)*size]
+            low=mul3(dot_nn,halves(off),halves(a))
+            low=-mul3(dot_nn,halves(d),halves(low))
+            new.append(jnp.concatenate([jnp.concatenate([a,jnp.zeros_like(a)],1),jnp.concatenate([low,d],1)],0))
+        invs=new; size*=2
+    return invs[0]
+
+def quads(a):
+    h=a.shape[0]//2
+    return a[:h,:h],a[h:,:h],a[h:,h:]
+
+def join(a11,a21,a22):
+    return jnp.concatenate([jnp.concatenate([a11,jnp.zeros_like(a11)],1),jnp.concatenate([a21,a22],1)],0)
+
+def low_nn(a,b):
+    a11,a21,a22=zip(*[quads(v) for v in a]); b11,b21,b22=zip(*[quads(v) for v in b])
+    return join(mul3(dot_nn,a11,b11), mul3(dot_nn,a21,b11)+mul3(dot_nn,a22,b21), mul3(dot_nn,a22,b22))
+def low_nt(a,b):
+    a11,a21,a22=zip(*[quads(v) for v in a]); b11,b21,b22=zip(*[quads(v) for v in b])
+    return join(mul3(dot_nt,a11,b11), mul3(dot_nt,a21,b11), mul3(dot_nt,a21,b21)+mul3(dot_nt,a22,b22))
+def low_tn(a,b):
+    a11,a21,a22=zip(*[quads(v) for v in a]); b11,b21,b22=zip(*[quads(v) for v in b])
+    return join(mul3(dot_tn,a11,b11)+mul3(dot_tn,a21,b21), mul3(dot_tn,a22,b21), mul3(dot_tn,a22,b22))
+
+def ordered(ref, mine, count):
+    return jnp.concatenate([ref[jnp.bitwise_xor(mine,j)] for j in range(count)],0)
+
+def unit(raw):
+    u=lax.rsqrt(jnp.sum(raw*raw,axis=-1,keepdims=True)+eps)
+    return u
+
+def fwd_kernel(scal, q_ref,k_ref,v_ref,w_ref,b_ref, mixed_ref, inv_ref, ctx_ref, p_ref):
+    mine=scal[0]; length=scal[1]
+    cnt=q_ref.shape[0]
+    q=ordered(q_ref,mine,cnt).astype(bf16); k=ordered(k_ref,mine,cnt).astype(bf16)
+    v=ordered(v_ref,mine,cnt).astype(bf16); raw=ordered(w_ref,mine,cnt)
+    w=(raw*unit(raw)).astype(bf16)
+    logit=jnp.concatenate([b_ref[0,pl.ds(jnp.bitwise_xor(mine,j),1),:] for j in range(cnt)],1)
+    beta=2.0*jax.nn.sigmoid(logit)
+    n=q.shape[0]
+    r=iota2(n,0); c=iota2(n,1)
+    strict=c<r; upto=c<=r
+    system=jnp.where(strict,dot_nt(w,w)*beta,0.0)
+    inv=tri_inverse(system,128)
+    coupled=jnp.where(strict,dot_nt(w,k),0.0)
+    invs=halves(inv)
+    ctx=low_nn(invs,halves(coupled))
+    ctxs=halves(ctx)
+    cross=jnp.where(upto,dot_nt(q,w)*beta,0.0)
+    scores=(dot_nt(q,k)-low_nn(halves(cross),ctxs))*(q.shape[1]**-0.5)
+    allowed=upto&(c<length)
+    masked=jnp.where(allowed,scores,-1e30)
+    top=jnp.max(masked,axis=1,keepdims=True)
+    e=jnp.where(allowed,jnp.exp(masked-top),0.0)
+    log_total=top+jnp.log(jnp.sum(e,axis=1,keepdims=True))
+    p=jnp.where(allowed,jnp.exp(masked-log_total),0.0)
+    out=dot_nn(p.astype(bf16),v).astype(bf16)
+    blk=n//cnt
+    for j in range(cnt):
+        mixed_ref[jnp.bitwise_xor(mine,j)]=out[j*blk:(j+1)*blk]
+    for i in range(2):
+        inv_ref[0,i]=invs[i]; ctx_ref[0,i]=ctxs[i]
+    p_ref[0]=p
+
+def bwd_kernel(scal, q_ref,k_ref,v_ref,w_ref,b_ref, inv_ref, ctx_ref, p_ref, dm_ref, dq_ref,dk_ref,dv_ref,dr_ref,dl_ref):
+    mine=scal[0]
+    cnt=q_ref.shape[0]
+    q=ordered(q_ref,mine,cnt).astype(bf16); k=ordered(k_ref,mine,cnt).astype(bf16)
+    v=ordered(v_ref,mine,cnt).astype(bf16); raw=ordered(w_ref,mine,cnt)
+    dm=ordered(dm_ref,mine,cnt)
+    u=unit(raw)
+    w=(raw*u).astype(bf16)
+    logit=jnp.concatenate([b_ref[0,pl.ds(jnp.bitwise_xor(mine,j),1),:] for j in range(cnt)],1)
+    beta=2.0*jax.nn.sigmoid(logit)
+    n=q.shape[0]
+    r=iota2(n,0); c=iota2(n,1)
+    strict=c<r; upto=c<=r
+    invs=(inv_ref[0,0],inv_ref[0,1]); ctxs=(ctx_ref[0,0],ctx_ref[0,1])
+    p=p_ref[0]
+    d_v=dot_tn(p.astype(bf16),dm)
+    dp=dot_nt(dm,v)
+    g=p*(dp-jnp.sum(p*dp,axis=1,keepdims=True))*(q.shape[1]**-0.5)
+    gs=halves(g)
+    qw=dot_nt(q,w)
+    cross=jnp.where(upto,qw*beta,0.0)
+    d_cross=-low_nt(gs,ctxs)
+    d_cross=jnp.where(upto,d_cross,0.0)
+    y=-low_tn(invs,halves(low_tn(halves(cross),gs)))
+    y=jnp.where(strict,y,0.0)
+    ys=halves(y)
+    d_sys=jnp.where(strict,-low_nt(ys,ctxs),0.0)
+    ww=dot_nt(w,w)
+    d_beta=jnp.sum(d_cross*qw+d_sys*ww,axis=0,keepdims=True)
+    dxb=halves(d_cross*beta)
+    bm=halves(d_sys*beta)
+    d_q=mul2(dot_nn,gs,k)+mul2(dot_nn,dxb,w)
+    d_k=mul2(dot_tn,gs,q)+mul2(dot_tn,ys,w)
+    d_w=mul2(dot_tn,dxb,q)+mul2(dot_nn,ys,k)+mul2(dot_nn,bm,w)+mul2(dot_tn,bm,w)
+    d_raw=u*d_w-raw*(u*u*u)*jnp.sum(raw*d_w,axis=1,keepdims=True)
+    d_logit=d_beta*beta*(1.0-0.5*beta)
+    blk=n//cnt
+    for j in range(cnt):
+        at=jnp.bitwise_xor(mine,j); sl=slice(j*blk,(j+1)*blk)
+        dq_ref[at]=d_q[sl].astype(bf16); dk_ref[at]=d_k[sl].astype(bf16)
+        dv_ref[at]=d_v[sl].astype(bf16); dr_ref[at]=d_raw[sl].astype(bf16)
+        dl_ref[0,pl.ds(at,1),:]=d_logit[:,sl]
+
+def specs(cnt,blk,width,heads,n):
+    def col(off): return pl.BlockSpec((cnt,blk,width),lambda h,s,off=off:(0,0,off+h))
+    bs=pl.BlockSpec((1,cnt,blk),lambda h,s:(s[2]+h,0,0))
+    pair=pl.BlockSpec((1,2,n,n),lambda h,s:(h,0,0,0))
+    full=pl.BlockSpec((1,n,n),lambda h,s:(h,0,0))
+    return col,bs,pair,full
+
+def attend_forward(scal, proj, logit, heads):
+    cnt,blk,cols=proj.shape; width=cols//(4*heads); n=cnt*blk
+    col,bs,pair,full=specs(cnt,blk,width,heads,n)
+    return pl.pallas_call(fwd_kernel,
+      grid_spec=pltpu.PrefetchScalarGridSpec(num_scalar_prefetch=1,grid=(heads,),
+        in_specs=[col(0),col(heads),col(2*heads),col(3*heads),bs],
+        out_specs=[col(0),pair,pair,full]),
+      out_shape=[jax.ShapeDtypeStruct((cnt,blk,heads*width),bf16),jax.ShapeDtypeStruct((heads,2,n,n),bf16),
+        jax.ShapeDtypeStruct((heads,2,n,n),bf16),jax.ShapeDtypeStruct((heads,n,n),f32)],
+      compiler_params=pltpu.CompilerParams(vmem_limit_bytes=56<<20),
+      name="path_forward")(scal,proj,proj,proj,proj,logit)
+
+def attend_backward(scal, proj, logit, inv, ctx, p, d_mixed, heads):
+    cnt,blk,cols=proj.shape; width=cols//(4*heads); n=cnt*blk
+    col,bs,pair,full=specs(cnt,blk,width,heads,n)
+    ob=pl.BlockSpec((1,cnt,blk),lambda h,s:(h,0,0))
+    act=jax.ShapeDtypeStruct((cnt,blk,heads*width),bf16)
+    return pl.pallas_call(bwd_kernel,
+      grid_spec=pltpu.PrefetchScalarGridSpec(num_scalar_prefetch=1,grid=(heads,),
+        in_specs=[col(0),col(heads),col(2*heads),col(3*heads),bs,pair,pair,full,col(0)],
+        out_specs=[col(0)]*4+[ob]),
+      out_shape=[act]*4+[jax.ShapeDtypeStruct((heads,cnt,blk),f32)],
+      compiler_params=pltpu.CompilerParams(vmem_limit_bytes=56<<20),
+      name="path_backward")(scal,proj,proj,proj,proj,logit,inv,ctx,p,d_mixed)
+
+SHARDS = 4
+CHIPS = 4
+
+
+def shard_swap(value, k):
+    return lax.ppermute(value, "shard", [(i, i ^ k) for i in range(SHARDS)])
+
+
+def core_swap(value):
+    return lax.ppermute(value, "rep", [(i, i ^ 1) for i in range(2 * CHIPS)])
+
+
+def chip_swap(value, k):
+    return lax.ppermute(value, "rep", [(i, i ^ (2 * k)) for i in range(2 * CHIPS)])
+
+
+def chip_send(value, pairs):
+    return lax.ppermute(value, "rep", [(2 * a + c, 2 * b + c) for a, b in pairs for c in (0, 1)])
+
+
+def gather_xor(value):
+    return [value] + [shard_swap(value, k) for k in range(1, SHARDS)]
+
+
+def mat(left, right):
+    return dot_nn(left, right)
+
+
+def put(target, value, row, col):
+    return lax.dynamic_update_slice(target, value, (row, col))
+
+
+def take_cols(value, at, size):
+    return lax.dynamic_slice_in_dim(value, at, size, axis=1)
+
+
+def take_rows(value, at, size):
+    return lax.dynamic_slice_in_dim(value, at, size, axis=0)
+
+
+def chip_sum(chunks, hub):
+    count = len(chunks)
+    arrived = {}
+    totals = {}
+    outs = {}
+    for t in range(count):
+        own = chunks[t]
+        if t >= 2:
+            own, _ = lax.optimization_barrier((own, arrived[t - 2]))
+        arrived[t] = chip_send(own, [(0, 1), (3, 2)])
+        pair = (chunks[t].astype(f32) + arrived[t].astype(f32)).astype(bf16)
+        other = chip_send(pair, [(1, 2), (2, 1)])
+        totals[t] = (pair.astype(f32) + other.astype(f32)).astype(bf16)
+        back = chip_send(totals[t], [(1, 0), (2, 3)])
+        outs[t] = jnp.where(hub, totals[t], back)
+    return [outs[t] for t in range(count)]
+
+
+def sharded_layer(
+    tokens,
+    cotangent,
+    lengths,
+    gain_one,
+    w_query,
+    w_key,
+    w_value,
+    w_path,
+    w_beta,
+    w_out,
+    gain_two,
+    w_gate,
+    w_up,
+    w_down,
+):
+    rows, width = tokens.shape
+    part = w_query.shape[0]
+    head_count = w_beta.shape[1]
+    heads = head_count // SHARDS
+    ff_part = w_down.shape[0]
+    ff_core = ff_part // 2
+    seq = rows * SHARDS
+    mine = lax.axis_index("shard")
+    rep = lax.axis_index("rep")
+    core = rep % 2
+    chip = rep // 2
+    hub = (chip == 1) | (chip == 2)
+    first_core = core == 0
+    length = lengths[0]
+    peers = [jnp.bitwise_xor(mine, k) for k in range(SHARDS)]
+    live = (mine * rows + jnp.arange(rows) < length).astype(f32)[:, None]
+    scal = jnp.stack([mine, length, mine * heads]).astype(jnp.int32)
+
+    tok = jnp.stack(gather_xor(tokens))
+    small = jnp.concatenate(
+        [w_beta.T, gain_one[None], gain_two[None], jnp.zeros((2, part), bf16)], 0
+    )
+    small_all = jnp.zeros((small.shape[0], width), bf16)
+    for k, piece in enumerate(gather_xor(small)):
+        small_all = put(small_all, piece, 0, peers[k] * part)
+    beta_w = small_all[:head_count]
+    gain_a = small_all[head_count].astype(f32)
+    gain_b = small_all[head_count + 1].astype(f32)
+
+    def head_cols(k, flip):
+        at = peers[k] * part
+        left = jnp.where(
+            first_core != flip, take_cols(w_query, at, part), take_cols(w_value, at, part)
+        )
+        right = jnp.where(
+            first_core != flip, take_cols(w_key, at, part), take_cols(w_path, at, part)
+        )
+        return jnp.concatenate([left, right], 1)
+
+    proj_w = jnp.zeros((width, 4 * part), bf16)
+    own_at, other_at = core * 2 * part, (1 - core) * 2 * part
+    for k in range(SHARDS):
+        at = peers[k] * part
+        if k == 0:
+            ours, theirs = head_cols(0, False), head_cols(0, True)
+        else:
+            ours = shard_swap(head_cols(k, False), k)
+            theirs = core_swap(ours)
+        proj_w = put(put(proj_w, ours, at, own_at), theirs, at, other_at)
+
+    tok_f = tok.astype(f32)
+    factor_one = lax.rsqrt(jnp.mean(tok_f * tok_f, axis=-1, keepdims=True) + eps)
+    normed = (tok_f * factor_one * gain_a).astype(bf16).reshape(seq, width)
+    proj = mat(normed, proj_w).reshape(SHARDS, rows, 4 * part)
+    logit = dot_nt(beta_w, normed).reshape(head_count, SHARDS, rows)
+    mixed, inv, ctx, probs = attend_forward(scal, proj, logit, heads)
+
+    half = width // 2
+    out_w = jnp.zeros((width, width), bf16)
+    for k in range(SHARDS):
+        if k == 0:
+            ours, theirs = take_cols(w_out, core * half, half), take_cols(w_out, (1 - core) * half, half)
+        else:
+            ours = shard_swap(take_cols(w_out, core * half, half), k)
+            theirs = core_swap(ours)
+        out_w = put(put(out_w, ours, k * part, core * half), theirs, k * part, (1 - core) * half)
+    ff_w = jnp.zeros((width, 2 * ff_core), bf16)
+    for k in range(SHARDS):
+        at = peers[k] * ff_part + core * ff_core
+        piece = jnp.concatenate([take_cols(w_gate, at, ff_core), take_cols(w_up, at, ff_core)], 1)
+        if k:
+            piece = shard_swap(piece, k)
+        ff_w = put(ff_w, piece, peers[k] * part, 0)
+    down_w = take_rows(w_down, core * ff_core, ff_core)
+    cot_rows = cotangent.astype(f32) * live
+    d_feed_own = gather_xor(cot_rows.astype(bf16))
+    d_feed = jnp.concatenate(d_feed_own + [core_swap(v) for v in d_feed_own], 0)
+
+    mixed_rows = jnp.concatenate(
+        [mixed[0]] + [shard_swap(mixed[k], k) for k in range(1, SHARDS)], 1
+    )
+    attn_out = mat(mixed_rows, out_w)
+    own_tok = tokens.astype(f32)
+    stream = own_tok + live * attn_out
+    factor_two = lax.rsqrt(jnp.mean(stream * stream, axis=-1, keepdims=True) + eps)
+    normed_two = (stream * factor_two * gain_b).astype(bf16)
+    n_two_own = gather_xor(normed_two)
+    n_two = jnp.concatenate(n_two_own + [core_swap(v) for v in n_two_own], 0)
+
+    gate_up = mat(n_two, ff_w)
+    gate, up = gate_up[:, :ff_core], gate_up[:, ff_core:]
+    sig = jax.nn.sigmoid(gate)
+    hidden = (gate * sig * up).astype(bf16)
+    d_hidden = dot_nt(d_feed, down_w)
+    d_gate = (d_hidden * up * sig * (1.0 + gate * (1.0 - sig))).astype(bf16)
+    d_up = (d_hidden * gate * sig).astype(bf16)
+    d_gate_up = jnp.concatenate([d_gate, d_up], 1)
+
+    def rows_home(partial):
+        sent = core_swap(partial[seq:].astype(bf16))
+        chip_part = partial[:seq] + sent.astype(f32)
+        total = chip_part[:rows]
+        for k in range(1, SHARDS):
+            piece = chip_part[k * rows : (k + 1) * rows].astype(bf16)
+            total = total + shard_swap(piece, k).astype(f32)
+        return total
+
+    d_n_two = rows_home(dot_nt(d_gate_up, ff_w))
+    g_down = dot_tn(hidden, d_feed).astype(bf16)
+    g_ff = dot_tn(n_two, d_gate_up).astype(bf16)
+    feed_out = rows_home(mat(hidden, down_w))
+    output = (live * (stream + feed_out)).astype(bf16)
+
+    def home_rows(grad):
+        pieces = [take_rows(grad, peers[k] * part, part) for k in range(SHARDS)]
+        return [pieces[0]] + [shard_swap(pieces[k], k) for k in range(1, SHARDS)]
+
+    chunks = [g_down[: ff_core // 2], g_down[ff_core // 2 :]] + home_rows(g_ff)
+
+    scaled = d_n_two * gain_b
+    mean_two = jnp.mean(stream * scaled, axis=-1, keepdims=True)
+    d_stream = cot_rows + factor_two * scaled - stream * (factor_two**3 * mean_two)
+    part_gain_b = jnp.sum(d_n_two * stream * factor_two, axis=0)
+    d_attn = jnp.concatenate(gather_xor((live * d_stream).astype(bf16)), 0)
+    d_mixed = dot_nt(d_attn, w_out).astype(bf16).reshape(SHARDS, rows, part)
+    g_out = dot_tn(mixed.reshape(seq, part), d_attn)
+    g_out_sent = core_swap(take_rows(g_out, (1 - core) * (part // 2), part // 2).astype(bf16))
+    g_out_own = take_rows(g_out, core * (part // 2), part // 2) + g_out_sent.astype(f32)
+    chunks.append(g_out_own.astype(bf16))
+
+    d_query, d_key, d_value, d_raw, d_logit = attend_backward(
+        scal, proj, logit, inv, ctx, probs, d_mixed, heads
+    )
+    d_proj = jnp.concatenate([d_query, d_key, d_value, d_raw], 2).reshape(seq, 4 * part)
+    d_logit_b = d_logit.astype(bf16).reshape(heads, seq)
+    g_theirs = dot_tn(normed, take_cols(d_proj, other_at, 2 * part)).astype(bf16)
+    g_ours = dot_tn(normed, take_cols(d_proj, own_at, 2 * part))
+    g_proj = (g_ours + core_swap(g_theirs).astype(f32)).astype(bf16)
+    chunks += home_rows(g_proj)
+    sums = chip_sum(chunks, hub)
+
+    beta_rows = take_rows(beta_w, mine * heads, heads)
+    d_n_one = dot_nt(d_proj, proj_w) + dot_tn(d_logit_b, beta_rows)
+    part_gain_a = jnp.sum(
+        d_n_one.reshape(SHARDS, rows, width) * tok_f * factor_one, axis=(0, 1)
+    )
+    d_one = d_n_one[:rows]
+    for k in range(1, SHARDS):
+        d_one = d_one + shard_swap(d_n_one[k * rows : (k + 1) * rows].astype(bf16), k).astype(f32)
+    scaled = d_one * gain_a
+    factor_own = factor_one[0]
+    mean_one = jnp.mean(own_tok * scaled, axis=-1, keepdims=True)
+    input_grad = (
+        d_stream + factor_own * scaled - own_tok * (factor_own**3 * mean_one)
+    ).astype(bf16)
+
+    part_beta = mat(d_logit_b, normed)
+    squares = jnp.stack(
+        [
+            jnp.sum(live * own_tok * own_tok),
+            jnp.sum(live * attn_out * attn_out),
+            jnp.sum(live * feed_out * feed_out),
+            jnp.sum(live),
+        ]
+    )
+    squares = jnp.concatenate([squares, jnp.zeros((part - 4,), f32)])
+    gains = jnp.stack([part_gain_a, part_gain_b])
+    beta_grad = jnp.zeros((head_count, part), f32)
+    shared = jnp.zeros((3, part), f32)
+    for k in range(SHARDS):
+        at = peers[k] * part
+        piece = jnp.concatenate(
+            [take_cols(part_beta, at, part), take_cols(gains, at, part), squares[None]], 0
+        )
+        if k:
+            piece = shard_swap(piece, k)
+        beta_grad = put(beta_grad, piece[:heads], peers[k] * heads, 0)
+        shared = shared + piece[heads:]
+    shared = jnp.concatenate([beta_grad, shared], 0)
+    shared = shared + core_swap(shared)
+    shared = shared + chip_swap(shared, 1)
+    shared = shared + chip_swap(shared, 2)
+    grad_beta = shared[:head_count].T
+    grad_gain_a, grad_gain_b = shared[head_count], shared[head_count + 1]
+    sq_input, sq_attn, sq_feed, live_total = (shared[head_count + 2, i] for i in range(4))
+    denom = live_total * width
+
+    down_sum = jnp.concatenate(sums[:2], 0)
+    grad_down = jnp.zeros((ff_part, width), f32)
+    grad_down = put(grad_down, down_sum.astype(f32), core * ff_core, 0)
+    grad_down = put(grad_down, core_swap(down_sum).astype(f32), (1 - core) * ff_core, 0)
+    grad_gate = jnp.zeros((part, SHARDS * ff_part), f32)
+    grad_up = jnp.zeros((part, SHARDS * ff_part), f32)
+    for k in range(SHARDS):
+        both = sums[2 + k]
+        for piece, which in ((both, core), (core_swap(both), 1 - core)):
+            piece = piece.astype(f32)
+            at = peers[k] * ff_part + which * ff_core
+            grad_gate = put(grad_gate, piece[:, :ff_core], 0, at)
+            grad_up = put(grad_up, piece[:, ff_core:], 0, at)
+    grad_out = jnp.zeros((part, width), f32)
+    grad_out = put(grad_out, sums[6].astype(f32), core * (part // 2), 0)
+    grad_out = put(grad_out, core_swap(sums[6]).astype(f32), (1 - core) * (part // 2), 0)
+    grads = [jnp.zeros((part, width), f32) for i in range(4)]
+    for k in range(SHARDS):
+        ours = sums[7 + k]
+        theirs = core_swap(ours)
+        low = jnp.where(first_core, ours, theirs).astype(f32)
+        high = jnp.where(first_core, theirs, ours).astype(f32)
+        for i, both in enumerate((low, low, high, high)):
+            off = (i % 2) * part
+            grads[i] = put(grads[i], both[:, off : off + part], 0, peers[k] * part)
+
+    return (
+        output,
+        input_grad,
+        grad_gain_a,
+        grads[0],
+        grads[1],
+        grads[2],
+        grads[3],
+        grad_beta,
+        grad_out,
+        grad_gain_b,
+        grad_gate,
+        grad_up,
+        grad_down,
+        jnp.sqrt(sq_input / denom),
+        jnp.sqrt(sq_attn / denom),
+        jnp.sqrt(sq_feed / denom),
+    )
+
+
+def pick(mesh):
+    def layer(*args):
+        head_count, ff_part = args[8].shape[1], args[13].shape[0]
+        fits = mesh.shape["shard"] == SHARDS and mesh.shape["rep"] == 2 * CHIPS
+        fits = fits and head_count % SHARDS == 0 and ff_part % 256 == 0
+        fits = fits and args[4].shape[1] == 128 * head_count and args[0].shape[0] == 128
+        return (sharded_layer if fits else gathered_layer)(*args)
+
+    return layer
+
+
 def solution(mesh):
     return jax.shard_map(
-        per_device,
+        pick(mesh),
         mesh=mesh,
         in_specs=(
             P(("rep", "shard"), None),

time: 2000 us -> 691 us (0.35)
  waiting for transfers between devices: 1330 us -> 252 us
  matrix products: 278 us -> 54.1 us
  starting transfers between devices: 2.62 us -> 169 us
  other arithmetic: 163 us -> 51.6 us
  blocking collectives: 105 us -> 0 us
  Pallas kernels: 0 us -> 40 us
  local copies, waits for them, and re-layouts: 78.5 us -> 109 us
    reduce_scatter x8 -> x0, waiting for transfers between devices: 594 us -> none  [the longest x1 124 us: per_device(): lax.psum_scatter(g_up.astype(jnp.bfloat16), 'shard', scatter_dimension=0,...]
    all_gather x11 -> x0, waiting for transfers between devices: 496 us -> none  [the longest x1 118 us: per_device(): lax.all_gather(w_gate, 'shard', axis=0, tiled=True)]
    ppermute x0 -> x109, waiting for transfers between devices: none -> 252 us  [the longest x33 160 us: chip_send(): lax.ppermute(value, 'rep', [(2 * a + c, 2 * b + c) for a, b in pairs for...]
    psum x1 -> x0, waiting for transfers between devices: 238 us -> none  [per_device(): lax.psum(part_sums[1].astype(jnp.bfloat16), 'rep').astype(jnp.float32)]
    dot_general x79 -> x16, matrix products: 259 us -> 54.1 us  [the longest x5 20.1 us: dot_nn(): lax.dot_general(a, b, (((1,), (0,)), ((), ())), preferred_element_type=f32)]
    ppermute x0 -> x109, starting transfers between devices: none -> 169 us  [the longest x33 94.9 us: chip_send(): lax.ppermute(value, 'rep', [(2 * a + c, 2 * b + c) for a, b in pairs for...]
    another operation x5 -> x4, other arithmetic: 118 us -> 3.88 us  [the longest x4 118 us: attend(): jax.scipy.linalg.solve_triangular(system, coupled, lower=True, unit_diago...]
    psum x2 -> x0, blocking collectives: 68.5 us -> none  [the longest x1 40.3 us: per_device(): lax.psum((jnp.sum(live_mask * stream_in * stream_in), jnp.sum(live_mask *...]
  transfers between devices with their start and end apart: 24 -> 109, of which waited for: 16 -> 34; matrix products, arithmetic and copies ran while one was open for 21% -> 26% of each run, Pallas kernels for 0% -> 6%
where the time goes in v1:
time: 691 us; the launch traced here: 685 us
  waiting for transfers between devices  252 us (36%)
  starting transfers between devices  169 us (24%)
  local copies, waits for them, and re-layouts  109 us (16%)
  matrix products  54.1 us (8%)
  other arithmetic  51.6 us (7%)
  Pallas kernels  40 us (6%)
  between operations  9.85 us (1%)
    ppermute x33, waiting for transfers between devices, chip_send(): lax.ppermute(value, 'rep', [(2 * a + c, 2 * b + c) for a, b in pairs for...  160 us
    ppermute x33, starting transfers between devices, chip_send(): lax.ppermute(value, 'rep', [(2 * a + c, 2 * b + c) for a, b in pairs for...  94.9 us
    ppermute x45, waiting for transfers between devices, shard_swap(): return lax.ppermute(value, 'shard', [(i, i ^ k) for i in range(SHARDS)])  85.6 us
    dynamic_update_slice x42, local copies, waits for them, and re-layouts, put(): return lax.dynamic_update_slice(target, value, (row, col))  58.8 us
    ppermute x45, starting transfers between devices, shard_swap(): return lax.ppermute(value, 'shard', [(i, i ^ k) for i in range(SHARDS)])  57.5 us
    unnamed x176, local copies, waits for them, and re-layouts  20.5 us
    pallas_call x1, Pallas kernels, attend_backward(): pl.pallas_call(bwd_kernel, grid_spec=pltpu.PrefetchScalarGridSpec(num_sca...  20.5 us
    dot_general x5, matrix products, dot_nn(): lax.dot_general(a, b, (((1,), (0,)), ((), ())), preferred_element_type=f32)  20.1 us
  transfers between devices with their start and end apart: 109, of which 34 were waited for; matrix products, arithmetic and copies ran while one was open for 26% of the time, Pallas kernels for 6%

profile of v1, /device:TPU:0, one launch (start us, length us, event | category | flops | bytes accessed | tf_op | source)
XLA Modules:
  0.0 684.6 jit_solution(17901450361171955148)
XLA Ops:
  4.4 2.9 collective-permute-start.3
  8.8 2.9 collective-permute-start.2
  13.5 3.9 dynamic-slice_select_fusion
  20.0 2.5 broadcast.100.clone.1
  45.2 4.6 collective-permute-done.35
  55.0 3.3 collective-permute-done
  62.5 5.3 collective-permute-done.37
  67.8 11.6 %collective-permute-done.6 = bf16[384,768]{1,0:T(8,128)(2,1)S(1)} collective-permute-done((bf16[384,768]{1,0:T(8,128)(2,1)}, bf16[384,768]{1,0:T(8,128)(2,1)S(1)}, u32[]{:S(2)}, u32[]{:S(2)}) %collective-permute-start.6) | collective-permute-done | bytes 589856 | tf_op jit(solution)/shard_map/ppermute | solution.py:561
  79.4 12.6 %collective-permute-done.15 = bf16[384,768]{1,0:T(8,128)(2,1)S(1)} collective-permute-done((bf16[384,768]{1,0:T(8,128)(2,1)}, bf16[384,768]{1,0:T(8,128)(2,1)S(1)}, u32[]{:S(2)}, u32[]{:S(2)}) %collective-permute-start.15) | collective-permute-done | bytes 589856 | tf_op jit(solution)/shard_map/ppermute | solution.py:561
  94.2 8.1 %dynamic_update_slice.198 = bf16[1536,1536]{1,0:T(8,128)(2,1)S(1)} dynamic-update-slice(bf16[1536,1536]{1,0:T(8,128)(2,1)S(1)} %bitcast.83, bf16[384,768]{1,0:T(8,128)(2,1)S(1)} %collective-permute-done.6, s32[]{:T(128)S(6)} %select_n.323, s32[]{:T(128)S(6)} %select_n.330) | dynamic-update-slice | bytes 1179652 | tf_op jit(solution)/shard_map/dynamic_update_slice | solution.py:585
  109.7 5.3 dynamic_update_slice.199
  115.0 7.9 %dynamic_update_slice.200 = bf16[1536,1536]{1,0:T(8,128)(2,1)S(1)} dynamic-update-slice(bf16[1536,1536]{1,0:T(8,128)(2,1)S(1)} %dynamic_update_slice.199, bf16[384,768]{1,0:T(8,128)(2,1)S(1)} %collective-permute-done.8, s32[]{:T(128)S(6)} %select_n.324, s32[]{:T(128)S(6)} %select_n.330) | dynamic-update-slice | bytes 1179652 | tf_op jit(solution)/shard_map/dynamic_update_slice | solution.py:585
  123.8 5.3 dynamic_update_slice.201
  129.1 7.4 %dynamic_update_slice.202 = bf16[1536,1536]{1,0:T(8,128)(2,1)S(1)} dynamic-update-slice(bf16[1536,1536]{1,0:T(8,128)(2,1)S(1)} %dynamic_update_slice.201, bf16[384,768]{1,0:T(8,128)(2,1)S(1)} %collective-permute-done.10, s32[]{:T(128)S(6)} %select_n.325, s32[]{:T(128)S(6)} %select_n.330) | dynamic-update-slice | bytes 1179652 | tf_op jit(solution)/shard_map/dynamic_update_slice | solution.py:585
  137.1 5.0 dynamic_update_slice.203
  144.4 5.4 fusion.q_ref.k_ref.v_ref.w_ref
  149.8 19.5 %path_forward.1 = (bf16[4,128,384]{2,1,0:T(8,128)(2,1)}, bf16[3,2,512,512]{3,2,1,0:T(8,128)(2,1)}, bf16[3,2,512,512]{3,2,1,0:T(8,128)(2,1)}, f32[3,512,512]{2,1,0:T(8,128)}) custom-call(s32[3]{0:T(128)} %pad_add_fusion.scal, f32[4,128,1536]{2,1,0:T(8,128)} %fusion.q_ref.k_ref.v_ref.w_ref, f32[4,128,1536]{2,1,0:T(8,128)} %fusion.q_ref.k_ref.v_ref.w_ref, ...), custom_call_target="tpu_custom_call" | custom-call | tf_op jit(solution)/shard_map/path_forward/pallas_call | solution.py:534
  185.2 4.1 multiply_reduce_fusion.2
  195.3 7.5 %collective-permute-done.30 = bf16[384,1024]{1,0:T(8,128)(2,1)S(1)} collective-permute-done((bf16[384,1024]{1,0:T(8,128)(2,1)S(1)}, bf16[384,1024]{1,0:T(8,128)(2,1)S(1)}, u32[]{:S(2)}, u32[]{:S(2)}) %collective-permute-start.30) | collective-permute-done | bytes 786464 | tf_op jit(solution)/shard_map/ppermute | solution.py:561
  203.7 2.6 collective-permute-start.24
  206.3 5.7 collective-permute-done.21
  212.0 2.3 collective-permute-start.25
  214.4 5.2 collective-permute-done.23
  222.2 5.7 fusion.85
  228.0 2.6 multiply_convert_fusion.1
  230.6 5.7 fusion.13
  239.5 2.3 convolution_convert_fusion.2
  241.9 3.5 collective-permute-start.61
  246.7 4.7 convolution_convert_fusion
  255.0 8.2 %collective-permute-done.61 = bf16[256,1536]{1,0:T(8,128)(2,1)S(1)} collective-permute-done((bf16[256,1536]{1,0:T(8,128)(2,1)S(1)}, bf16[256,1536]{1,0:T(8,128)(2,1)S(1)}, u32[]{:S(2)}, u32[]{:S(2)}) %collective-permute-start.61) | collective-permute-done | bytes 786464 | tf_op jit(solution)/shard_map/ppermute | solution.py:573
  263.2 16.3 %collective-permute-done.71 = bf16[256,1536]{1,0:T(8,128)(2,1)S(1)} collective-permute-done((bf16[256,1536]{1,0:T(8,128)(2,1)S(1)}, bf16[256,1536]{1,0:T(8,128)(2,1)S(1)}, u32[]{:S(2)}, u32[]{:S(2)}) %collective-permute-start.71) | collective-permute-done | bytes 786464 | tf_op jit(solution)/shard_map/ppermute | solution.py:573
  284.0 3.2 fusion.11
  291.6 15.1 %collective-permute-start.62 = (bf16[384,1024]{1,0:T(8,128)(2,1)}, bf16[384,1024]{1,0:T(8,128)(2,1)S(1)}, u32[]{:S(2)}, u32[]{:S(2)}) collective-permute-start(bf16[384,1024]{1,0:T(8,128)(2,1)} %collective-permute-done.60), channel_id=1, source_target_pairs={{0,8},{4,12},{24,16},{28,20},{1,9},{5,13},{25,17},{29,21},{2,10},{... | collective-permute-start | bytes 2359304 | tf_op jit(solution)/shard_map/ppermute | solution.py:573
  312.2 4.1 collective-permute-start.72
  321.3 18.0 %collective-permute-done.72 = bf16[384,1024]{1,0:T(8,128)(2,1)S(1)} collective-permute-done((bf16[384,1024]{1,0:T(8,128)(2,1)S(1)}, bf16[384,1024]{1,0:T(8,128)(2,1)S(1)}, u32[]{:S(2)}, u32[]{:S(2)}) %collective-permute-start.72) | collective-permute-done | bytes 786464 | tf_op jit(solution)/shard_map/ppermute | solution.py:573
  344.7 4.6 collective-permute-start.73
  353.7 19.2 %collective-permute-start.63 = (bf16[384,1024]{1,0:T(8,128)(2,1)S(1)}, bf16[384,1024]{1,0:T(8,128)(2,1)S(1)}, u32[]{:S(2)}, u32[]{:S(2)}) collective-permute-start(bf16[384,1024]{1,0:T(8,128)(2,1)S(1)} %collective-permute-done.59), channel_id=1, source_target_pairs={{0,8},{4,12},{24,16},{28,20},{1,9},{5,13},{25,17},{29,21},{2,10},{... | collective-permute-start | bytes 2359304 | tf_op jit(solution)/shard_map/ppermute | solution.py:573
  379.3 4.5 collective-permute-done.63
  386.6 17.9 %collective-permute-done.107 = bf16[256,1536]{1,0:T(8,128)(2,1)S(1)} collective-permute-done((bf16[256,1536]{1,0:T(8,128)(2,1)S(1)}, bf16[256,1536]{1,0:T(8,128)(2,1)S(1)}, u32[]{:S(2)}, u32[]{:S(2)}) %collective-permute-start.107) | collective-permute-done | bytes 786464 | tf_op jit(solution)/shard_map/ppermute | solution.py:573
  406.6 11.1 %collective-permute-done.105 = bf16[256,1536]{1,0:T(8,128)(2,1)S(1)} collective-permute-done((bf16[256,1536]{1,0:T(8,128)(2,1)S(1)}, bf16[256,1536]{1,0:T(8,128)(2,1)S(1)}, u32[]{:S(2)}, u32[]{:S(2)}) %collective-permute-start.105) | collective-permute-done | bytes 786464 | tf_op jit(solution)/shard_map/ppermute | solution.py:573
  422.3 7.0 %collective-permute-done.46 = bf16[128,1536]{1,0:T(8,128)(2,1)S(1)} collective-permute-done((bf16[128,1536]{1,0:T(8,128)(2,1)S(1)}, bf16[128,1536]{1,0:T(8,128)(2,1)S(1)}, u32[]{:S(2)}, u32[]{:S(2)}) %collective-permute-start.46) | collective-permute-done | bytes 393248 | tf_op jit(solution)/shard_map/ppermute | solution.py:561
  431.1 20.5 %path_backward.1 = (bf16[4,128,384]{2,1,0:T(8,128)(2,1)}, bf16[4,128,384]{2,1,0:T(8,128)(2,1)}, bf16[4,128,384]{2,1,0:T(8,128)(2,1)}, bf16[4,128,384]{2,1,0:T(8,128)(2,1)}, f32[3,4,128]{2,1,0:T(4,128)}) custom-call(s32[3]{0:T(128)} %pad_add_fusion.scal, f32[4,128,1536]{2,1,0:T(8,128)} %fusion.q_ref.k_ref.v_ref.w_ref, ...), custom_call_target="tpu_custom_call" | custom-call | tf_op jit(solution)/shard_map/path_backward/pallas_call | solution.py:548
  455.6 5.5 fusion.6
  467.8 2.8 convolution_convert_fusion.1
  474.7 3.6 fusion.23
  478.3 2.7 concatenate.85
  485.3 3.8 fusion.45
  493.7 3.7 collective-permute-start.56
  500.3 2.4 collective-permute-start.57
  502.7 2.2 fusion.22
  512.5 4.0 collective-permute-start.74
  524.9 4.8 collective-permute-done.74
  531.2 14.4 %collective-permute-done.99 = bf16[384,1024]{1,0:T(8,128)(2,1)S(1)} collective-permute-done((bf16[384,1024]{1,0:T(8,128)(2,1)S(1)}, bf16[384,1024]{1,0:T(8,128)(2,1)S(1)}, u32[]{:S(2)}, u32[]{:S(2)}) %collective-permute-start.99) | collective-permute-done | bytes 786464 | tf_op jit(solution)/shard_map/ppermute | solution.py:573
  545.7 16.0 %collective-permute-done.102 = bf16[384,1024]{1,0:T(8,128)(2,1)S(1)} collective-permute-done((bf16[384,1024]{1,0:T(8,128)(2,1)S(1)}, bf16[384,1024]{1,0:T(8,128)(2,1)S(1)}, u32[]{:S(2)}, u32[]{:S(2)}) %collective-permute-start.102) | collective-permute-done | bytes 786464 | tf_op jit(solution)/shard_map/ppermute | solution.py:573
  569.9 13.0 %collective-permute-start.64 = (bf16[384,768]{1,0:T(8,128)(2,1)S(1)}, bf16[384,768]{1,0:T(8,128)(2,1)S(1)}, u32[]{:S(2)}, u32[]{:S(2)}) collective-permute-start(bf16[384,768]{1,0:T(8,128)(2,1)S(1)} %get-tuple-element.45), channel_id=1, source_target_pairs={{0,8},{4,12},{24,16},{28,20},{1,9},{5,13},{25,17},{29,21},{2,10},{... | collective-permute-start | bytes 1769480 | tf_op jit(solution)/shard_map/ppermute | solution.py:573
  584.4 6.7 collective-permute-done.90
  595.0 4.2 collective-permute-done.68
  602.0 14.9 %collective-permute-done.79 = bf16[384,768]{1,0:T(8,128)(2,1)S(1)} collective-permute-done((bf16[384,768]{1,0:T(8,128)(2,1)S(1)}, bf16[384,768]{1,0:T(8,128)(2,1)S(1)}, u32[]{:S(2)}, u32[]{:S(2)}) %collective-permute-start.79) | collective-permute-done | bytes 589856 | tf_op jit(solution)/shard_map/ppermute | solution.py:561
  619.5 3.2 collective-permute-start.85
  624.1 8.1 %collective-permute-done.80 = bf16[384,768]{1,0:T(8,128)(2,1)S(1)} collective-permute-done((bf16[384,768]{1,0:T(8,128)(2,1)S(1)}, bf16[384,768]{1,0:T(8,128)(2,1)S(1)}, u32[]{:S(2)}, u32[]{:S(2)}) %collective-permute-start.80) | collective-permute-done | bytes 589856 | tf_op jit(solution)/shard_map/ppermute | solution.py:573
  634.5 6.4 collective-permute-done.85
  643.7 5.5 collective-permute-done.77
  651.4 13.0 %collective-permute-done.82 = bf16[384,768]{1,0:T(8,128)(2,1)S(1)} collective-permute-done((bf16[384,768]{1,0:T(8,128)(2,1)S(1)}, bf16[384,768]{1,0:T(8,128)(2,1)S(1)}, u32[]{:S(2)}, u32[]{:S(2)}) %collective-permute-start.82) | collective-permute-done | bytes 589856 | tf_op jit(solution)/shard_map/ppermute | solution.py:573
  665.6 8.9 %collective-permute-done.87 = bf16[384,768]{1,0:T(8,128)(2,1)S(1)} collective-permute-done((bf16[384,768]{1,0:T(8,128)(2,1)S(1)}, bf16[384,768]{1,0:T(8,128)(2,1)S(1)}, u32[]{:S(2)}, u32[]{:S(2)}) %collective-permute-start.87) | collective-permute-done | bytes 589856 | tf_op jit(solution)/shard_map/ppermute | solution.py:573
  (517 shorter events, 209.6 us)
Async XLA Ops:
  4.4 33.2 %collective-permute-start.3 = (bf16[16,384]{1,0:T(8,128)(2,1)}, bf16[16,384]{1,0:T(8,128)(2,1)}, u32[]{:S(2)}, u32[]{:S(2)}) collective-permute-start(bf16[16,384]{1,0:T(8,128)(2,1)} %get-tuple-element.88), channel_id=1, source_target_pairs={{0,1},{1,0},{2,3},{3,2},{4,5},{5,4},{6,7},{7,6},{8,9},{9,8},{10,11... | collective-permute-start | bytes 36872 | tf_op jit(solution)/shard_map/ppermute | solution.py:561
  7.3 31.7 %collective-permute-start.4 = (bf16[16,384]{1,0:T(8,128)(2,1)}, bf16[16,384]{1,0:T(8,128)(2,1)}, u32[]{:S(2)}, u32[]{:S(2)}) collective-permute-start(bf16[16,384]{1,0:T(8,128)(2,1)} %get-tuple-element.88), channel_id=1, source_target_pairs={{0,2},{1,3},{2,0},{3,1},{4,6},{5,7},{6,4},{7,5},{8,10},{9,11},{10,... | collective-permute-start | bytes 36872 | tf_op jit(solution)/shard_map/ppermute | solution.py:561
  8.8 33.4 %collective-permute-start.5 = (bf16[16,384]{1,0:T(8,128)(2,1)}, bf16[16,384]{1,0:T(8,128)(2,1)S(1)}, u32[]{:S(2)}, u32[]{:S(2)}) collective-permute-start(bf16[16,384]{1,0:T(8,128)(2,1)} %get-tuple-element.88), channel_id=1, source_target_pairs={{0,3},{1,2},{2,1},{3,0},{4,7},{5,6},{6,5},{7,4},{8,11},{9,10},{10,... | collective-permute-start | bytes 36872 | tf_op jit(solution)/shard_map/ppermute | solution.py:561
  8.8 44.1 %collective-permute-start.2 = (bf16[128,1536]{1,0:T(8,128)(2,1)}, bf16[128,1536]{1,0:T(8,128)(2,1)}, u32[]{:S(2)}, u32[]{:S(2)}) collective-permute-start(bf16[128,1536]{1,0:T(8,128)(2,1)} %param.14), channel_id=1, source_target_pairs={{0,3},{1,2},{2,1},{3,0},{4,7},{5,6},{6,5},{7,4},{8,11},{9,10},{10,... | collective-permute-start | bytes 1179656 | tf_op jit(solution)/shard_map/ppermute | solution.py:561
  11.8 42.7 %collective-permute-start.1 = (bf16[128,1536]{1,0:T(8,128)(2,1)}, bf16[128,1536]{1,0:T(8,128)(2,1)}, u32[]{:S(2)}, u32[]{:S(2)}) collective-permute-start(bf16[128,1536]{1,0:T(8,128)(2,1)} %param.14), channel_id=1, source_target_pairs={{0,2},{1,3},{2,0},{3,1},{4,6},{5,7},{6,4},{7,5},{8,10},{9,11},{10,... | collective-permute-start | bytes 1179656 | tf_op jit(solution)/shard_map/ppermute | solution.py:561
  39.0 19.3 %collective-permute-start = (bf16[128,1536]{1,0:T(8,128)(2,1)S(1)}, bf16[128,1536]{1,0:T(8,128)(2,1)S(1)}, u32[]{:S(2)}, u32[]{:S(2)}) collective-permute-start(bf16[128,1536]{1,0:T(8,128)(2,1)S(1)} %copy-done.8), channel_id=1, source_target_pairs={{0,1},{1,0},{2,3},{3,2},{4,5},{5,4},{6,7},{7,6},{8,9},{9,8},{10,11... | collective-permute-start | bytes 1179656 | tf_op jit(solution)/shard_map/ppermute | solution.py:561
  53.0 26.5 %collective-permute-start.6 = (bf16[384,768]{1,0:T(8,128)(2,1)}, bf16[384,768]{1,0:T(8,128)(2,1)S(1)}, u32[]{:S(2)}, u32[]{:S(2)}) collective-permute-start(bf16[384,768]{1,0:T(8,128)(2,1)} %pad_maximum_fusion.10), channel_id=1, source_target_pairs={{0,1},{1,0},{2,3},{3,2},{4,5},{5,4},{6,7},{7,6},{8,9},{9,8},{10,11... | collective-permute-start | bytes 1769480 | tf_op jit(solution)/shard_map/ppermute | solution.py:561
  54.5 48.7 %collective-permute-start.8 = (bf16[384,768]{1,0:T(8,128)(2,1)}, bf16[384,768]{1,0:T(8,128)(2,1)S(1)}, u32[]{:S(2)}, u32[]{:S(2)}) collective-permute-start(bf16[384,768]{1,0:T(8,128)(2,1)} %pad_maximum_fusion.11), channel_id=1, source_target_pairs={{0,2},{1,3},{2,0},{3,1},{4,6},{5,7},{6,4},{7,5},{8,10},{9,11},{10,... | collective-permute-start | bytes 1769480 | tf_op jit(solution)/shard_map/ppermute | solution.py:561
  58.3 33.8 %collective-permute-start.15 = (bf16[384,768]{1,0:T(8,128)(2,1)}, bf16[384,768]{1,0:T(8,128)(2,1)S(1)}, u32[]{:S(2)}, u32[]{:S(2)}) collective-permute-start(bf16[384,768]{1,0:T(8,128)(2,1)} %get-tuple-element.169), channel_id=1, source_target_pairs={{0,1},{1,0},{2,3},{3,2},{4,5},{5,4},{6,7},{7,6},{8,9},{9,8},{10,11... | collective-permute-start | bytes 1769480 | tf_op jit(solution)/shard_map/ppermute | solution.py:561
  67.7 36.5 %collective-permute-start.10 = (bf16[384,768]{1,0:T(8,128)(2,1)S(1)}, bf16[384,768]{1,0:T(8,128)(2,1)S(1)}, u32[]{:S(2)}, u32[]{:S(2)}) collective-permute-start(bf16[384,768]{1,0:T(8,128)(2,1)S(1)} %copy-done.45), channel_id=1, source_target_pairs={{0,3},{1,2},{2,1},{3,0},{4,7},{5,6},{6,5},{7,4},{8,11},{9,10},{10,... | collective-permute-start | bytes 1769480 | tf_op jit(solution)/shard_map/ppermute | solution.py:561
  67.7 37.1 %collective-permute-start.39 = (bf16[128,1536]{1,0:T(8,128)(2,1)S(1)}, bf16[128,1536]{1,0:T(8,128)(2,1)S(1)}, u32[]{:S(2)}, u32[]{:S(2)}) collective-permute-start(bf16[128,1536]{1,0:T(8,128)(2,1)S(1)} %collective-permute-done.35), channel_id=1, source_target_pairs={{0,4},{4,0},{8,12},{12,8},{16,20},{20,16},{24,28},{28,24},{1,5},{5... | collective-permute-start | bytes 1179656 | tf_op jit(solution)/shard_map/ppermute | solution.py:565
  79.4 25.4 %collective-permute-start.40 = (bf16[128,1536]{1,0:T(8,128)(2,1)S(1)}, bf16[128,1536]{1,0:T(8,128)(2,1)S(1)}, u32[]{:S(2)}, u32[]{:S(2)}) collective-permute-start(bf16[128,1536]{1,0:T(8,128)(2,1)S(1)} %collective-permute-done.36), channel_id=1, source_target_pairs={{0,4},{4,0},{8,12},{12,8},{16,20},{20,16},{24,28},{28,24},{1,5},{5... | collective-permute-start | bytes 1179656 | tf_op jit(solution)/shard_map/ppermute | solution.py:565
  103.2 33.3 %collective-permute-start.17 = (bf16[384,768]{1,0:T(8,128)(2,1)S(1)}, bf16[384,768]{1,0:T(8,128)(2,1)}, u32[]{:S(2)}, u32[]{:S(2)}) collective-permute-start(bf16[384,768]{1,0:T(8,128)(2,1)S(1)} %copy-done.46), channel_id=1, source_target_pairs={{0,2},{1,3},{2,0},{3,1},{4,6},{5,7},{6,4},{7,5},{8,10},{9,11},{10,... | collective-permute-start | bytes 1769480 | tf_op jit(solution)/shard_map/ppermute | solution.py:561
  104.2 32.3 %collective-permute-start.19 = (bf16[384,768]{1,0:T(8,128)(2,1)S(1)}, bf16[384,768]{1,0:T(8,128)(2,1)S(1)}, u32[]{:S(2)}, u32[]{:S(2)}) collective-permute-start(bf16[384,768]{1,0:T(8,128)(2,1)S(1)} %copy-done.46), channel_id=1, source_target_pairs={{0,3},{1,2},{2,1},{3,0},{4,7},{5,6},{6,5},{7,4},{8,11},{9,10},{10,... | collective-permute-start | bytes 1769480 | tf_op jit(solution)/shard_map/ppermute | solution.py:561
  105.4 31.7 %collective-permute-start.11 = (bf16[384,768]{1,0:T(8,128)(2,1)S(1)}, bf16[384,768]{1,0:T(8,128)(2,1)S(1)}, u32[]{:S(2)}, u32[]{:S(2)}) collective-permute-start(bf16[384,768]{1,0:T(8,128)(2,1)S(1)} %collective-permute-done.10), channel_id=1, source_target_pairs={{0,4},{4,0},{8,12},{12,8},{16,20},{20,16},{24,28},{28,24},{1,5},{5... | collective-permute-start | bytes 1769480 | tf_op jit(solution)/shard_map/ppermute | solution.py:565
  107.8 84.4 %collective-permute-start.28 = (bf16[384,1024]{1,0:T(8,128)(2,1)S(1)}, bf16[384,1024]{1,0:T(8,128)(2,1)S(1)}, u32[]{:S(2)}, u32[]{:S(2)}) collective-permute-start(bf16[384,1024]{1,0:T(8,128)(2,1)S(1)} %copy-done.41), channel_id=1, source_target_pairs={{0,1},{1,0},{2,3},{3,2},{4,5},{5,4},{6,7},{7,6},{8,9},{9,8},{10,11... | collective-permute-start | bytes 2359304 | tf_op jit(solution)/shard_map/ppermute | solution.py:561
  123.0 71.3 %collective-permute-start.29 = (bf16[384,1024]{1,0:T(8,128)(2,1)S(1)}, bf16[384,1024]{1,0:T(8,128)(2,1)S(1)}, u32[]{:S(2)}, u32[]{:S(2)}) collective-permute-start(bf16[384,1024]{1,0:T(8,128)(2,1)S(1)} %copy-done.40), channel_id=1, source_target_pairs={{0,2},{1,3},{2,0},{3,1},{4,6},{5,7},{6,4},{7,5},{8,10},{9,11},{10,... | collective-permute-start | bytes 2359304 | tf_op jit(solution)/shard_map/ppermute | solution.py:561
  136.5 34.0 %collective-permute-start.16 = (bf16[384,768]{1,0:T(8,128)(2,1)S(1)}, bf16[384,768]{1,0:T(8,128)(2,1)}, u32[]{:S(2)}, u32[]{:S(2)}) collective-permute-start(bf16[384,768]{1,0:T(8,128)(2,1)S(1)} %collective-permute-done.15), channel_id=1, source_target_pairs={{0,4},{4,0},{8,12},{12,8},{16,20},{20,16},{24,28},{28,24},{1,5},{5... | collective-permute-start | bytes 1769480 | tf_op jit(solution)/shard_map/ppermute | solution.py:565
  136.6 39.7 %collective-permute-start.18 = (bf16[384,768]{1,0:T(8,128)(2,1)}, bf16[384,768]{1,0:T(8,128)(2,1)}, u32[]{:S(2)}, u32[]{:S(2)}) collective-permute-start(bf16[384,768]{1,0:T(8,128)(2,1)} %collective-permute-done.17), channel_id=1, source_target_pairs={{0,4},{4,0},{8,12},{12,8},{16,20},{20,16},{24,28},{28,24},{1,5},{5... | collective-permute-start | bytes 1769480 | tf_op jit(solution)/shard_map/ppermute | solution.py:565
  137.1 43.5 %collective-permute-start.20 = (bf16[384,768]{1,0:T(8,128)(2,1)S(1)}, bf16[384,768]{1,0:T(8,128)(2,1)}, u32[]{:S(2)}, u32[]{:S(2)}) collective-permute-start(bf16[384,768]{1,0:T(8,128)(2,1)S(1)} %collective-permute-done.19), channel_id=1, source_target_pairs={{0,4},{4,0},{8,12},{12,8},{16,20},{20,16},{24,28},{28,24},{1,5},{5... | collective-permute-start | bytes 1769480 | tf_op jit(solution)/shard_map/ppermute | solution.py:565
  182.8 20.0 %collective-permute-start.30 = (bf16[384,1024]{1,0:T(8,128)(2,1)S(1)}, bf16[384,1024]{1,0:T(8,128)(2,1)S(1)}, u32[]{:S(2)}, u32[]{:S(2)}) collective-permute-start(bf16[384,1024]{1,0:T(8,128)(2,1)S(1)} %copy-done.39), channel_id=1, source_target_pairs={{0,3},{1,2},{2,1},{3,0},{4,7},{5,6},{6,5},{7,4},{8,11},{9,10},{10,... | collective-permute-start | bytes 2359304 | tf_op jit(solution)/shard_map/ppermute | solution.py:561
  189.9 22.2 %collective-permute-start.21 = (bf16[128,1536]{1,0:T(8,128)(2,1)S(1)}, bf16[128,1536]{1,0:T(8,128)(2,1)S(1)}, u32[]{:S(2)}, u32[]{:S(2)}) collective-permute-start(bf16[128,1536]{1,0:T(8,128)(2,1)S(1)} %get-tuple-element.84), channel_id=1, source_target_pairs={{0,1},{1,0},{2,3},{3,2},{4,5},{5,4},{6,7},{7,6},{8,9},{9,8},{10,11... | collective-permute-start | bytes 1179656 | tf_op jit(solution)/shard_map/ppermute | solution.py:561
  191.0 23.4 %collective-permute-start.22 = (bf16[128,1536]{1,0:T(8,128)(2,1)S(1)}, bf16[128,1536]{1,0:T(8,128)(2,1)S(1)}, u32[]{:S(2)}, u32[]{:S(2)}) collective-permute-start(bf16[128,1536]{1,0:T(8,128)(2,1)S(1)} %get-tuple-element.84), channel_id=1, source_target_pairs={{0,2},{1,3},{2,0},{3,1},{4,6},{5,7},{6,4},{7,5},{8,10},{9,11},{10,... | collective-permute-start | bytes 1179656 | tf_op jit(solution)/shard_map/ppermute | solution.py:561
  193.1 26.5 %collective-permute-start.23 = (bf16[128,1536]{1,0:T(8,128)(2,1)S(1)}, bf16[128,1536]{1,0:T(8,128)(2,1)S(1)}, u32[]{:S(2)}, u32[]{:S(2)}) collective-permute-start(bf16[128,1536]{1,0:T(8,128)(2,1)S(1)} %get-tuple-element.84), channel_id=1, source_target_pairs={{0,3},{1,2},{2,1},{3,0},{4,7},{5,6},{6,5},{7,4},{8,11},{9,10},{10,... | collective-permute-start | bytes 1179656 | tf_op jit(solution)/shard_map/ppermute | solution.py:561
  237.8 70.5 %collective-permute-start.42 = (bf16[512,1536]{1,0:T(8,128)(2,1)}, bf16[512,1536]{1,0:T(8,128)(2,1)}, u32[]{:S(2)}, u32[]{:S(2)}) collective-permute-start(bf16[512,1536]{1,0:T(8,128)(2,1)} %slice.467), channel_id=1, source_target_pairs={{0,4},{4,0},{8,12},{12,8},{16,20},{20,16},{24,28},{28,24},{1,5},{5... | collective-permute-start | bytes 4718600 | tf_op jit(solution)/shard_map/ppermute | solution.py:565
  241.9 21.3 %collective-permute-start.61 = (bf16[256,1536]{1,0:T(8,128)(2,1)S(1)}, bf16[256,1536]{1,0:T(8,128)(2,1)S(1)}, u32[]{:S(2)}, u32[]{:S(2)}) collective-permute-start(bf16[256,1536]{1,0:T(8,128)(2,1)S(1)} %get-tuple-element.139), channel_id=1, source_target_pairs={{0,8},{4,12},{24,16},{28,20},{1,9},{5,13},{25,17},{29,21},{2,10},{... | collective-permute-start | bytes 2359304 | tf_op jit(solution)/shard_map/ppermute | solution.py:573
  245.4 34.1 %collective-permute-start.71 = (bf16[256,1536]{1,0:T(8,128)(2,1)S(1)}, bf16[256,1536]{1,0:T(8,128)(2,1)S(1)}, u32[]{:S(2)}, u32[]{:S(2)}) collective-permute-start(bf16[256,1536]{1,0:T(8,128)(2,1)S(1)} %get-tuple-element.138), channel_id=1, source_target_pairs={{0,8},{4,12},{24,16},{28,20},{1,9},{5,13},{25,17},{29,21},{2,10},{... | collective-permute-start | bytes 2359304 | tf_op jit(solution)/shard_map/ppermute | solution.py:573
  253.2 36.8 %collective-permute-start.60 = (bf16[384,1024]{1,0:T(8,128)(2,1)}, bf16[384,1024]{1,0:T(8,128)(2,1)}, u32[]{:S(2)}, u32[]{:S(2)}) collective-permute-start(bf16[384,1024]{1,0:T(8,128)(2,1)} %get-tuple-element.95), channel_id=1, source_target_pairs={{0,1},{1,0},{2,3},{3,2},{4,5},{5,4},{6,7},{7,6},{8,9},{9,8},{10,11... | collective-permute-start | bytes 2359304 | tf_op jit(solution)/shard_map/ppermute | solution.py:561
  287.4 23.7 %collective-permute-start.31 = (bf16[512,1536]{1,0:T(8,128)(2,1)S(1)}, bf16[512,1536]{1,0:T(8,128)(2,1)S(1)}, u32[]{:S(2)}, u32[]{:S(2)}) collective-permute-start(bf16[512,1536]{1,0:T(8,128)(2,1)S(1)} %slice.468), channel_id=1, source_target_pairs={{0,4},{4,0},{8,12},{12,8},{16,20},{20,16},{24,28},{28,24},{1,5},{5... | collective-permute-start | bytes 4718600 | tf_op jit(solution)/shard_map/ppermute | solution.py:565
  288.3 31.5 %collective-permute-start.59 = (bf16[384,1024]{1,0:T(8,128)(2,1)S(1)}, bf16[384,1024]{1,0:T(8,128)(2,1)S(1)}, u32[]{:S(2)}, u32[]{:S(2)}) collective-permute-start(bf16[384,1024]{1,0:T(8,128)(2,1)S(1)} %copy-done.44), channel_id=1, source_target_pairs={{0,3},{1,2},{2,1},{3,0},{4,7},{5,6},{6,5},{7,4},{8,11},{9,10},{10,... | collective-permute-start | bytes 2359304 | tf_op jit(solution)/shard_map/ppermute | solution.py:561
  290.0 53.2 %collective-permute-start.70 = (bf16[384,1024]{1,0:T(8,128)(2,1)S(1)}, bf16[384,1024]{1,0:T(8,128)(2,1)S(1)}, u32[]{:S(2)}, u32[]{:S(2)}) collective-permute-start(bf16[384,1024]{1,0:T(8,128)(2,1)S(1)} %copy-done.43), channel_id=1, source_target_pairs={{0,2},{1,3},{2,0},{3,1},{4,6},{5,7},{6,4},{7,5},{8,10},{9,11},{10,... | collective-permute-start | bytes 2359304 | tf_op jit(solution)/shard_map/ppermute | solution.py:561
  291.6 49.9 %collective-permute-start.62 = (bf16[384,1024]{1,0:T(8,128)(2,1)}, bf16[384,1024]{1,0:T(8,128)(2,1)S(1)}, u32[]{:S(2)}, u32[]{:S(2)}) collective-permute-start(bf16[384,1024]{1,0:T(8,128)(2,1)} %collective-permute-done.60), channel_id=1, source_target_pairs={{0,8},{4,12},{24,16},{28,20},{1,9},{5,13},{25,17},{29,21},{2,10},{... | collective-permute-start | bytes 2359304 | tf_op jit(solution)/shard_map/ppermute | solution.py:573
  312.2 27.2 %collective-permute-start.72 = (bf16[384,1024]{1,0:T(8,128)(2,1)S(1)}, bf16[384,1024]{1,0:T(8,128)(2,1)S(1)}, u32[]{:S(2)}, u32[]{:S(2)}) collective-permute-start(bf16[384,1024]{1,0:T(8,128)(2,1)S(1)} %copy-done.16), channel_id=1, source_target_pairs={{0,8},{4,12},{24,16},{28,20},{1,9},{5,13},{25,17},{29,21},{2,10},{... | collective-permute-start | bytes 2359304 | tf_op jit(solution)/shard_map/ppermute | solution.py:573
  316.9 27.8 %collective-permute-start.45 = (bf16[128,1536]{1,0:T(8,128)(2,1)S(1)}, bf16[128,1536]{1,0:T(8,128)(2,1)S(1)}, u32[]{:S(2)}, u32[]{:S(2)}) collective-permute-start(bf16[128,1536]{1,0:T(8,128)(2,1)S(1)} %get-tuple-element.144), channel_id=1, source_target_pairs={{0,3},{1,2},{2,1},{3,0},{4,7},{5,6},{6,5},{7,4},{8,11},{9,10},{10,... | collective-permute-start | bytes 1179656 | tf_op jit(solution)/shard_map/ppermute | solution.py:561
  319.8 29.5 %collective-permute-start.44 = (bf16[128,1536]{1,0:T(8,128)(2,1)S(1)}, bf16[128,1536]{1,0:T(8,128)(2,1)S(1)}, u32[]{:S(2)}, u32[]{:S(2)}) collective-permute-start(bf16[128,1536]{1,0:T(8,128)(2,1)S(1)} %get-tuple-element.145), channel_id=1, source_target_pairs={{0,2},{1,3},{2,0},{3,1},{4,6},{5,7},{6,4},{7,5},{8,10},{9,11},{10,... | collective-permute-start | bytes 1179656 | tf_op jit(solution)/shard_map/ppermute | solution.py:561
  341.5 125.1 %collective-permute-start.34 = (bf16[128,1536]{1,0:T(8,128)(2,1)}, bf16[128,1536]{1,0:T(8,128)(2,1)}, u32[]{:S(2)}, u32[]{:S(2)}) collective-permute-start(bf16[128,1536]{1,0:T(8,128)(2,1)} %get-tuple-element.147), channel_id=1, source_target_pairs={{0,3},{1,2},{2,1},{3,0},{4,7},{5,6},{6,5},{7,4},{8,11},{9,10},{10,... | collective-permute-start | bytes 1179656 | tf_op jit(solution)/shard_map/ppermute | solution.py:561
  343.2 127.4 %collective-permute-start.33 = (bf16[128,1536]{1,0:T(8,128)(2,1)}, bf16[128,1536]{1,0:T(8,128)(2,1)}, u32[]{:S(2)}, u32[]{:S(2)}) collective-permute-start(bf16[128,1536]{1,0:T(8,128)(2,1)} %get-tuple-element.148), channel_id=1, source_target_pairs={{0,2},{1,3},{2,0},{3,1},{4,6},{5,7},{6,4},{7,5},{8,10},{9,11},{10,... | collective-permute-start | bytes 1179656 | tf_op jit(solution)/shard_map/ppermute | solution.py:561
  344.7 32.0 %collective-permute-start.73 = (bf16[384,1024]{1,0:T(8,128)(2,1)S(1)}, bf16[384,1024]{1,0:T(8,128)(2,1)S(1)}, u32[]{:S(2)}, u32[]{:S(2)}) collective-permute-start(bf16[384,1024]{1,0:T(8,128)(2,1)S(1)} %collective-permute-done.70), channel_id=1, source_target_pairs={{0,8},{4,12},{24,16},{28,20},{1,9},{5,13},{25,17},{29,21},{2,10},{... | collective-permute-start | bytes 2359304 | tf_op jit(solution)/shard_map/ppermute | solution.py:573
  351.4 22.8 %collective-permute-start.95 = (bf16[384,1024]{1,0:T(8,128)(2,1)S(1)}, bf16[384,1024]{1,0:T(8,128)(2,1)S(1)}, u32[]{:S(2)}, u32[]{:S(2)}) collective-permute-start(bf16[384,1024]{1,0:T(8,128)(2,1)S(1)} %add_convert_fusion.10), channel_id=1, source_target_pairs={{8,16},{12,20},{16,8},{20,12},{9,17},{13,21},{17,9},{21,13},{10,18... | collective-permute-start | bytes 2359304 | tf_op jit(solution)/shard_map/ppermute | solution.py:573
  353.7 30.1 %collective-permute-start.63 = (bf16[384,1024]{1,0:T(8,128)(2,1)S(1)}, bf16[384,1024]{1,0:T(8,128)(2,1)S(1)}, u32[]{:S(2)}, u32[]{:S(2)}) collective-permute-start(bf16[384,1024]{1,0:T(8,128)(2,1)S(1)} %collective-permute-done.59), channel_id=1, source_target_pairs={{0,8},{4,12},{24,16},{28,20},{1,9},{5,13},{25,17},{29,21},{2,10},{... | collective-permute-start | bytes 2359304 | tf_op jit(solution)/shard_map/ppermute | solution.py:573
  374.2 30.4 %collective-permute-start.107 = (bf16[256,1536]{1,0:T(8,128)(2,1)S(1)}, bf16[256,1536]{1,0:T(8,128)(2,1)S(1)}, u32[]{:S(2)}, u32[]{:S(2)}) collective-permute-start(bf16[256,1536]{1,0:T(8,128)(2,1)S(1)} %add_convert_fusion.1), channel_id=1, source_target_pairs={{8,0},{12,4},{16,24},{20,28},{9,1},{13,5},{17,25},{21,29},{10,2},{... | collective-permute-start | bytes 2359304 | tf_op jit(solution)/shard_map/ppermute | solution.py:573
  376.7 41.0 %collective-permute-start.105 = (bf16[256,1536]{1,0:T(8,128)(2,1)S(1)}, bf16[256,1536]{1,0:T(8,128)(2,1)S(1)}, u32[]{:S(2)}, u32[]{:S(2)}) collective-permute-start(bf16[256,1536]{1,0:T(8,128)(2,1)S(1)} %add_convert_fusion.3), channel_id=1, source_target_pairs={{8,0},{12,4},{16,24},{20,28},{9,1},{13,5},{17,25},{21,29},{10,2},{... | collective-permute-start | bytes 2359304 | tf_op jit(solution)/shard_map/ppermute | solution.py:573
  383.9 38.0 %collective-permute-start.48 = (bf16[128,1536]{1,0:T(8,128)(2,1)S(1)}, bf16[128,1536]{1,0:T(8,128)(2,1)S(1)}, u32[]{:S(2)}, u32[]{:S(2)}) collective-permute-start(bf16[128,1536]{1,0:T(8,128)(2,1)S(1)} %get-tuple-element.74), channel_id=1, source_target_pairs={{0,3},{1,2},{2,1},{3,0},{4,7},{5,6},{6,5},{7,4},{8,11},{9,10},{10,... | collective-permute-start | bytes 1179656 | tf_op jit(solution)/shard_map/ppermute | solution.py:561
  421.8 50.1 %collective-permute-start.32 = (bf16[128,1536]{1,0:T(8,128)(2,1)}, bf16[128,1536]{1,0:T(8,128)(2,1)}, u32[]{:S(2)}, u32[]{:S(2)}) collective-permute-start(bf16[128,1536]{1,0:T(8,128)(2,1)} %get-tuple-element.146), channel_id=1, source_target_pairs={{0,1},{1,0},{2,3},{3,2},{4,5},{5,4},{6,7},{7,6},{8,9},{9,8},{10,11... | collective-permute-start | bytes 1179656 | tf_op jit(solution)/shard_map/ppermute | solution.py:561
  470.6 41.9 %collective-permute-start.93 = (bf16[384,1024]{1,0:T(8,128)(2,1)}, bf16[384,1024]{1,0:T(8,128)(2,1)}, u32[]{:S(2)}, u32[]{:S(2)}) collective-permute-start(bf16[384,1024]{1,0:T(8,128)(2,1)} %add_convert_fusion.11), channel_id=1, source_target_pairs={{8,0},{12,4},{16,24},{20,28},{9,1},{13,5},{17,25},{21,29},{10,2},{... | collective-permute-start | bytes 2359304 | tf_op jit(solution)/shard_map/ppermute | solution.py:573
  471.9 45.9 %collective-permute-start.96 = (bf16[384,1024]{1,0:T(8,128)(2,1)}, bf16[384,1024]{1,0:T(8,128)(2,1)}, u32[]{:S(2)}, u32[]{:S(2)}) collective-permute-start(bf16[384,1024]{1,0:T(8,128)(2,1)} %add_convert_fusion.9), channel_id=1, source_target_pairs={{8,0},{12,4},{16,24},{20,28},{9,1},{13,5},{17,25},{21,29},{10,2},{... | collective-permute-start | bytes 2359304 | tf_op jit(solution)/shard_map/ppermute | solution.py:573
  489.3 31.8 %collective-permute-start.98 = (bf16[384,1024]{1,0:T(8,128)(2,1)}, bf16[384,1024]{1,0:T(8,128)(2,1)}, u32[]{:S(2)}, u32[]{:S(2)}) collective-permute-start(bf16[384,1024]{1,0:T(8,128)(2,1)} %add_convert_fusion.8), channel_id=1, source_target_pairs={{8,16},{12,20},{16,8},{20,12},{9,17},{13,21},{17,9},{21,13},{10,18... | collective-permute-start | bytes 2359304 | tf_op jit(solution)/shard_map/ppermute | solution.py:573
  512.4 51.8 %collective-permute-start.108 = (bf16[512,1536]{1,0:T(8,128)(2,1)S(1)}, bf16[512,1536]{1,0:T(8,128)(2,1)S(1)}, u32[]{:S(2)}, u32[]{:S(2)}) collective-permute-start(bf16[512,1536]{1,0:T(8,128)(2,1)S(1)} %copy-done.22), channel_id=1, source_target_pairs={{0,4},{4,0},{8,12},{12,8},{16,20},{20,16},{24,28},{28,24},{1,5},{5... | collective-permute-start | bytes 4718600 | tf_op jit(solution)/shard_map/ppermute | solution.py:565
  517.9 44.7 %collective-permute-start.94 = (bf16[384,1024]{1,0:T(8,128)(2,1)S(1)}, bf16[384,1024]{1,0:T(8,128)(2,1)S(1)}, u32[]{:S(2)}, u32[]{:S(2)}) collective-permute-start(bf16[384,1024]{1,0:T(8,128)(2,1)S(1)} %get-tuple-element.69), channel_id=1, source_target_pairs={{0,4},{4,0},{8,12},{12,8},{16,20},{20,16},{24,28},{28,24},{1,5},{5... | collective-permute-start | bytes 2359304 | tf_op jit(solution)/shard_map/ppermute | solution.py:565
  521.1 41.7 %collective-permute-start.97 = (bf16[384,1024]{1,0:T(8,128)(2,1)S(1)}, bf16[384,1024]{1,0:T(8,128)(2,1)S(1)}, u32[]{:S(2)}, u32[]{:S(2)}) collective-permute-start(bf16[384,1024]{1,0:T(8,128)(2,1)S(1)} %get-tuple-element.67), channel_id=1, source_target_pairs={{0,4},{4,0},{8,12},{12,8},{16,20},{20,16},{24,28},{28,24},{1,5},{5... | collective-permute-start | bytes 2359304 | tf_op jit(solution)/shard_map/ppermute | solution.py:565
  523.2 22.4 %collective-permute-start.99 = (bf16[384,1024]{1,0:T(8,128)(2,1)S(1)}, bf16[384,1024]{1,0:T(8,128)(2,1)S(1)}, u32[]{:S(2)}, u32[]{:S(2)}) collective-permute-start(bf16[384,1024]{1,0:T(8,128)(2,1)S(1)} %add_convert_fusion.7), channel_id=1, source_target_pairs={{8,0},{12,4},{16,24},{20,28},{9,1},{13,5},{17,25},{21,29},{10,2},{... | collective-permute-start | bytes 2359304 | tf_op jit(solution)/shard_map/ppermute | solution.py:573
  529.7 32.0 %collective-permute-start.102 = (bf16[384,1024]{1,0:T(8,128)(2,1)S(1)}, bf16[384,1024]{1,0:T(8,128)(2,1)S(1)}, u32[]{:S(2)}, u32[]{:S(2)}) collective-permute-start(bf16[384,1024]{1,0:T(8,128)(2,1)S(1)} %add_convert_fusion.5), channel_id=1, source_target_pairs={{8,0},{12,4},{16,24},{20,28},{9,1},{13,5},{17,25},{21,29},{10,2},{... | collective-permute-start | bytes 2359304 | tf_op jit(solution)/shard_map/ppermute | solution.py:573
  545.6 22.6 %collective-permute-start.58 = (bf16[1536,768]{1,0:T(8,128)(2,1)S(1)}, bf16[1536,768]{1,0:T(8,128)(2,1)S(1)}, u32[]{:S(2)}, u32[]{:S(2)}) collective-permute-start(bf16[1536,768]{1,0:T(8,128)(2,1)S(1)} %copy-done.69), channel_id=1, source_target_pairs={{0,4},{4,0},{8,12},{12,8},{16,20},{20,16},{24,28},{28,24},{1,5},{5... | collective-permute-start | bytes 7077896 | tf_op jit(solution)/shard_map/ppermute | solution.py:565
  562.6 30.9 %collective-permute-start.100 = (bf16[384,1024]{1,0:T(8,128)(2,1)S(1)}, bf16[384,1024]{1,0:T(8,128)(2,1)S(1)}, u32[]{:S(2)}, u32[]{:S(2)}) collective-permute-start(bf16[384,1024]{1,0:T(8,128)(2,1)S(1)} %get-tuple-element.65), channel_id=1, source_target_pairs={{0,4},{4,0},{8,12},{12,8},{16,20},{20,16},{24,28},{28,24},{1,5},{5... | collective-permute-start | bytes 2359304 | tf_op jit(solution)/shard_map/ppermute | solution.py:565
  562.8 37.9 %collective-permute-start.103 = (bf16[384,1024]{1,0:T(8,128)(2,1)S(1)}, bf16[384,1024]{1,0:T(8,128)(2,1)S(1)}, u32[]{:S(2)}, u32[]{:S(2)}) collective-permute-start(bf16[384,1024]{1,0:T(8,128)(2,1)S(1)} %get-tuple-element.63), channel_id=1, source_target_pairs={{0,4},{4,0},{8,12},{12,8},{16,20},{20,16},{24,28},{28,24},{1,5},{5... | collective-permute-start | bytes 2359304 | tf_op jit(solution)/shard_map/ppermute | solution.py:565
  566.9 24.2 %collective-permute-start.90 = (bf16[192,1536]{1,0:T(8,128)(2,1)S(1)}, bf16[192,1536]{1,0:T(8,128)(2,1)S(1)}, u32[]{:S(2)}, u32[]{:S(2)}) collective-permute-start(bf16[192,1536]{1,0:T(8,128)(2,1)S(1)} %add_convert_fusion.13), channel_id=1, source_target_pairs={{8,0},{12,4},{16,24},{20,28},{9,1},{13,5},{17,25},{21,29},{10,2},{... | collective-permute-start | bytes 1769480 | tf_op jit(solution)/shard_map/ppermute | solution.py:573
  569.9 31.3 %collective-permute-start.64 = (bf16[384,768]{1,0:T(8,128)(2,1)S(1)}, bf16[384,768]{1,0:T(8,128)(2,1)S(1)}, u32[]{:S(2)}, u32[]{:S(2)}) collective-permute-start(bf16[384,768]{1,0:T(8,128)(2,1)S(1)} %get-tuple-element.45), channel_id=1, source_target_pairs={{0,8},{4,12},{24,16},{28,20},{1,9},{5,13},{25,17},{29,21},{2,10},{... | collective-permute-start | bytes 1769480 | tf_op jit(solution)/shard_map/ppermute | solution.py:573
  591.1 25.8 %collective-permute-start.79 = (bf16[384,768]{1,0:T(8,128)(2,1)S(1)}, bf16[384,768]{1,0:T(8,128)(2,1)S(1)}, u32[]{:S(2)}, u32[]{:S(2)}) collective-permute-start(bf16[384,768]{1,0:T(8,128)(2,1)S(1)} %get-tuple-element.108), channel_id=1, source_target_pairs={{0,2},{1,3},{2,0},{3,1},{4,6},{5,7},{6,4},{7,5},{8,10},{9,11},{10,... | collective-permute-start | bytes 1769480 | tf_op jit(solution)/shard_map/ppermute | solution.py:561
  593.5 26.0 %collective-permute-start.84 = (bf16[384,768]{1,0:T(8,128)(2,1)S(1)}, bf16[384,768]{1,0:T(8,128)(2,1)S(1)}, u32[]{:S(2)}, u32[]{:S(2)}) collective-permute-start(bf16[384,768]{1,0:T(8,128)(2,1)S(1)} %get-tuple-element.107), channel_id=1, source_target_pairs={{0,3},{1,2},{2,1},{3,0},{4,7},{5,6},{6,5},{7,4},{8,11},{9,10},{10,... | collective-permute-start | bytes 1769480 | tf_op jit(solution)/shard_map/ppermute | solution.py:561
  601.3 21.3 %collective-permute-start.65 = (bf16[384,768]{1,0:T(8,128)(2,1)S(1)}, bf16[384,768]{1,0:T(8,128)(2,1)S(1)}, u32[]{:S(2)}, u32[]{:S(2)}) collective-permute-start(bf16[384,768]{1,0:T(8,128)(2,1)S(1)} %add_convert_fusion.23), channel_id=1, source_target_pairs={{8,16},{12,20},{16,8},{20,12},{9,17},{13,21},{17,9},{21,13},{10,18... | collective-permute-start | bytes 1769480 | tf_op jit(solution)/shard_map/ppermute | solution.py:573
  619.5 21.5 %collective-permute-start.85 = (bf16[384,768]{1,0:T(8,128)(2,1)S(1)}, bf16[384,768]{1,0:T(8,128)(2,1)S(1)}, u32[]{:S(2)}, u32[]{:S(2)}) collective-permute-start(bf16[384,768]{1,0:T(8,128)(2,1)S(1)} %collective-permute-done.84), channel_id=1, source_target_pairs={{0,8},{4,12},{24,16},{28,20},{1,9},{5,13},{25,17},{29,21},{2,10},{... | collective-permute-start | bytes 1769480 | tf_op jit(solution)/shard_map/ppermute | solution.py:573
  642.1 22.3 %collective-permute-start.82 = (bf16[384,768]{1,0:T(8,128)(2,1)S(1)}, bf16[384,768]{1,0:T(8,128)(2,1)S(1)}, u32[]{:S(2)}, u32[]{:S(2)}) collective-permute-start(bf16[384,768]{1,0:T(8,128)(2,1)S(1)} %add_convert_fusion.17), channel_id=1, source_target_pairs={{8,0},{12,4},{16,24},{20,28},{9,1},{13,5},{17,25},{21,29},{10,2},{... | collective-permute-start | bytes 1769480 | tf_op jit(solution)/shard_map/ppermute | solution.py:573
  649.3 25.4 %collective-permute-start.78 = (bf16[384,768]{1,0:T(8,128)(2,1)S(1)}, bf16[384,768]{1,0:T(8,128)(2,1)S(1)}, u32[]{:S(2)}, u32[]{:S(2)}) collective-permute-start(bf16[384,768]{1,0:T(8,128)(2,1)S(1)} %broadcast_select_fusion.9), channel_id=1, source_target_pairs={{0,4},{4,0},{8,12},{12,8},{16,20},{20,16},{24,28},{28,24},{1,5},{5... | collective-permute-start | bytes 1769480 | tf_op jit(solution)/shard_map/ppermute | solution.py:565
  649.6 25.0 %collective-permute-start.87 = (bf16[384,768]{1,0:T(8,128)(2,1)S(1)}, bf16[384,768]{1,0:T(8,128)(2,1)S(1)}, u32[]{:S(2)}, u32[]{:S(2)}) collective-permute-start(bf16[384,768]{1,0:T(8,128)(2,1)S(1)} %add_convert_fusion.15), channel_id=1, source_target_pairs={{8,0},{12,4},{16,24},{20,28},{9,1},{13,5},{17,25},{21,29},{10,2},{... | collective-permute-start | bytes 1769480 | tf_op jit(solution)/shard_map/ppermute | solution.py:573
  (127 other events, 1765.9 us)

commit v2 on v0

--- a/solution.py
+++ b/solution.py
@@ -1,7 +1,14 @@
+import functools
+
 import jax
 import jax.numpy as jnp
 from jax import lax
+from jax.experimental import pallas as pl
+from jax.experimental.pallas import tpu as pltpu
 from jax.sharding import PartitionSpec as P
+
+f32 = jnp.float32
+bf16 = jnp.bfloat16
 
 eps = 1e-06
 highest = lax.Precision.HIGHEST
@@ -133,7 +140,7 @@
     )
 
 
-def per_device(
+def gathered_layer(
     tokens,
     cotangent,
     lengths,
@@ -370,9 +377,892 @@
     )
 
 
+def dot_nn(a, b):
+    return lax.dot_general(a, b, (((1,), (0,)), ((), ())), preferred_element_type=f32)
+
+
+def dot_nt(a, b):
+    return lax.dot_general(a, b, (((1,), (1,)), ((), ())), preferred_element_type=f32)
+
+
+def dot_tn(a, b):
+    return lax.dot_general(a, b, (((0,), (0,)), ((), ())), preferred_element_type=f32)
+
+
+def halves(a):
+    hi = a.astype(bf16)
+    return hi, (a - hi.astype(f32)).astype(bf16)
+
+
+def mul3(dot, a, b):
+    return dot(a[0], b[0]) + (dot(a[0], b[1]) + dot(a[1], b[0]))
+
+
+def mul2(dot, a, b):
+    return dot(a[0], b) + dot(a[1], b)
+
+
+def iota2(n, ax):
+    return lax.broadcasted_iota(jnp.int32, (n, n), ax)
+
+
+def tri_inverse(system, blk):
+    n = system.shape[0]
+    r, c = iota2(blk, 0), iota2(blk, 1)
+    eye = jnp.where(r == c, 1.0, 0.0)
+    tiles = [system[i * blk : (i + 1) * blk, i * blk : (i + 1) * blk] for i in range(n // blk)]
+    pairs = ((r >> 1) == (c >> 1)) & ((r & 1) == 1) & ((c & 1) == 0)
+    invs = [eye - jnp.where(pairs, t, 0.0) for t in tiles]
+    b = 2
+    while b < blk:
+        m = ((r // (2 * b)) == (c // (2 * b))) & (((r // b) & 1) == 1) & (((c // b) & 1) == 0)
+        new = []
+        for t, v in zip(tiles, invs):
+            vs = halves(v)
+            low = mul3(dot_nn, halves(jnp.where(m, t, 0.0)), vs)
+            new.append(v - mul3(dot_nn, vs, halves(low)))
+        invs = new
+        b *= 2
+    size = blk
+    while size < n:
+        new = []
+        for i in range(0, len(invs), 2):
+            a, d = invs[i], invs[i + 1]
+            off = system[(i + 1) * size : (i + 2) * size, i * size : (i + 1) * size]
+            low = mul3(dot_nn, halves(off), halves(a))
+            new.append(join(a, -mul3(dot_nn, halves(d), halves(low)), d))
+        invs = new
+        size *= 2
+    return invs[0]
+
+
+def quads(a):
+    h = a.shape[0] // 2
+    return a[:h, :h], a[h:, :h], a[h:, h:]
+
+
+def join(a11, a21, a22):
+    upper = jnp.concatenate([a11, jnp.zeros_like(a11)], 1)
+    return jnp.concatenate([upper, jnp.concatenate([a21, a22], 1)], 0)
+
+
+def low_nn(a, b):
+    a11, a21, a22 = zip(*[quads(v) for v in a])
+    b11, b21, b22 = zip(*[quads(v) for v in b])
+    return join(
+        mul3(dot_nn, a11, b11),
+        mul3(dot_nn, a21, b11) + mul3(dot_nn, a22, b21),
+        mul3(dot_nn, a22, b22),
+    )
+
+
+def low_nt(a, b):
+    a11, a21, a22 = zip(*[quads(v) for v in a])
+    b11, b21, b22 = zip(*[quads(v) for v in b])
+    return join(
+        mul3(dot_nt, a11, b11),
+        mul3(dot_nt, a21, b11),
+        mul3(dot_nt, a21, b21) + mul3(dot_nt, a22, b22),
+    )
+
+
+def low_tn(a, b):
+    a11, a21, a22 = zip(*[quads(v) for v in a])
+    b11, b21, b22 = zip(*[quads(v) for v in b])
+    return join(
+        mul3(dot_tn, a11, b11) + mul3(dot_tn, a21, b21),
+        mul3(dot_tn, a22, b21),
+        mul3(dot_tn, a22, b22),
+    )
+
+
+def aligned(at, size):
+    return pl.ds(pl.multiple_of(at, 128), size)
+
+
+def unit_factor(raw):
+    return lax.rsqrt(jnp.sum(raw * raw, axis=-1, keepdims=True) + eps)
+
+
+def forward_kernel(scal, q_ref, k_ref, v_ref, w_ref, b_ref, mixed_ref, inv_ref, ctx_ref, p_ref):
+    length = scal[2]
+    q, k, v, raw = q_ref[...], k_ref[...], v_ref[...], w_ref[...]
+    w = (raw * unit_factor(raw)).astype(bf16)
+    beta = 2.0 * jax.nn.sigmoid(b_ref[0])
+    n = q.shape[0]
+    r, c = iota2(n, 0), iota2(n, 1)
+    strict, upto = c < r, c <= r
+    inv = halves(tri_inverse(jnp.where(strict, dot_nt(w, w) * beta, 0.0), 128))
+    ctx = halves(low_nn(inv, halves(jnp.where(strict, dot_nt(w, k), 0.0))))
+    cross = jnp.where(upto, dot_nt(q, w) * beta, 0.0)
+    scores = (dot_nt(q, k) - low_nn(halves(cross), ctx)) * (q.shape[1] ** -0.5)
+    allowed = upto & (c < length)
+    masked = jnp.where(allowed, scores, -1e30)
+    top = jnp.max(masked, axis=1, keepdims=True)
+    e = jnp.where(allowed, jnp.exp(masked - top), 0.0)
+    log_total = top + jnp.log(jnp.sum(e, axis=1, keepdims=True))
+    p = jnp.where(allowed, jnp.exp(masked - log_total), 0.0)
+    mixed_ref[...] = dot_nn(p.astype(bf16), v).astype(bf16)
+    for i in range(2):
+        inv_ref[0, i] = inv[i]
+        ctx_ref[0, i] = ctx[i]
+    p_ref[0] = p
+
+
+def backward_kernel(scal, *refs):
+    q_ref, k_ref, v_ref, w_ref, b_ref, inv_ref, ctx_ref, p_ref, dm_ref = refs[:9]
+    dq_ref, dk_ref, dv_ref, dr_ref, dl_ref = refs[9:]
+    q, k, v, raw, dm = q_ref[...], k_ref[...], v_ref[...], w_ref[...], dm_ref[...]
+    u = unit_factor(raw)
+    w = (raw * u).astype(bf16)
+    beta = 2.0 * jax.nn.sigmoid(b_ref[0])
+    n = q.shape[0]
+    r, c = iota2(n, 0), iota2(n, 1)
+    strict, upto = c < r, c <= r
+    inv = inv_ref[0, 0], inv_ref[0, 1]
+    ctx = ctx_ref[0, 0], ctx_ref[0, 1]
+    p = p_ref[0]
+    d_v = dot_tn(p.astype(bf16), dm)
+    dp = dot_nt(dm, v)
+    g = p * (dp - jnp.sum(p * dp, axis=1, keepdims=True)) * (q.shape[1] ** -0.5)
+    gs = halves(g)
+    qw = dot_nt(q, w)
+    cross = jnp.where(upto, qw * beta, 0.0)
+    d_cross = jnp.where(upto, -low_nt(gs, ctx), 0.0)
+    y = jnp.where(strict, -low_tn(inv, halves(low_tn(halves(cross), gs))), 0.0)
+    ys = halves(y)
+    d_sys = jnp.where(strict, -low_nt(ys, ctx), 0.0)
+    d_beta = jnp.sum(d_cross * qw + d_sys * dot_nt(w, w), axis=0, keepdims=True)
+    dx = halves(d_cross * beta)
+    bm = halves(d_sys * beta)
+    d_q = mul2(dot_nn, gs, k) + mul2(dot_nn, dx, w)
+    d_k = mul2(dot_tn, gs, q) + mul2(dot_tn, ys, w)
+    d_w = mul2(dot_tn, dx, q) + mul2(dot_nn, ys, k) + mul2(dot_nn, bm, w) + mul2(dot_tn, bm, w)
+    d_raw = u * d_w - raw * (u * u * u) * jnp.sum(raw * d_w, axis=1, keepdims=True)
+    for ref, val in ((dq_ref, d_q), (dk_ref, d_k), (dv_ref, d_v), (dr_ref, d_raw)):
+        ref[...] = val.astype(bf16)
+    dl_ref[0] = d_beta * beta * (1.0 - 0.5 * beta)
+
+
+def grant():
+    return pltpu.CompilerParams(vmem_limit_bytes=60 << 20)
+
+
+def cost(micros):
+    return pl.CostEstimate(flops=int(micros * 1e6), bytes_accessed=0, transcendentals=0)
+
+
+def struct(shape, kind):
+    return jax.ShapeDtypeStruct(shape, kind)
+
+
+def head_specs(n, width):
+    col = pl.BlockSpec((n, width), lambda h, s: (0, h))
+    row = pl.BlockSpec((1, 1, n), lambda h, s: (h, 0, 0))
+    pair = pl.BlockSpec((1, 2, n, n), lambda h, s: (h, 0, 0, 0))
+    full = pl.BlockSpec((1, n, n), lambda h, s: (h, 0, 0))
+    return col, row, pair, full
+
+
+def attend_forward(scal, q, k, v, raw, logit, heads):
+    n, width = q.shape[0], q.shape[1] // heads
+    col, row, pair, full = head_specs(n, width)
+    two = struct((heads, 2, n, n), bf16)
+    return pl.pallas_call(
+        forward_kernel,
+        grid_spec=pltpu.PrefetchScalarGridSpec(
+            num_scalar_prefetch=1,
+            grid=(heads,),
+            in_specs=[col] * 4 + [row],
+            out_specs=[col, pair, pair, full],
+        ),
+        out_shape=[struct(q.shape, bf16), two, two, struct((heads, n, n), f32)],
+        compiler_params=grant(),
+        cost_estimate=cost(8),
+        name="attend_forward",
+    )(scal, q, k, v, raw, logit)
+
+
+def attend_backward(scal, q, k, v, raw, logit, inv, ctx, p, dm, heads):
+    n, width = q.shape[0], q.shape[1] // heads
+    col, row, pair, full = head_specs(n, width)
+    return pl.pallas_call(
+        backward_kernel,
+        grid_spec=pltpu.PrefetchScalarGridSpec(
+            num_scalar_prefetch=1,
+            grid=(heads,),
+            in_specs=[col] * 4 + [row, pair, pair, full, col],
+            out_specs=[col] * 4 + [row],
+        ),
+        out_shape=[struct(q.shape, bf16)] * 4 + [struct((heads, 1, n), f32)],
+        compiler_params=grant(),
+        cost_estimate=cost(4),
+        name="attend_backward",
+    )(scal, q, k, v, raw, logit, inv, ctx, p, dm)
+
+
+def whole(kernel, name, micros, outs, scal, *args, scratch=()):
+    vmem = pl.BlockSpec(memory_space=pltpu.VMEM)
+    return pl.pallas_call(
+        kernel,
+        in_specs=[pl.BlockSpec(memory_space=pltpu.SMEM)] + [vmem] * len(args),
+        out_specs=[vmem] * len(outs),
+        out_shape=list(outs),
+        scratch_shapes=list(scratch),
+        compiler_params=grant(),
+        cost_estimate=cost(micros),
+        name=name,
+    )(scal, *args)
+
+
+def head_pick_kernel(scal, wq, wk, wv, wp, *outs):
+    mine, first = scal[0], scal[1] == 0
+    part = wq.shape[0]
+    for k, out in enumerate(outs, 1):
+        at = aligned((mine ^ k) * part, part)
+        out[:, :part] = jnp.where(first, wq[:, at], wv[:, at])
+        out[:, part:] = jnp.where(first, wk[:, at], wp[:, at])
+
+
+def ff_pick_kernel(scal, wg, wu, out):
+    half = out.shape[2] // 2
+    for k in range(4):
+        at = aligned((2 * k + scal[1]) * half, half)
+        out[k, :, :half] = wg[:, at]
+        out[k, :, half:] = wu[:, at]
+
+
+def project_kernel(scal, *refs):
+    toks, own_w, ours, theirs = refs[:4], refs[4:8], refs[8:11], refs[11:14]
+    tok_ref, normed, q_ref, k_ref, v_ref, raw_ref = refs[14:20]
+    logit_ref, beta_ref, gain_a, gain_b, small = refs[20:]
+    mine, first = scal[0], scal[1] == 0
+    part = own_w[0].shape[0]
+    rows = tok_ref.shape[1]
+    heads = beta_ref.shape[0]
+    count = 4 * heads
+    ats = [aligned((mine ^ k) * part, part) for k in range(4)]
+    for k in range(4):
+        lines = toks[k][rows : rows + 4, :].astype(f32)
+        for r in range(count + 2):
+            piece = lines[r // 4 : r // 4 + 1, (r % 4) * part : (r % 4 + 1) * part]
+            small[r : r + 1, ats[k]] = piece
+    gain_a[...] = small[count : count + 1, :]
+    gain_b[...] = small[count + 1 : count + 2, :]
+    for h in range(heads):
+        beta_ref[h : h + 1, :] = small[pl.ds(mine * heads + h, 1), :]
+    for b in range(4):
+        tok_ref[mine ^ b] = toks[b][:rows, :]
+        x = toks[b][:rows, :].astype(f32)
+        factor = lax.rsqrt(jnp.mean(x * x, axis=-1, keepdims=True) + eps)
+        normed[aligned((mine ^ b) * rows, rows), :] = (x * factor * gain_a[...]).astype(bf16)
+    logit = dot_nt(beta_ref[...].astype(bf16), normed[...])
+    for h in range(heads):
+        logit_ref[h] = logit[h : h + 1]
+    n_own = normed[:, ats[0]]
+    sums = [dot_nn(n_own, w[:, ats[0]]) for w in own_w]
+    left, right = jnp.concatenate(sums[:2], 1), jnp.concatenate(sums[2:], 1)
+    a, b = jnp.where(first, left, right), jnp.where(first, right, left)
+    for k in range(1, 4):
+        n_k = normed[:, ats[k]]
+        a = a + dot_nn(n_k, ours[k - 1][...])
+        b = b + dot_nn(n_k, theirs[k - 1][...])
+    qk, vp = jnp.where(first, a, b), jnp.where(first, b, a)
+    q_ref[...] = qk[:, :part].astype(bf16)
+    k_ref[...] = qk[:, part:].astype(bf16)
+    v_ref[...] = vp[:, :part].astype(bf16)
+    raw_ref[...] = vp[:, part:]
+
+
+def live_rows(scal, rows):
+    at = scal[0] * rows + lax.broadcasted_iota(jnp.int32, (rows, 1), 0)
+    return jnp.where(at < scal[2], 1.0, 0.0)
+
+
+def block_sum(ref):
+    return (ref[0].astype(f32) + ref[1].astype(f32)) + (ref[2].astype(f32) + ref[3].astype(f32))
+
+
+def middle_kernel(scal, tok, gain, come, stream_ref, normed_ref, square_ref):
+    rows = stream_ref.shape[0]
+    attn = live_rows(scal, rows) * block_sum(come)
+    square_ref[...] = jnp.sum(attn * attn, axis=0, keepdims=True)
+    stream = tok[...].astype(f32) + attn
+    stream_ref[...] = stream
+    factor = lax.rsqrt(jnp.mean(stream * stream, axis=-1, keepdims=True) + eps)
+    normed = (stream * factor * gain[...]).astype(bf16)
+    for k in range(4):
+        normed_ref[k] = normed
+
+
+def feed_kernel(scal, n_two, c0, c1, c2, c3, w_down, ours, theirs, *refs):
+    hid_a, hid_b, dgu_a, dgu_b, d_feed = refs
+    core = scal[1]
+    rows = c0.shape[0]
+    for k, piece in enumerate((c0, c1, c2, c3)):
+        d_feed[aligned((scal[0] ^ k) * rows, rows), :] = piece[...]
+    part = ours.shape[1]
+    half = hid_a.shape[1]
+    for which, ws, hid, dgu in ((core, ours, hid_a, dgu_a), (1 - core, theirs, hid_b, dgu_b)):
+        gu = 0.0
+        for k in range(4):
+            gu = gu + dot_nn(n_two[:, k * part : (k + 1) * part], ws[k])
+        gate, up = gu[:, :half], gu[:, half:]
+        d_hid = dot_nt(d_feed[...], w_down[aligned(which * half, half), :])
+        sig = jax.nn.sigmoid(gate)
+        act = gate * sig
+        hid[...] = (act * up).astype(bf16)
+        dgu[:, :half] = (d_hid * up * sig * (1.0 + gate * (1.0 - sig))).astype(bf16)
+        dgu[:, half:] = (d_hid * act).astype(bf16)
+
+
+def feed_back_kernel(scal, dgu_a, dgu_b, ours, theirs, out):
+    part = ours.shape[1]
+    for k in range(4):
+        d_n = dot_nt(dgu_a[...], ours[k]) + dot_nt(dgu_b[...], theirs[k])
+        out[:, k * part : (k + 1) * part] = d_n.astype(bf16)
+
+
+def norm_two_kernel(scal, stream_ref, cot, gain, come, d_stream_ref, d_attn_ref, gain_ref):
+    rows = stream_ref.shape[0]
+    live = live_rows(scal, rows)
+    d_n = block_sum(come)
+    stream = stream_ref[...]
+    factor = lax.rsqrt(jnp.mean(stream * stream, axis=-1, keepdims=True) + eps)
+    scaled = d_n * gain[...]
+    mean = jnp.mean(stream * scaled, axis=-1, keepdims=True)
+    d_stream = cot[...].astype(f32) * live + factor * scaled - stream * (factor**3 * mean)
+    d_stream_ref[...] = d_stream
+    d_attn = (live * d_stream).astype(bf16)
+    for k in range(4):
+        d_attn_ref[k] = d_attn
+    gain_ref[...] = jnp.sum(d_n * stream * factor, axis=0, keepdims=True)
+
+
+def input_kernel(scal, tok, dq, dk, dv, dr, dl, beta, hid_a, hid_b, w_down, *refs):
+    own_w, ours, theirs, (out, gain_ref) = refs[:4], refs[4:7], refs[7:10], refs[10:]
+    mine, core = scal[0], scal[1]
+    first = core == 0
+    part = own_w[0].shape[0]
+    rows = tok.shape[1]
+    half = hid_a.shape[1]
+    qk = jnp.concatenate([dq[...], dk[...]], 1)
+    vp = jnp.concatenate([dv[...], dr[...]], 1)
+    x, y = jnp.where(first, qk, vp), jnp.where(first, vp, qk)
+    d_logit = jnp.concatenate([dl[h] for h in range(dl.shape[0])], 0).astype(bf16)
+    factors = []
+    for b in range(4):
+        t = tok[b].astype(f32)
+        factors.append(lax.rsqrt(jnp.mean(t * t, axis=-1, keepdims=True) + eps))
+    for k in range(4):
+        at = aligned((mine ^ k) * part, part)
+        d_n = dot_tn(d_logit, beta[:, at].astype(bf16))
+        if k == 0:
+            for d, w in zip((dq, dk, dv, dr), own_w):
+                d_n = d_n + dot_nt(d[...], w[:, at])
+        else:
+            d_n = d_n + dot_nt(x, ours[k - 1][...]) + dot_nt(y, theirs[k - 1][...])
+        total = jnp.zeros((1, part), f32)
+        for b in range(4):
+            piece = d_n[b * rows : (b + 1) * rows]
+            out[b, :rows, at] = piece.astype(bf16)
+            piece = piece * tok[b, :, at].astype(f32) * factors[b]
+            total = total + jnp.sum(piece, axis=0, keepdims=True)
+        gain_ref[:, at] = total
+        cols = slice(k * part, (k + 1) * part)
+        feed = dot_nn(hid_a[...], w_down[aligned(core * half, half), cols])
+        feed = feed + dot_nn(hid_b[...], w_down[aligned((1 - core) * half, half), cols])
+        for b in range(4):
+            out[b, rows:, cols] = feed[b * rows : (b + 1) * rows].astype(bf16)
+
+
+def last_kernel(scal, tok, gain, come, d_stream, stream, grad_out, out, square_ref):
+    rows = tok.shape[0]
+    live = live_rows(scal, rows)
+    x = tok[...].astype(f32)
+    both = block_sum(come)
+    d_n, feed = both[:rows], live * both[rows:]
+    factor = lax.rsqrt(jnp.mean(x * x, axis=-1, keepdims=True) + eps)
+    scaled = d_n * gain[...]
+    mean = jnp.mean(x * scaled, axis=-1, keepdims=True)
+    grad_out[...] = (d_stream[...] + factor * scaled - x * (factor**3 * mean)).astype(bf16)
+    square_ref[...] = jnp.sum(feed * feed, axis=0, keepdims=True)
+    out[...] = (live * stream[...] + feed).astype(bf16)
+
+
+def head_grads_kernel(scal, *refs):
+    ours, theirs, outs = refs[:3], refs[3:6], refs[6:]
+    first = scal[1] == 0
+    part, width = outs[0].shape
+    for k in range(5):
+        at = slice((k % 2) * part, (k % 2 + 1) * part)
+        a, b = ours[k // 2][at, :], theirs[k // 2][at, :]
+        low, high = jnp.where(first, a, b).astype(f32), jnp.where(first, b, a).astype(f32)
+        if k == 0:
+            outs[4][:, : width // 2] = low
+            outs[4][:, width // 2 :] = high
+        else:
+            at = slice((k - 1) * part, k * part)
+            outs[0][:, at] = low[:, :part]
+            outs[1][:, at] = low[:, part:]
+            outs[2][:, at] = high[:, :part]
+            outs[3][:, at] = high[:, part:]
+
+
+def ff_grads_kernel(scal, ours, theirs_low, theirs_high, gate, up):
+    first = scal[1] == 0
+    half = ours.shape[2] // 2
+    for k in range(4):
+        a, b = ours[k], (theirs_low, theirs_high)[k // 2][k % 2]
+        for i, v in enumerate((jnp.where(first, a, b), jnp.where(first, b, a))):
+            at = slice((2 * k + i) * half, (2 * k + i + 1) * half)
+            gate[:, at] = v[:, :half].astype(f32)
+            up[:, at] = v[:, half:].astype(f32)
+
+
+def blocked(kernel, name, flag, *args):
+    rows, width = args[0].shape
+    step = max(s for s in (384, 256, 208, 200, 192, 128, 80) if rows % s == 0)
+    spec = pl.BlockSpec((step, width), lambda i: (i, 0))
+    return pl.pallas_call(
+        kernel,
+        grid=(rows // step,),
+        in_specs=[pl.BlockSpec(memory_space=pltpu.SMEM)] + [spec] * len(args),
+        out_specs=spec,
+        out_shape=struct((rows, width), bf16),
+        compiler_params=grant(),
+        cost_estimate=cost(1),
+        name=name,
+    )(flag, *args)
+
+
+def add_kernel(flag, a, b, out):
+    out[...] = (a[...].astype(f32) + b[...].astype(f32)).astype(bf16)
+
+
+def choose_kernel(flag, a, b, out):
+    out[...] = jnp.where(flag[0] == 1, a[...], b[...])
+
+
+def down_grads_kernel(scal, a0, a1, b0, b1, out):
+    first = scal[1] == 0
+    rows = a0.shape[0]
+    for i, (a, b) in enumerate(((a0, b0), (a1, b1))):
+        a, b = a[...], b[...]
+        out[i * rows : (i + 1) * rows, :] = jnp.where(first, a, b).astype(f32)
+        out[(i + 2) * rows : (i + 3) * rows, :] = jnp.where(first, b, a).astype(f32)
+
+
+def out_kernel(scal, mixed, w_out, out):
+    out[...] = dot_nn(mixed[...], w_out[...]).astype(bf16)
+
+SHARDS = 4
+CHIPS = 4
+
+
+def shard_exchange(blocks):
+    return lax.all_to_all(blocks, "shard", 0, 0)
+
+
+def shard_gather(value):
+    return shard_exchange(jnp.broadcast_to(value[None], (SHARDS,) + value.shape))
+
+
+def shard_swap(value, k):
+    return lax.ppermute(value, "shard", [(i, i ^ k) for i in range(SHARDS)])
+
+
+def core_swap(value):
+    return lax.ppermute(value, "rep", [(i, i ^ 1) for i in range(2 * CHIPS)])
+
+
+def chip_send(value, pairs):
+    return lax.ppermute(value, "rep", [(2 * a + c, 2 * b + c) for a, b in pairs for c in (0, 1)])
+
+
+def take_rows(value, at, size):
+    return lax.dynamic_slice_in_dim(value, at, size, axis=0)
+
+
+def after(value, *others):
+    return lax.optimization_barrier((value,) + others)[0]
+
+
+def product_low(left, right, add=None):
+    total = dot_tn(left, right)
+    return (total if add is None else total + add.astype(f32)).astype(bf16)
+
+
+class ChipSum:
+    def __init__(self, hub):
+        self.hub = hub.astype(jnp.int32).reshape(1)
+        self.own, self.come, self.pair, self.other, self.total, self.back, self.out = (
+            {} for _ in range(7)
+        )
+
+    def send(self, name, value, *deps):
+        self.own[name] = value
+        self.come[name] = chip_send(after(value, *deps) if deps else value, [(0, 1), (3, 2)])
+
+    def cross(self, name, *deps):
+        come = after(self.come[name], *deps) if deps else self.come[name]
+        self.pair[name] = blocked(add_kernel, "pair", self.hub, self.own[name], come)
+        self.other[name] = chip_send(self.pair[name], [(1, 2), (2, 1)])
+        return self.pair[name]
+
+    def give(self, name, *deps):
+        other = after(self.other[name], *deps) if deps else self.other[name]
+        self.total[name] = blocked(add_kernel, "total", self.hub, self.pair[name], other)
+        self.back[name] = chip_send(self.total[name], [(1, 0), (2, 3)])
+        return self.total[name]
+
+    def result(self, name, *deps):
+        back = after(self.back[name], *deps) if deps else self.back[name]
+        self.out[name] = blocked(choose_kernel, "result", self.hub, self.total[name], back)
+        return self.out[name]
+
+    def play(self, events, tick):
+        for what, name in events:
+            tick = getattr(self, what)(name, tick)
+        return tick
+
+
+def sharded_layer(
+    tokens,
+    cotangent,
+    lengths,
+    gain_one,
+    w_query,
+    w_key,
+    w_value,
+    w_path,
+    w_beta,
+    w_out,
+    gain_two,
+    w_gate,
+    w_up,
+    w_down,
+):
+    rows, width = tokens.shape
+    part = w_query.shape[0]
+    head_count = w_beta.shape[1]
+    heads = head_count // SHARDS
+    ff_part = w_down.shape[0]
+    ff_core = ff_part // 2
+    seq = rows * SHARDS
+    mine = lax.axis_index("shard")
+    rep = lax.axis_index("rep")
+    core = rep % 2
+    chip = rep // 2
+    first_core = core == 0
+    length = lengths[0]
+    scal = jnp.stack([mine, core, length]).astype(jnp.int32)
+    live = (mine * rows + jnp.arange(rows) < length).astype(f32)[:, None]
+    row_f = struct((rows, width), f32)
+    blocks = struct((SHARDS, rows, width), bf16)
+    half = width // 2
+    line = struct((1, width), f32)
+    wide = struct((seq, width), bf16)
+
+    small = jnp.concatenate(
+        [w_beta.T, gain_one[None], gain_two[None], jnp.zeros((2, part), bf16)], 0
+    )
+    extra = small.size // width
+    pad = jnp.zeros((16 - extra, width), bf16)
+    tok = jnp.concatenate([tokens, small.reshape(extra, width), pad], 0)
+    toks = [tok] + [shard_swap(tok, k) for k in range(1, SHARDS)]
+    own_w = (w_query, w_key, w_value, w_path)
+    picked = whole(
+        head_pick_kernel,
+        "pick_heads",
+        1,
+        [struct((part, 2 * part), bf16)] * 3,
+        scal,
+        w_query,
+        w_key,
+        w_value,
+        w_path,
+    )
+    heads_ours = [shard_swap(v, k) for k, v in enumerate(picked, 1)]
+    heads_theirs = [core_swap(v) for v in heads_ours]
+
+    low = struct((seq, part), bf16)
+    tok, normed, queries, keyset, values, raw, logit, beta_rows, gain_a, gain_b = whole(
+        project_kernel,
+        "project",
+        4,
+        [
+            blocks,
+            wide,
+            low,
+            low,
+            low,
+            struct((seq, part), f32),
+            struct((heads, 1, seq), f32),
+            struct((heads, width), f32),
+            line,
+            line,
+        ],
+        scal,
+        *toks,
+        *own_w,
+        *heads_ours,
+        *heads_theirs,
+        scratch=[pltpu.VMEM((16, width), f32)],
+    )
+
+    d_feed_own = (cotangent.astype(f32) * live).astype(bf16)
+    d_feeds = [d_feed_own] + [
+        shard_swap(after(d_feed_own, *toks[1:], *heads_ours), k) for k in range(1, SHARDS)
+    ]
+    (picked,) = whole(
+        ff_pick_kernel,
+        "pick_hidden",
+        1,
+        [struct((SHARDS, part, 2 * ff_core), bf16)],
+        scal,
+        w_gate,
+        w_up,
+    )
+    ff_ours = shard_exchange(after(picked, *toks[1:], *heads_ours))
+    mixed, inv, ctx, probs = attend_forward(
+        scal, queries, keyset, values, raw, logit, heads
+    )
+    (attn_part,) = whole(
+        out_kernel, "out_project", 1, [wide], scal, after(mixed, ff_ours), w_out
+    )
+
+    attn_come = shard_exchange(attn_part.reshape(SHARDS, rows, width))
+    ff_theirs = core_swap(after(ff_ours, attn_part))
+    stream, normed_two, attn_square = whole(
+        middle_kernel,
+        "residual_norm",
+        1,
+        [row_f, blocks, line],
+        scal,
+        tokens,
+        gain_b,
+        after(attn_come, *d_feeds[1:]),
+    )
+    n_two = shard_exchange(normed_two).reshape(seq, width)
+
+    hid = struct((seq, ff_core), bf16)
+    dgu = struct((seq, 2 * ff_core), bf16)
+    ff_half = ff_core // 2
+    hid_a, hid_b, dgu_a, dgu_b, d_feed = whole(
+        feed_kernel,
+        "feed",
+        6,
+        [hid, hid, dgu, dgu, wide],
+        scal,
+        n_two,
+        *d_feeds,
+        w_down,
+        ff_ours,
+        ff_theirs,
+    )
+
+    zsum = ChipSum((chip == 1) | (chip == 2))
+    down_theirs = product_low(hid_b, d_feed)
+    down_come = core_swap(down_theirs)
+    ff_theirs_grad = product_low(n_two, after(dgu_b, down_theirs))
+    ff_come = core_swap(ff_theirs_grad)
+    (d_n_part,) = whole(
+        feed_back_kernel,
+        "feed_back",
+        3,
+        [wide],
+        scal,
+        after(dgu_a, ff_theirs_grad),
+        dgu_b,
+        ff_ours,
+        ff_theirs,
+    )
+    tick = d_n_part
+    for i in range(2):
+        at = slice(i * (ff_core // 2), (i + 1) * (ff_core // 2))
+        tick = product_low(after(hid_a, tick)[:, at], d_feed, down_come[at])
+        zsum.send(f"down{i}", tick)
+    for i in range(2):
+        at = slice(i * 2 * part, (i + 1) * 2 * part)
+        tick = product_low(n_two[:, at], after(dgu_a, tick), ff_come[at])
+        zsum.send(f"ff{i}", tick)
+    d_n_come = shard_exchange(after(d_n_part, tick).reshape(SHARDS, rows, width))
+
+    d_stream, d_attn_own, part_gain_b = whole(
+        norm_two_kernel,
+        "norm_two_back",
+        1,
+        [row_f, blocks, line],
+        scal,
+        stream,
+        cotangent,
+        gain_b,
+        d_n_come,
+    )
+    tick = zsum.play([("cross", "down0")], d_attn_own)
+    d_attn = shard_exchange(after(d_attn_own, tick)).reshape(seq, width)
+    tick = zsum.play([("cross", "down1")], d_attn)
+    d_attn = after(d_attn, tick)
+
+    d_mixed = dot_nt(d_attn, w_out).astype(bf16)
+    d_query, d_key, d_value, d_raw, d_logit = attend_backward(
+        scal, queries, keyset, values, raw, logit, inv, ctx, probs, d_mixed, heads
+    )
+    tick = zsum.play([("give", "down0"), ("give", "down1"), ("cross", "ff0")], d_logit)
+
+    qk = jnp.concatenate([d_query, d_key], 1)
+    vp = jnp.concatenate([d_value, d_raw], 1)
+    keep = after(jnp.where(first_core, vp, qk), tick)
+    p_theirs = [product_low(normed[:, i * 2 * part : (i + 1) * 2 * part], keep) for i in range(2)]
+    come = [core_swap(v) for v in p_theirs]
+    g_out_theirs = product_low(
+        mixed, lax.dynamic_slice_in_dim(after(d_attn, *p_theirs), (1 - core) * half, half, axis=1)
+    )
+    g_out_come = core_swap(g_out_theirs)
+    tick = zsum.play([("cross", "ff1")], g_out_theirs)
+    keep = after(jnp.where(first_core, qk, vp), tick)
+    grad = [
+        product_low(normed[:, i * 2 * part : (i + 1) * 2 * part], keep, come[i]) for i in range(2)
+    ]
+    grad = jnp.concatenate(grad, 0)
+    grad_home = shard_exchange(grad.reshape(SHARDS, part, 2 * part))
+    last_part, part_gain_a = whole(
+        input_kernel,
+        "input_back",
+        4,
+        [struct((SHARDS, 2 * rows, width), bf16), line],
+        scal,
+        tok,
+        d_query,
+        d_key,
+        d_value,
+        d_raw,
+        after(d_logit, grad),
+        beta_rows,
+        hid_a,
+        hid_b,
+        w_down,
+        *own_w,
+        *heads_ours,
+        *heads_theirs,
+    )
+    g_out = product_low(
+        mixed,
+        lax.dynamic_slice_in_dim(after(d_attn, grad), core * half, half, axis=1),
+        g_out_come,
+    )
+    tick = zsum.play([("result", "down0")], part_gain_a)
+    grad_home = after(grad_home, tick)
+    zsum.send("first", jnp.concatenate([g_out, grad_home[0]], 0))
+    zsum.send("second", grad_home[1:3].reshape(2 * part, 2 * part))
+    tick = zsum.play([("give", "ff0"), ("result", "down1")], grad_home)
+    last_come = shard_exchange(after(last_part, zsum.own["first"]))
+    tick = zsum.play([("give", "ff1"), ("cross", "first"), ("result", "ff0")], tick)
+    input_grad, output, feed_square = whole(
+        last_kernel,
+        "last",
+        1,
+        [struct((rows, width), bf16), struct((rows, width), bf16), line],
+        scal,
+        tokens,
+        gain_a,
+        after(last_come, tick),
+        d_stream,
+        stream,
+    )
+    tick = zsum.play([("cross", "second"), ("give", "first"), ("result", "ff1")], feed_square)
+
+    part_beta = dot_nn(d_logit[:, 0].astype(bf16), normed)
+    pack = jnp.concatenate([part_beta, part_gain_a, part_gain_b], 0)
+    pack = pack.reshape(heads + 2, SHARDS, part).transpose(1, 0, 2)
+    own_tok = tokens.astype(f32)
+    squares = jnp.stack(
+        [
+            jnp.sum(live * own_tok * own_tok),
+            jnp.sum(attn_square),
+            jnp.sum(feed_square),
+            jnp.sum(live),
+        ]
+    )
+    squares = jnp.concatenate([squares, jnp.zeros((part - 4,), f32)])
+    pack = jnp.concatenate([pack, jnp.broadcast_to(squares, (SHARDS, 1, part))], 1)
+    pack = shard_exchange(pack)
+    pack = jnp.concatenate(
+        [
+            pack[:, :heads].reshape(head_count, part),
+            jnp.sum(pack[:, heads:], axis=0),
+            jnp.zeros((1, part), f32),
+        ],
+        0,
+    )
+    pack = pack + core_swap(pack)
+    pack_hi = pack.astype(bf16)
+    pack_lo = (pack - pack_hi.astype(f32)).astype(bf16)
+    pack = jnp.concatenate([pack_hi, pack_lo], 1)
+    zsum.send("third", jnp.concatenate([grad_home[SHARDS - 1], pack], 0))
+    tick = zsum.play([("cross", "third"), ("give", "second"), ("result", "first"), ("give", "third")], tick)
+    ff_sum = jnp.concatenate([zsum.out["ff0"], zsum.out["ff1"]], 0)
+    ff_sum = shard_exchange(ff_sum.reshape(SHARDS, part, 2 * ff_core))
+    ff_sum = after(ff_sum, tick)
+    ff_other = [core_swap(ff_sum[:2]), core_swap(ff_sum[2:])]
+    tick = zsum.play([("result", "second")], ff_sum)
+    ff_grad = struct((part, SHARDS * ff_part), f32)
+    grad_gate, grad_up = whole(
+        ff_grads_kernel, "ff_grads", 4, [ff_grad] * 2, scal, ff_sum, after(ff_other[0], tick), ff_other[1]
+    )
+    tick = zsum.play([("result", "third")], grad_gate)
+    last = zsum.out["third"]
+    pack = last[part:, :part].astype(f32) + last[part:, part:].astype(f32)
+    grad_beta = pack[:head_count].T
+    grad_gain_a, grad_gain_b = pack[head_count], pack[head_count + 1]
+    sq_input, sq_attn, sq_feed, live_total = (pack[head_count + 2, i] for i in range(4))
+    denom = live_total * width
+
+    downs = [zsum.out["down0"], zsum.out["down1"]]
+    (grad_down,) = whole(
+        down_grads_kernel, "down_grads", 2, [struct((ff_part, width), f32)], scal, *downs, *map(core_swap, downs)
+    )
+    ours = (zsum.out["first"], zsum.out["second"], last)
+    theirs = [core_swap(v) for v in (zsum.out["first"], zsum.out["second"], last[:part])]
+    head_grad = struct((part, width), f32)
+    grad_query, grad_key, grad_value, grad_path, grad_out = whole(
+        head_grads_kernel, "head_grads", 3, [head_grad] * 5, scal, *ours, *theirs
+    )
+    return (
+        output,
+        input_grad,
+        grad_gain_a,
+        grad_query,
+        grad_key,
+        grad_value,
+        grad_path,
+        grad_beta,
+        grad_out,
+        grad_gain_b,
+        grad_gate,
+        grad_up,
+        grad_down,
+        jnp.sqrt(sq_input / denom),
+        jnp.sqrt(sq_attn / denom),
+        jnp.sqrt(sq_feed / denom),
+    )
+
+
+def pick(mesh):
+    def layer(*args):
+        head_count, ff_part = args[8].shape[1], args[13].shape[0]
+        fits = mesh.shape["shard"] == SHARDS and mesh.shape["rep"] == 2 * CHIPS
+        fits = fits and head_count % SHARDS == 0 and ff_part % 256 == 0
+        fits = fits and args[4].shape[1] == 128 * head_count and args[0].shape[0] == 128
+        return (sharded_layer if fits else gathered_layer)(*args)
+
+    return layer
+
+
 def solution(mesh):
     return jax.shard_map(
-        per_device,
+        pick(mesh),
         mesh=mesh,
         in_specs=(
             P(("rep", "shard"), None),

time: 2000 us -> 612 us (0.31)
  the two profiles are of different devices: /device:TPU:0 before, /device:TPU:19 now
where the time goes in v2:
time: 612 us; the launch traced here: 601 us
  waiting for transfers between devices  189 us (31%)
  Pallas kernels  185 us (30%)
  starting transfers between devices  108 us (18%)
  matrix products  46.8 us (8%)
  local copies, waits for them, and re-layouts  24.4 us (4%)
  blocking collectives  22.8 us (4%)
  other arithmetic  16.9 us (3%)
  between operations  8.4 us (1%)
    ppermute x21, waiting for transfers between devices, chip_send(): lax.ppermute(value, 'rep', [(2 * a + c, 2 * b + c) for a, b in pairs for...  102 us
    pallas_call x13, Pallas kernels, whole(): pl.pallas_call(kernel, in_specs=[pl.BlockSpec(memory_space=pltpu.SMEM)] +...  92.4 us
    ppermute x9, waiting for transfers between devices, shard_swap(): return lax.ppermute(value, 'shard', [(i, i ^ k) for i in range(SHARDS)])  64.4 us
    pallas_call x21, Pallas kernels, blocked(): pl.pallas_call(kernel, grid=(rows // step,), in_specs=[pl.BlockSpec(memor...  53.5 us
    ppermute x21, starting transfers between devices, chip_send(): lax.ppermute(value, 'rep', [(2 * a + c, 2 * b + c) for a, b in pairs for...  47.5 us
    dot_general x12, matrix products, dot_tn(): lax.dot_general(a, b, (((0,), (0,)), ((), ())), preferred_element_type=f32)  41.6 us
    all_to_all x8, starting transfers between devices, shard_exchange(): return lax.all_to_all(blocks, 'shard', 0, 0)  33 us
    all_to_all x1, blocking collectives, shard_exchange(): return lax.all_to_all(blocks, 'shard', 0, 0)  22.8 us
  transfers between devices with their start and end apart: 55, of which 20 were waited for; matrix products, arithmetic and copies ran while one was open for 8% of the time, Pallas kernels for 26%

profile of v2, /device:TPU:19, one launch (start us, length us, event | category | flops | bytes accessed | tf_op | source)
XLA Modules:
  0.0 600.9 jit_solution(5570472610668833598)
XLA Ops:
  6.6 3.8 pick_heads.1
  13.3 2.8 collective-permute-done.2.refs_3_
  16.4 4.8 pick_hidden.1
  21.2 30.8 %collective-permute-done.1.refs_2_ = bf16[144,1536]{1,0:T(8,128)(2,1)S(1)} collective-permute-done((bf16[144,1536]{1,0:T(8,128)(2,1)S(1)}, bf16[144,1536]{1,0:T(8,128)(2,1)S(1)}, u32[]{:S(2)}, u32[]{:S(2)}) %collective-permute-start.1) | collective-permute-done | bytes 442400 | tf_op jit(solution)/shard_map/ppermute | solution.py:872
  53.5 3.9 all-to-all-start
  61.9 10.9 %project.1 = (bf16[4,128,1536]{2,1,0:T(8,128)(2,1)}, bf16[512,1536]{1,0:T(8,128)(2,1)}, bf16[512,384]{1,0:T(8,128)(2,1)}, bf16[512,384]{1,0:T(8,128)(2,1)}, bf16...) custom-call(s32[3]{0:T(128)} %pad_add_fusion.scal, ...), custom_call_target="tpu_custom_call" | custom-call | flops 4000000 | tf_op jit(solution)/shard_map/project/pallas_call | solution.py:606
  72.8 19.1 %attend_forward.1 = (bf16[512,384]{1,0:T(8,128)(2,1)}, bf16[3,2,512,512]{3,2,1,0:T(8,128)(2,1)}, bf16[3,2,512,512]{3,2,1,0:T(8,128)(2,1)}, f32[3,512,512]{2,1,0:T(8,128)}) custom-call(s32[3]{0:T(128)} %pad_add_fusion.scal, bf16[512,384]{1,0:T(8,128)(2,1)} %get-tuple-element.111.q_ref.refs_0_, bf16[512,384]{1,0:T(8,128)(2,1)} %get-tuple-element.112.k_ref.refs_1_, ...), custom_call_target="tpu_custom_call" | custom-call | flops 8000000 | tf_op jit(solution)/shard_map/attend_forward/pallas_call | solution.py:571
  92.7 4.7 out_project.1
  98.8 4.8 all-to-all-start.1
  108.7 22.4 %collective-permute-done.11.c3 = bf16[128,1536]{1,0:T(8,128)(2,1)S(1)} collective-permute-done((bf16[128,1536]{1,0:T(8,128)(2,1)S(1)}, bf16[128,1536]{1,0:T(8,128)(2,1)S(1)}, u32[]{:S(2)}, u32[]{:S(2)}) %collective-permute-start.11) | collective-permute-done | bytes 393248 | tf_op jit(solution)/shard_map/ppermute | solution.py:872
  131.1 8.4 %collective-permute-done.10.c2 = bf16[128,1536]{1,0:T(8,128)(2,1)S(1)} collective-permute-done((bf16[128,1536]{1,0:T(8,128)(2,1)S(1)}, bf16[128,1536]{1,0:T(8,128)(2,1)S(1)}, u32[]{:S(2)}, u32[]{:S(2)}) %collective-permute-start.10) | collective-permute-done | bytes 393248 | tf_op jit(solution)/shard_map/ppermute | solution.py:872
  140.2 3.3 residual_norm.1
  143.5 22.8 %all_to_all.45 = bf16[4,128,1536]{2,1,0:T(8,128)(2,1)} all-to-all(bf16[4,128,1536]{2,1,0:T(8,128)(2,1)} %get-tuple-element.126), channel_id=1, replica_groups=mesh['rep'=8,'shard'=4] {'shard'}, dimensions={0} | all-to-all | bytes 3145728 | tf_op jit(solution)/shard_map/all_to_all | solution.py:864
  166.3 12.8 %feed.1 = (bf16[512,512]{1,0:T(8,128)(2,1)}, bf16[512,512]{1,0:T(8,128)(2,1)}, bf16[512,1024]{1,0:T(8,128)(2,1)}, bf16[512,1024]{1,0:T(8,128)(2,1)}, bf16[512,1536]{1,0:T(8,128)(2,1)}) custom-call(s32[3]{0:T(128)} %pad_add_fusion.scal, bf16[512,1536]{1,0:T(8,128)(2,1)} %bitcast.52, bf16[128,1536]{1,0:T(8,128)(2,1)} %copy-done.13, ...), custom_call_target="tpu_custom_call" | custom-call | flops 6000000 | tf_op jit(solution)/shard_map/feed/pallas_call | solution.py:606
  179.2 3.9 convolution_convert_fusion.1
  183.1 3.6 convolution_convert_fusion
  188.5 9.3 %feed_back.1 = bf16[512,1536]{1,0:T(8,128)(2,1)} custom-call(s32[3]{0:T(128)} %pad_add_fusion.scal, bf16[512,1024]{1,0:T(8,128)(2,1)} %get-tuple-element.138.dgu_a, bf16[512,1024]{1,0:T(8,128)(2,1)} %get-tuple-element.132.dgu_b, bf16[4,384,1024]{2,1,0:T(8,128)(2,1)} %copy-done.1, bf16[4,384,1024]{2,1,0:T(8,128)(2,1)} %collective-permute-done.12.theirs), custom_call_target="tpu_custom_call" | custom-call | flops 3000000 | tf_op jit(solution)/shard_map/feed_back/pallas_call | solution.py:606
  197.8 2.6 fusion.a
  200.4 2.7 fusion.1.a
  203.1 3.6 add_convert_fusion.1.a
  206.7 11.9 %add_convert_fusion.a = bf16[768,1024]{1,0:T(8,128)(2,1)S(1)} fusion(bf16[1536,1024]{1,0:T(8,128)(2,1)} %collective-permute-done.14, bf16[512,1024]{1,0:T(8,128)(2,1)S(1)} %copy-done.20, bf16[512,1536]{1,0:T(8,128)(2,1)S(1)} %bitcast.55), kind=kOutput, calls=%fused_computation.2 | convolution fusion | flops 807665664 | bytes 4980736 | tf_op jit(solution)/shard_map/dot_general | solution.py:389
  218.7 4.4 all-to-all-start.3
  224.4 17.2 %all-to-all-done.3.come = bf16[4,128,1536]{2,1,0:T(8,128)(2,1)S(1)} async-done(((bf16[4,128,1536]{2,1,0:T(8,128)(2,1)}), bf16[4,128,1536]{2,1,0:T(8,128)(2,1)S(1)}, u32[]{:S(2)}, u32[]{:S(2)}) %all-to-all-start.3) | async-done | bytes 1572896 | tf_op jit(solution)/shard_map/all_to_all | solution.py:864
  242.7 4.1 norm_two_back.1
  249.4 4.9 all-to-all-start.4
  260.2 13.5 %collective-permute-done.16.b = bf16[256,1536]{1,0:T(8,128)(2,1)} collective-permute-done((bf16[256,1536]{1,0:T(8,128)(2,1)S(1)}, bf16[256,1536]{1,0:T(8,128)(2,1)}, u32[]{:S(2)}, u32[]{:S(2)}) %collective-permute-start.16) | collective-permute-done | bytes 786464 | tf_op jit(solution)/shard_map/ppermute | solution.py:880
  278.2 3.5 convolution_convert_fusion.5.refs_8_
  281.7 20.4 %attend_backward.1 = (bf16[512,384]{1,0:T(8,128)(2,1)}, bf16[512,384]{1,0:T(8,128)(2,1)}, bf16[512,384]{1,0:T(8,128)(2,1)}, bf16[512,384]{1,0:T(8,128)(2,1)}, f32[3,1,512]{2,1,0:T(1,128)}) custom-call(s32[3]{0:T(128)} %pad_add_fusion.scal, bf16[512,384]{1,0:T(8,128)(2,1)} %get-tuple-element.111.q_ref.refs_0_, ...), custom_call_target="tpu_custom_call" | custom-call | flops 4000000 | tf_op jit(solution)/shard_map/attend_backward/pallas_call | solution.py:589
  310.7 3.0 pair.9.a
  313.7 3.0 convolution_convert_fusion.3
  316.8 4.8 collective-permute-start.21
  325.8 15.3 %collective-permute-done.17.b = bf16[768,1024]{1,0:T(8,128)(2,1)} collective-permute-done((bf16[768,1024]{1,0:T(8,128)(2,1)S(1)}, bf16[768,1024]{1,0:T(8,128)(2,1)}, u32[]{:S(2)}, u32[]{:S(2)}) %collective-permute-start.17) | collective-permute-done | bytes 1572896 | tf_op jit(solution)/shard_map/ppermute | solution.py:880
  341.1 3.0 pair.10.a
  349.9 4.1 all-to-all-start.5
  356.1 2.8 collective-permute-start.23
  360.9 3.4 collective-permute-start.28
  364.4 13.7 %input_back.1 = (bf16[4,256,1536]{2,1,0:T(8,128)(2,1)}, f32[1,1536]{1,0:T(1,128)}) custom-call(s32[3]{0:T(128)} %pad_add_fusion.scal, bf16[4,128,1536]{2,1,0:T(8,128)(2,1)} %get-tuple-element.110.tok, bf16[512,384]{1,0:T(8,128)(2,1)} %get-tuple-element.145.dq, bf16[512,384]{1,0:T(8,128)(2,1)} %get-tuple-element.146.dk, ...), custom_call_target="tpu_custom_call" | custom-call | flops 4000000 | tf_op jit(solution)/shard_map/input_back/pallas_call | solution.py:606
  384.3 3.7 all-to-all-start.6
  391.5 5.6 collective-permute-done.25.b
  397.1 2.9 total.9.a
  402.4 3.3 collective-permute-done.29.b
  408.0 22.8 %collective-permute-done.28.b = bf16[768,1024]{1,0:T(8,128)(2,1)} collective-permute-done((bf16[768,1024]{1,0:T(8,128)(2,1)}, bf16[768,1024]{1,0:T(8,128)(2,1)}, u32[]{:S(2)}, u32[]{:S(2)}) %collective-permute-start.28) | collective-permute-done | bytes 1572896 | tf_op jit(solution)/shard_map/ppermute | solution.py:880
  430.8 2.9 total.10.a
  439.9 2.6 pair.11.a
  447.1 2.8 result.9
  451.6 4.3 last.1
  457.2 10.3 %collective-permute-done.34.b = bf16[768,768]{1,0:T(8,128)(2,1)} collective-permute-done((bf16[768,768]{1,0:T(8,128)(2,1)}, bf16[768,768]{1,0:T(8,128)(2,1)}, u32[]{:S(2)}, u32[]{:S(2)}) %collective-permute-start.34) | collective-permute-done | bytes 1179680 | tf_op jit(solution)/shard_map/ppermute | solution.py:880
  467.5 2.7 concatenate.46
  470.9 3.6 all-to-all-start.7
  479.6 2.9 result.10
  482.5 3.4 pad_maximum_fusion
  485.9 3.7 all-to-all-start.8
  489.8 2.7 collective-permute-start.30
  498.8 5.6 collective-permute-start.36
  504.4 8.1 %collective-permute-done.31.b = bf16[400,768]{1,0:T(8,128)(2,1)} collective-permute-done((bf16[400,768]{1,0:T(8,128)(2,1)S(1)}, bf16[400,768]{1,0:T(8,128)(2,1)}, u32[]{:S(2)}, u32[]{:S(2)}) %collective-permute-start.31) | collective-permute-done | bytes 614432 | tf_op jit(solution)/shard_map/ppermute | solution.py:880
  516.6 9.5 %collective-permute-done.37.b = bf16[768,768]{1,0:T(8,128)(2,1)} collective-permute-done((bf16[768,768]{1,0:T(8,128)(2,1)}, bf16[768,768]{1,0:T(8,128)(2,1)}, u32[]{:S(2)}, u32[]{:S(2)}) %collective-permute-start.37) | collective-permute-done | bytes 1179680 | tf_op jit(solution)/shard_map/ppermute | solution.py:880
  528.7 2.6 collective-permute-start.40
  533.8 5.5 collective-permute-done.35.b
  545.6 8.2 %collective-permute-done.40.b = bf16[768,768]{1,0:T(8,128)(2,1)} collective-permute-done((bf16[768,768]{1,0:T(8,128)(2,1)}, bf16[768,768]{1,0:T(8,128)(2,1)}, u32[]{:S(2)}, u32[]{:S(2)}) %collective-permute-start.40) | collective-permute-done | bytes 1179680 | tf_op jit(solution)/shard_map/ppermute | solution.py:880
  553.8 4.9 collective-permute-start.38
  561.3 2.9 collective-permute-start.42
  564.4 5.0 down_grads.1
  570.5 8.4 %ff_grads.1 = (f32[384,4096]{1,0:T(8,128)}, f32[384,4096]{1,0:T(8,128)}) custom-call(s32[3]{0:T(128)} %pad_add_fusion.scal, bf16[4,384,1024]{2,1,0:T(8,128)(2,1)} %copy-done, bf16[2,384,1024]{2,1,0:T(8,128)(2,1)} %copy-done.16, bf16[2,384,1024]{2,1,0:T(8,128)(2,1)} %collective-permute-done.41.theirs_high), custom_call_target="tpu_custom_call" | custom-call | flops 4000000 | tf_op jit(solution)/shard_map/ff_grads/pallas_call | solution.py:606
  589.6 7.5 %head_grads.1 = (f32[384,1536]{1,0:T(8,128)}, f32[384,1536]{1,0:T(8,128)}, f32[384,1536]{1,0:T(8,128)}, f32[384,1536]{1,0:T(8,128)}, f32[384,1536]{1,0:T(8,128)}) custom-call(s32[3]{0:T(128)} %pad_add_fusion.scal, bf16[768,768]{1,0:T(8,128)(2,1)} %result.11.refs_0_, bf16[768,768]{1,0:T(8,128)(2,1)} %result.12.refs_1_, bf16[400,768]{1,0:T(8,128)(2,1)} %result.13.refs_2_, ...), custom_call_target="tpu_custom_call" | custom-call | flops 3000000 | tf_op jit(solution)/shard_map/head_grads/pallas_call | solution.py:606
  (214 shorter events, 130.2 us)
Async XLA Ops:
  4.1 12.0 %copy-start.12 = (bf16[144,1536]{1,0:T(8,128)(2,1)}, bf16[144,1536]{1,0:T(8,128)(2,1)S(1)}, u32[]{:S(2)}) copy-start(bf16[144,1536]{1,0:T(8,128)(2,1)S(1)} %maximum_maximum_fusion.1.refs_0_) | copy-start | bytes 1327108
  4.1 12.0 %collective-permute-start.2 = (bf16[144,1536]{1,0:T(8,128)(2,1)S(1)}, bf16[144,1536]{1,0:T(8,128)(2,1)S(1)}, u32[]{:S(2)}, u32[]{:S(2)}) collective-permute-start(bf16[144,1536]{1,0:T(8,128)(2,1)S(1)} %maximum_maximum_fusion.1.refs_0_), channel_id=1, source_target_pairs={{0,3},{1,2},{2,1},{3,0},{4,7},{5,6},{6,5},{7,4},{8,11},{9,10},{10,... | collective-permute-start | bytes 1327112 | tf_op jit(solution)/shard_map/ppermute | solution.py:872
  10.4 42.3 %collective-permute-start.3 = (bf16[384,768]{1,0:T(8,128)(2,1)}, bf16[384,768]{1,0:T(8,128)(2,1)}, u32[]{:S(2)}, u32[]{:S(2)}) collective-permute-start(bf16[384,768]{1,0:T(8,128)(2,1)} %get-tuple-element.106), channel_id=1, source_target_pairs={{0,1},{1,0},{2,3},{3,2},{4,5},{5,4},{6,7},{7,6},{8,9},{9,8},{10,11... | collective-permute-start | bytes 1769480 | tf_op jit(solution)/shard_map/ppermute | solution.py:872
  11.6 41.1 %collective-permute-start.4 = (bf16[384,768]{1,0:T(8,128)(2,1)}, bf16[384,768]{1,0:T(8,128)(2,1)}, u32[]{:S(2)}, u32[]{:S(2)}) collective-permute-start(bf16[384,768]{1,0:T(8,128)(2,1)} %get-tuple-element.107), channel_id=1, source_target_pairs={{0,2},{1,3},{2,0},{3,1},{4,6},{5,7},{6,4},{7,5},{8,10},{9,11},{10,... | collective-permute-start | bytes 1769480 | tf_op jit(solution)/shard_map/ppermute | solution.py:872
  11.9 40.8 %collective-permute-start.5 = (bf16[384,768]{1,0:T(8,128)(2,1)}, bf16[384,768]{1,0:T(8,128)(2,1)}, u32[]{:S(2)}, u32[]{:S(2)}) collective-permute-start(bf16[384,768]{1,0:T(8,128)(2,1)} %get-tuple-element.108), channel_id=1, source_target_pairs={{0,3},{1,2},{2,1},{3,0},{4,7},{5,6},{6,5},{7,4},{8,11},{9,10},{10,... | collective-permute-start | bytes 1769480 | tf_op jit(solution)/shard_map/ppermute | solution.py:872
  13.1 38.8 %collective-permute-start.1 = (bf16[144,1536]{1,0:T(8,128)(2,1)S(1)}, bf16[144,1536]{1,0:T(8,128)(2,1)S(1)}, u32[]{:S(2)}, u32[]{:S(2)}) collective-permute-start(bf16[144,1536]{1,0:T(8,128)(2,1)S(1)} %maximum_maximum_fusion.1.refs_0_), channel_id=1, source_target_pairs={{0,2},{1,3},{2,0},{3,1},{4,6},{5,7},{6,4},{7,5},{8,10},{9,11},{10,... | collective-permute-start | bytes 1327112 | tf_op jit(solution)/shard_map/ppermute | solution.py:872
  16.1 35.8 %collective-permute-start = (bf16[144,1536]{1,0:T(8,128)(2,1)S(1)}, bf16[144,1536]{1,0:T(8,128)(2,1)S(1)}, u32[]{:S(2)}, u32[]{:S(2)}) collective-permute-start(bf16[144,1536]{1,0:T(8,128)(2,1)S(1)} %maximum_maximum_fusion.1.refs_0_), channel_id=1, source_target_pairs={{0,1},{1,0},{2,3},{3,2},{4,5},{5,4},{6,7},{7,6},{8,9},{9,8},{10,11... | collective-permute-start | bytes 1327112 | tf_op jit(solution)/shard_map/ppermute | solution.py:872
  53.5 39.3 %all-to-all-start = ((bf16[4,384,1024]{2,1,0:T(8,128)(2,1)}), bf16[4,384,1024]{2,1,0:T(8,128)(2,1)S(1)}, u32[]{:S(2)}, u32[]{:S(2)}) async-start(bf16[4,384,1024]{2,1,0:T(8,128)(2,1)} %pick_hidden.1), calls=%async_computation | async-start | bytes 6291456 | tf_op jit(solution)/shard_map/all_to_all | solution.py:864
  57.4 2.8 collective-permute-start.6
  58.2 2.8 collective-permute-start.7
  58.2 3.7 collective-permute-start.8
  97.4 69.0 %collective-permute-start.12 = (bf16[4,384,1024]{2,1,0:T(8,128)(2,1)S(1)}, bf16[4,384,1024]{2,1,0:T(8,128)(2,1)}, u32[]{:S(2)}, u32[]{:S(2)}) collective-permute-start(bf16[4,384,1024]{2,1,0:T(8,128)(2,1)S(1)} %all-to-all-done.ours), channel_id=1, source_target_pairs={{0,4},{4,0},{8,12},{12,8},{16,20},{20,16},{24,28},{28,24},{1,5},{5... | collective-permute-start | bytes 9437192 | tf_op jit(solution)/shard_map/ppermute | solution.py:876
  98.8 41.5 %all-to-all-start.1 = ((bf16[4,128,1536]{2,1,0:T(8,128)(2,1)}), bf16[4,128,1536]{2,1,0:T(8,128)(2,1)}, u32[]{:S(2)}, u32[]{:S(2)}) async-start(bf16[4,128,1536]{2,1,0:T(8,128)(2,1)} %bitcast.56), calls=%async_computation.1 | async-start | bytes 3145728 | tf_op jit(solution)/shard_map/all_to_all | solution.py:864
  106.0 25.1 %collective-permute-start.11 = (bf16[128,1536]{1,0:T(8,128)(2,1)S(1)}, bf16[128,1536]{1,0:T(8,128)(2,1)S(1)}, u32[]{:S(2)}, u32[]{:S(2)}) collective-permute-start(bf16[128,1536]{1,0:T(8,128)(2,1)S(1)} %get-tuple-element.123.c0), channel_id=1, source_target_pairs={{0,3},{1,2},{2,1},{3,0},{4,7},{5,6},{6,5},{7,4},{8,11},{9,10},{10,... | collective-permute-start | bytes 1179656 | tf_op jit(solution)/shard_map/ppermute | solution.py:872
  107.2 32.3 %collective-permute-start.10 = (bf16[128,1536]{1,0:T(8,128)(2,1)S(1)}, bf16[128,1536]{1,0:T(8,128)(2,1)S(1)}, u32[]{:S(2)}, u32[]{:S(2)}) collective-permute-start(bf16[128,1536]{1,0:T(8,128)(2,1)S(1)} %get-tuple-element.123.c0), channel_id=1, source_target_pairs={{0,2},{1,3},{2,0},{3,1},{4,6},{5,7},{6,4},{7,5},{8,10},{9,11},{10,... | collective-permute-start | bytes 1179656 | tf_op jit(solution)/shard_map/ppermute | solution.py:872
  107.3 33.0 %collective-permute-start.9 = (bf16[128,1536]{1,0:T(8,128)(2,1)S(1)}, bf16[128,1536]{1,0:T(8,128)(2,1)}, u32[]{:S(2)}, u32[]{:S(2)}) collective-permute-start(bf16[128,1536]{1,0:T(8,128)(2,1)S(1)} %get-tuple-element.123.c0), channel_id=1, source_target_pairs={{0,1},{1,0},{2,3},{3,2},{4,5},{5,4},{6,7},{7,6},{8,9},{9,8},{10,11... | collective-permute-start | bytes 1179656 | tf_op jit(solution)/shard_map/ppermute | solution.py:872
  131.1 35.2 %copy-start.30 = (bf16[128,1536]{1,0:T(8,128)(2,1)}, bf16[128,1536]{1,0:T(8,128)(2,1)S(1)}, u32[]{:S(2)}) copy-start(bf16[128,1536]{1,0:T(8,128)(2,1)S(1)} %collective-permute-done.11.c3) | copy-start | bytes 1179652
  186.6 16.5 %collective-permute-start.14 = (bf16[1536,1024]{1,0:T(8,128)(2,1)}, bf16[1536,1024]{1,0:T(8,128)(2,1)}, u32[]{:S(2)}, u32[]{:S(2)}) collective-permute-start(bf16[1536,1024]{1,0:T(8,128)(2,1)} %convolution_convert_fusion), channel_id=1, source_target_pairs={{0,4},{4,0},{8,12},{12,8},{16,20},{20,16},{24,28},{28,24},{1,5},{5... | collective-permute-start | bytes 9437192 | tf_op jit(solution)/shard_map/ppermute | solution.py:876
  188.5 9.3 %collective-permute-start.13 = (bf16[512,1536]{1,0:T(8,128)(2,1)}, bf16[512,1536]{1,0:T(8,128)(2,1)}, u32[]{:S(2)}, u32[]{:S(2)}) collective-permute-start(bf16[512,1536]{1,0:T(8,128)(2,1)} %convolution_convert_fusion.1), channel_id=1, source_target_pairs={{0,4},{4,0},{8,12},{12,8},{16,20},{20,16},{24,28},{28,24},{1,5},{5... | collective-permute-start | bytes 4718600 | tf_op jit(solution)/shard_map/ppermute | solution.py:876
  188.5 9.3 %copy-start.26 = (bf16[512,512]{1,0:T(8,128)(2,1)S(1)}, bf16[512,512]{1,0:T(8,128)(2,1)}, u32[]{:S(2)}) copy-start(bf16[512,512]{1,0:T(8,128)(2,1)} %get-tuple-element.136.hid_a) | copy-start | bytes 1572868
  188.5 9.3 %copy-start.37 = (bf16[512,1536]{1,0:T(8,128)(2,1)S(1)}, bf16[512,1536]{1,0:T(8,128)(2,1)}, u32[]{:S(2)}) copy-start(bf16[512,1536]{1,0:T(8,128)(2,1)} %get-tuple-element.131) | copy-start | bytes 4718596
  218.7 38.2 %copy-start.14 = (bf16[768,1024]{1,0:T(8,128)(2,1)}, bf16[768,1024]{1,0:T(8,128)(2,1)S(1)}, u32[]{:S(2)}) copy-start(bf16[768,1024]{1,0:T(8,128)(2,1)S(1)} %add_convert_fusion.a) | copy-start | bytes 4718596
  218.7 22.9 %all-to-all-start.3 = ((bf16[4,128,1536]{2,1,0:T(8,128)(2,1)}), bf16[4,128,1536]{2,1,0:T(8,128)(2,1)S(1)}, u32[]{:S(2)}, u32[]{:S(2)}) async-start(bf16[4,128,1536]{2,1,0:T(8,128)(2,1)} %bitcast.6), calls=%async_computation.3 | async-start | bytes 3145728 | tf_op jit(solution)/shard_map/all_to_all | solution.py:864
  223.1 23.8 %collective-permute-start.15 = (bf16[256,1536]{1,0:T(8,128)(2,1)}, bf16[256,1536]{1,0:T(8,128)(2,1)}, u32[]{:S(2)}, u32[]{:S(2)}) collective-permute-start(bf16[256,1536]{1,0:T(8,128)(2,1)} %fusion.a), channel_id=1, source_target_pairs={{0,8},{4,12},{24,16},{28,20},{1,9},{5,13},{25,17},{29,21},{2,10},{... | collective-permute-start | bytes 2359304 | tf_op jit(solution)/shard_map/ppermute | solution.py:880
  249.4 8.8 %copy-start.10 = (bf16[256,1536]{1,0:T(8,128)(2,1)S(1)}, bf16[256,1536]{1,0:T(8,128)(2,1)}, u32[]{:S(2)}) copy-start(bf16[256,1536]{1,0:T(8,128)(2,1)} %pair.7.a) | copy-start | bytes 2359300
  249.4 24.4 %all-to-all-start.4 = ((bf16[4,128,1536]{2,1,0:T(8,128)(2,1)}), bf16[4,128,1536]{2,1,0:T(8,128)(2,1)}, u32[]{:S(2)}, u32[]{:S(2)}) async-start(bf16[4,128,1536]{2,1,0:T(8,128)(2,1)} %get-tuple-element.142), calls=%async_computation.4 | async-start | bytes 3145728 | tf_op jit(solution)/shard_map/all_to_all | solution.py:864
  254.2 19.5 %collective-permute-start.16 = (bf16[256,1536]{1,0:T(8,128)(2,1)S(1)}, bf16[256,1536]{1,0:T(8,128)(2,1)}, u32[]{:S(2)}, u32[]{:S(2)}) collective-permute-start(bf16[256,1536]{1,0:T(8,128)(2,1)S(1)} %copy-done.22), channel_id=1, source_target_pairs={{0,8},{4,12},{24,16},{28,20},{1,9},{5,13},{25,17},{29,21},{2,10},{... | collective-permute-start | bytes 2359304 | tf_op jit(solution)/shard_map/ppermute | solution.py:880
  255.5 55.2 %collective-permute-start.18 = (bf16[768,1024]{1,0:T(8,128)(2,1)}, bf16[768,1024]{1,0:T(8,128)(2,1)}, u32[]{:S(2)}, u32[]{:S(2)}) collective-permute-start(bf16[768,1024]{1,0:T(8,128)(2,1)} %add_convert_fusion.1.a), channel_id=1, source_target_pairs={{0,8},{4,12},{24,16},{28,20},{1,9},{5,13},{25,17},{29,21},{2,10},{... | collective-permute-start | bytes 4718600 | tf_op jit(solution)/shard_map/ppermute | solution.py:880
  256.8 84.3 %collective-permute-start.17 = (bf16[768,1024]{1,0:T(8,128)(2,1)S(1)}, bf16[768,1024]{1,0:T(8,128)(2,1)}, u32[]{:S(2)}, u32[]{:S(2)}) collective-permute-start(bf16[768,1024]{1,0:T(8,128)(2,1)S(1)} %add_convert_fusion.a), channel_id=1, source_target_pairs={{0,8},{4,12},{24,16},{28,20},{1,9},{5,13},{25,17},{29,21},{2,10},{... | collective-permute-start | bytes 4718600 | tf_op jit(solution)/shard_map/ppermute | solution.py:880
  258.1 47.6 %collective-permute-start.20 = (bf16[256,1536]{1,0:T(8,128)(2,1)S(1)}, bf16[256,1536]{1,0:T(8,128)(2,1)}, u32[]{:S(2)}, u32[]{:S(2)}) collective-permute-start(bf16[256,1536]{1,0:T(8,128)(2,1)S(1)} %copy-done.10), channel_id=1, source_target_pairs={{8,16},{12,20},{16,8},{20,12},{9,17},{13,21},{17,9},{21,13},{10,18... | collective-permute-start | bytes 2359304 | tf_op jit(solution)/shard_map/ppermute | solution.py:880
  276.2 32.0 %collective-permute-start.19 = (bf16[256,1536]{1,0:T(8,128)(2,1)}, bf16[256,1536]{1,0:T(8,128)(2,1)}, u32[]{:S(2)}, u32[]{:S(2)}) collective-permute-start(bf16[256,1536]{1,0:T(8,128)(2,1)} %pair.8.a), channel_id=1, source_target_pairs={{8,16},{12,20},{16,8},{20,12},{9,17},{13,21},{17,9},{21,13},{10,18... | collective-permute-start | bytes 2359304 | tf_op jit(solution)/shard_map/ppermute | solution.py:880
  313.7 7.8 %copy-start.24 = (bf16[512,768]{1,0:T(8,128)(2,1)S(1)}, bf16[512,768]{1,0:T(8,128)(2,1)}, u32[]{:S(2)}) copy-start(bf16[512,768]{1,0:T(8,128)(2,1)} %get-tuple-element.154) | copy-start | bytes 2359300
  316.8 27.4 %collective-permute-start.21 = (bf16[768,768]{1,0:T(8,128)(2,1)}, bf16[768,768]{1,0:T(8,128)(2,1)}, u32[]{:S(2)}, u32[]{:S(2)}) collective-permute-start(bf16[768,768]{1,0:T(8,128)(2,1)} %convolution_convert_fusion.3), channel_id=1, source_target_pairs={{0,4},{4,0},{8,12},{12,8},{16,20},{20,16},{24,28},{28,24},{1,5},{5... | collective-permute-start | bytes 3538952 | tf_op jit(solution)/shard_map/ppermute | solution.py:876
  323.4 22.8 %collective-permute-start.22 = (bf16[768,768]{1,0:T(8,128)(2,1)}, bf16[768,768]{1,0:T(8,128)(2,1)}, u32[]{:S(2)}, u32[]{:S(2)}) collective-permute-start(bf16[768,768]{1,0:T(8,128)(2,1)} %convolution_convert_fusion.2), channel_id=1, source_target_pairs={{0,4},{4,0},{8,12},{12,8},{16,20},{20,16},{24,28},{28,24},{1,5},{5... | collective-permute-start | bytes 3538952 | tf_op jit(solution)/shard_map/ppermute | solution.py:876
  349.9 32.3 %all-to-all-start.5 = ((bf16[4,384,768]{2,1,0:T(8,128)(2,1)}), bf16[4,384,768]{2,1,0:T(8,128)(2,1)S(1)}, u32[]{:S(2)}, u32[]{:S(2)}) async-start(bf16[4,384,768]{2,1,0:T(8,128)(2,1)} %bitcast.51), calls=%async_computation.5 | async-start | bytes 4718592 | tf_op jit(solution)/shard_map/all_to_all | solution.py:864
  353.9 24.1 %collective-permute-start.24 = (bf16[256,1536]{1,0:T(8,128)(2,1)S(1)}, bf16[256,1536]{1,0:T(8,128)(2,1)}, u32[]{:S(2)}, u32[]{:S(2)}) collective-permute-start(bf16[256,1536]{1,0:T(8,128)(2,1)S(1)} %copy-done.9), channel_id=1, source_target_pairs={{8,0},{12,4},{16,24},{20,28},{9,1},{13,5},{17,25},{21,29},{10,2},{... | collective-permute-start | bytes 2359304 | tf_op jit(solution)/shard_map/ppermute | solution.py:880
  356.1 24.3 %collective-permute-start.23 = (bf16[384,768]{1,0:T(8,128)(2,1)}, bf16[384,768]{1,0:T(8,128)(2,1)}, u32[]{:S(2)}, u32[]{:S(2)}) collective-permute-start(bf16[384,768]{1,0:T(8,128)(2,1)} %convolution_convert_fusion.4), channel_id=1, source_target_pairs={{0,4},{4,0},{8,12},{12,8},{16,20},{20,16},{24,28},{28,24},{1,5},{5... | collective-permute-start | bytes 1769480 | tf_op jit(solution)/shard_map/ppermute | solution.py:876
  358.9 38.2 %collective-permute-start.25 = (bf16[768,1024]{1,0:T(8,128)(2,1)}, bf16[768,1024]{1,0:T(8,128)(2,1)}, u32[]{:S(2)}, u32[]{:S(2)}) collective-permute-start(bf16[768,1024]{1,0:T(8,128)(2,1)} %pair.9.a), channel_id=1, source_target_pairs={{8,16},{12,20},{16,8},{20,12},{9,17},{13,21},{17,9},{21,13},{10,18... | collective-permute-start | bytes 4718600 | tf_op jit(solution)/shard_map/ppermute | solution.py:880
  360.9 69.8 %collective-permute-start.28 = (bf16[768,1024]{1,0:T(8,128)(2,1)}, bf16[768,1024]{1,0:T(8,128)(2,1)}, u32[]{:S(2)}, u32[]{:S(2)}) collective-permute-start(bf16[768,1024]{1,0:T(8,128)(2,1)} %pair.10.a), channel_id=1, source_target_pairs={{8,16},{12,20},{16,8},{20,12},{9,17},{13,21},{17,9},{21,13},{10,18... | collective-permute-start | bytes 4718600 | tf_op jit(solution)/shard_map/ppermute | solution.py:880
  384.3 65.7 %all-to-all-start.6 = ((bf16[4,256,1536]{2,1,0:T(8,128)(2,1)}), bf16[4,256,1536]{2,1,0:T(8,128)(2,1)S(1)}, u32[]{:S(2)}, u32[]{:S(2)}) async-start(bf16[4,256,1536]{2,1,0:T(8,128)(2,1)} %get-tuple-element.165), calls=%async_computation.6 | async-start | bytes 6291456 | tf_op jit(solution)/shard_map/all_to_all | solution.py:864
  388.0 17.7 %collective-permute-start.29 = (bf16[256,1536]{1,0:T(8,128)(2,1)}, bf16[256,1536]{1,0:T(8,128)(2,1)}, u32[]{:S(2)}, u32[]{:S(2)}) collective-permute-start(bf16[256,1536]{1,0:T(8,128)(2,1)} %total.8.a), channel_id=1, source_target_pairs={{8,0},{12,4},{16,24},{20,28},{9,1},{13,5},{17,25},{21,29},{10,2},{... | collective-permute-start | bytes 2359304 | tf_op jit(solution)/shard_map/ppermute | solution.py:880
  390.2 49.8 %collective-permute-start.27 = (bf16[768,768]{1,0:T(8,128)(2,1)}, bf16[768,768]{1,0:T(8,128)(2,1)}, u32[]{:S(2)}, u32[]{:S(2)}) collective-permute-start(bf16[768,768]{1,0:T(8,128)(2,1)} %pad_maximum_fusion.2.a), channel_id=1, source_target_pairs={{0,8},{4,12},{24,16},{28,20},{1,9},{5,13},{25,17},{29,21},{2,10},{... | collective-permute-start | bytes 3538952 | tf_op jit(solution)/shard_map/ppermute | solution.py:880
  400.0 47.1 %collective-permute-start.26 = (bf16[768,1024]{1,0:T(8,128)(2,1)}, bf16[768,1024]{1,0:T(8,128)(2,1)}, u32[]{:S(2)}, u32[]{:S(2)}) collective-permute-start(bf16[768,1024]{1,0:T(8,128)(2,1)} %total.9.a), channel_id=1, source_target_pairs={{8,0},{12,4},{16,24},{20,28},{9,1},{13,5},{17,25},{21,29},{10,2},{... | collective-permute-start | bytes 4718600 | tf_op jit(solution)/shard_map/ppermute | solution.py:880
  433.7 45.9 %collective-permute-start.32 = (bf16[768,1024]{1,0:T(8,128)(2,1)}, bf16[768,1024]{1,0:T(8,128)(2,1)}, u32[]{:S(2)}, u32[]{:S(2)}) collective-permute-start(bf16[768,1024]{1,0:T(8,128)(2,1)} %total.10.a), channel_id=1, source_target_pairs={{8,0},{12,4},{16,24},{20,28},{9,1},{13,5},{17,25},{21,29},{10,2},{... | collective-permute-start | bytes 4718600 | tf_op jit(solution)/shard_map/ppermute | solution.py:880
  438.5 6.8 %copy-start.33 = (f32[3,1,512]{2,1,0:T(1,128)S(1)}, f32[3,1,512]{2,1,0:T(1,128)}, u32[]{:S(2)}) copy-start(f32[3,1,512]{2,1,0:T(1,128)} %get-tuple-element.158.dl) | copy-start | bytes 18436
  438.5 29.0 %collective-permute-start.34 = (bf16[768,768]{1,0:T(8,128)(2,1)}, bf16[768,768]{1,0:T(8,128)(2,1)}, u32[]{:S(2)}, u32[]{:S(2)}) collective-permute-start(bf16[768,768]{1,0:T(8,128)(2,1)} %bitcast.18.a), channel_id=1, source_target_pairs={{0,8},{4,12},{24,16},{28,20},{1,9},{5,13},{25,17},{29,21},{2,10},{... | collective-permute-start | bytes 3538952 | tf_op jit(solution)/shard_map/ppermute | solution.py:880
  442.5 34.5 %collective-permute-start.33 = (bf16[768,768]{1,0:T(8,128)(2,1)}, bf16[768,768]{1,0:T(8,128)(2,1)}, u32[]{:S(2)}, u32[]{:S(2)}) collective-permute-start(bf16[768,768]{1,0:T(8,128)(2,1)} %pair.11.a), channel_id=1, source_target_pairs={{8,16},{12,20},{16,8},{20,12},{9,17},{13,21},{17,9},{21,13},{10,18... | collective-permute-start | bytes 3538952 | tf_op jit(solution)/shard_map/ppermute | solution.py:880
  470.9 15.1 %all-to-all-start.7 = ((f32[4,6,384]{2,1,0:T(8,128)}), f32[4,6,384]{2,1,0:T(8,128)S(1)}, u32[]{:S(2)}, u32[]{:S(2)}) async-start(f32[4,6,384]{2,1,0:T(8,128)} %pad_maximum_fusion.4), calls=%async_computation.7 | async-start | bytes 98304 | tf_op jit(solution)/shard_map/all_to_all | solution.py:864
  485.9 55.4 %all-to-all-start.8 = ((bf16[4,384,1024]{2,1,0:T(8,128)(2,1)}), bf16[4,384,1024]{2,1,0:T(8,128)(2,1)S(1)}, u32[]{:S(2)}, u32[]{:S(2)}) async-start(bf16[4,384,1024]{2,1,0:T(8,128)(2,1)} %bitcast.50), calls=%async_computation.8 | async-start | bytes 6291456 | tf_op jit(solution)/shard_map/all_to_all | solution.py:864
  489.8 3.6 collective-permute-start.30
  495.4 17.1 %collective-permute-start.31 = (bf16[400,768]{1,0:T(8,128)(2,1)S(1)}, bf16[400,768]{1,0:T(8,128)(2,1)}, u32[]{:S(2)}, u32[]{:S(2)}) collective-permute-start(bf16[400,768]{1,0:T(8,128)(2,1)S(1)} %maximum_maximum_fusion.a), channel_id=1, source_target_pairs={{0,8},{4,12},{24,16},{28,20},{1,9},{5,13},{25,17},{29,21},{2,10},{... | collective-permute-start | bytes 1843208 | tf_op jit(solution)/shard_map/ppermute | solution.py:880
  496.7 29.4 %collective-permute-start.37 = (bf16[768,768]{1,0:T(8,128)(2,1)}, bf16[768,768]{1,0:T(8,128)(2,1)}, u32[]{:S(2)}, u32[]{:S(2)}) collective-permute-start(bf16[768,768]{1,0:T(8,128)(2,1)} %pair.12.a), channel_id=1, source_target_pairs={{8,16},{12,20},{16,8},{20,12},{9,17},{13,21},{17,9},{21,13},{10,18... | collective-permute-start | bytes 3538952 | tf_op jit(solution)/shard_map/ppermute | solution.py:880
  498.8 32.5 %collective-permute-start.36 = (bf16[768,768]{1,0:T(8,128)(2,1)}, bf16[768,768]{1,0:T(8,128)(2,1)}, u32[]{:S(2)}, u32[]{:S(2)}) collective-permute-start(bf16[768,768]{1,0:T(8,128)(2,1)} %total.11.a), channel_id=1, source_target_pairs={{8,0},{12,4},{16,24},{20,28},{9,1},{13,5},{17,25},{21,29},{10,2},{... | collective-permute-start | bytes 3538952 | tf_op jit(solution)/shard_map/ppermute | solution.py:880
  514.5 24.8 %collective-permute-start.35 = (bf16[400,768]{1,0:T(8,128)(2,1)}, bf16[400,768]{1,0:T(8,128)(2,1)}, u32[]{:S(2)}, u32[]{:S(2)}) collective-permute-start(bf16[400,768]{1,0:T(8,128)(2,1)} %pair.13.a), channel_id=1, source_target_pairs={{8,16},{12,20},{16,8},{20,12},{9,17},{13,21},{17,9},{21,13},{10,18... | collective-permute-start | bytes 1843208 | tf_op jit(solution)/shard_map/ppermute | solution.py:880
  528.7 25.2 %collective-permute-start.40 = (bf16[768,768]{1,0:T(8,128)(2,1)}, bf16[768,768]{1,0:T(8,128)(2,1)}, u32[]{:S(2)}, u32[]{:S(2)}) collective-permute-start(bf16[768,768]{1,0:T(8,128)(2,1)} %total.12.a), channel_id=1, source_target_pairs={{8,0},{12,4},{16,24},{20,28},{9,1},{13,5},{17,25},{21,29},{10,2},{... | collective-permute-start | bytes 3538952 | tf_op jit(solution)/shard_map/ppermute | solution.py:880
  544.0 25.4 %collective-permute-start.39 = (bf16[2,384,1024]{2,1,0:T(8,128)(2,1)}, bf16[2,384,1024]{2,1,0:T(8,128)(2,1)S(1)}, u32[]{:S(2)}, u32[]{:S(2)}) collective-permute-start(bf16[2,384,1024]{2,1,0:T(8,128)(2,1)} %get-tuple-element.201), channel_id=1, source_target_pairs={{0,4},{4,0},{8,12},{12,8},{16,20},{20,16},{24,28},{28,24},{1,5},{5... | collective-permute-start | bytes 4718600 | tf_op jit(solution)/shard_map/ppermute | solution.py:876
  545.1 16.2 %copy-start.8 = (bf16[768,768]{1,0:T(8,128)(2,1)S(1)}, bf16[768,768]{1,0:T(8,128)(2,1)}, u32[]{:S(2)}) copy-start(bf16[768,768]{1,0:T(8,128)(2,1)} %result.11.refs_0_) | copy-start | bytes 3538948
  545.1 24.2 %collective-permute-start.41 = (bf16[2,384,1024]{2,1,0:T(8,128)(2,1)}, bf16[2,384,1024]{2,1,0:T(8,128)(2,1)}, u32[]{:S(2)}, u32[]{:S(2)}) collective-permute-start(bf16[2,384,1024]{2,1,0:T(8,128)(2,1)} %get-tuple-element.200), channel_id=1, source_target_pairs={{0,4},{4,0},{8,12},{12,8},{16,20},{20,16},{24,28},{28,24},{1,5},{5... | collective-permute-start | bytes 4718600 | tf_op jit(solution)/shard_map/ppermute | solution.py:876
  545.1 16.2 %collective-permute-start.45 = (bf16[256,1536]{1,0:T(8,128)(2,1)}, bf16[256,1536]{1,0:T(8,128)(2,1)}, u32[]{:S(2)}, u32[]{:S(2)}) collective-permute-start(bf16[256,1536]{1,0:T(8,128)(2,1)} %result.7.a0), channel_id=1, source_target_pairs={{0,4},{4,0},{8,12},{12,8},{16,20},{20,16},{24,28},{28,24},{1,5},{5... | collective-permute-start | bytes 2359304 | tf_op jit(solution)/shard_map/ppermute | solution.py:876
  545.6 18.6 %collective-permute-start.46 = (bf16[256,1536]{1,0:T(8,128)(2,1)}, bf16[256,1536]{1,0:T(8,128)(2,1)}, u32[]{:S(2)}, u32[]{:S(2)}) collective-permute-start(bf16[256,1536]{1,0:T(8,128)(2,1)} %result.8.a1), channel_id=1, source_target_pairs={{0,4},{4,0},{8,12},{12,8},{16,20},{20,16},{24,28},{28,24},{1,5},{5... | collective-permute-start | bytes 2359304 | tf_op jit(solution)/shard_map/ppermute | solution.py:876
  553.8 25.0 %collective-permute-start.38 = (bf16[400,768]{1,0:T(8,128)(2,1)}, bf16[400,768]{1,0:T(8,128)(2,1)}, u32[]{:S(2)}, u32[]{:S(2)}) collective-permute-start(bf16[400,768]{1,0:T(8,128)(2,1)} %total.13.a), channel_id=1, source_target_pairs={{8,0},{12,4},{16,24},{20,28},{9,1},{13,5},{17,25},{21,29},{10,2},{... | collective-permute-start | bytes 1843208 | tf_op jit(solution)/shard_map/ppermute | solution.py:880
  561.3 26.4 %collective-permute-start.42 = (bf16[768,768]{1,0:T(8,128)(2,1)S(1)}, bf16[768,768]{1,0:T(8,128)(2,1)S(1)}, u32[]{:S(2)}, u32[]{:S(2)}) collective-permute-start(bf16[768,768]{1,0:T(8,128)(2,1)S(1)} %copy-done.8), channel_id=1, source_target_pairs={{0,4},{4,0},{8,12},{12,8},{16,20},{20,16},{24,28},{28,24},{1,5},{5... | collective-permute-start | bytes 3538952 | tf_op jit(solution)/shard_map/ppermute | solution.py:876
  564.3 23.5 %collective-permute-start.43 = (bf16[768,768]{1,0:T(8,128)(2,1)}, bf16[768,768]{1,0:T(8,128)(2,1)}, u32[]{:S(2)}, u32[]{:S(2)}) collective-permute-start(bf16[768,768]{1,0:T(8,128)(2,1)} %result.12.refs_1_), channel_id=1, source_target_pairs={{0,4},{4,0},{8,12},{12,8},{16,20},{20,16},{24,28},{28,24},{1,5},{5... | collective-permute-start | bytes 3538952 | tf_op jit(solution)/shard_map/ppermute | solution.py:876
  581.9 5.8 collective-permute-start.44
  (29 other events, 84.6 us)

commit v3 on v2

--- a/solution.py
+++ b/solution.py
@@ -820,6 +820,30 @@
             up[:, at] = v[:, half:].astype(f32)
 
 
+def product_kernel(a, b, c, out):
+    out[...] = (dot_tn(a[...], b[...]) + c[...].astype(f32)).astype(bf16)
+
+
+def product(name, left, right, add, start, size):
+    step = 384
+    rows, width = right.shape
+    line = pl.BlockSpec((step, width), lambda i: (start // step + i, 0))
+    return pl.pallas_call(
+        product_kernel,
+        grid=(size // step,),
+        in_specs=[
+            pl.BlockSpec((rows, step), lambda i: (0, start // step + i)),
+            pl.BlockSpec((rows, width), lambda i: (0, 0)),
+            line,
+        ],
+        out_specs=pl.BlockSpec((step, width), lambda i: (i, 0)),
+        out_shape=struct((size, width), bf16),
+        compiler_params=grant(),
+        cost_estimate=cost(1),
+        name=name,
+    )(left, right, add)
+
+
 def blocked(kernel, name, flag, *args):
     rows, width = args[0].shape
     step = max(s for s in (384, 256, 208, 200, 192, 128, 80) if rows % s == 0)
@@ -1085,7 +1109,7 @@
         zsum.send(f"down{i}", tick)
     for i in range(2):
         at = slice(i * 2 * part, (i + 1) * 2 * part)
-        tick = product_low(n_two[:, at], after(dgu_a, tick), ff_come[at])
+        tick = product(f"ff{i}", n_two, after(dgu_a, tick), ff_come, i * 2 * part, 2 * part)
         zsum.send(f"ff{i}", tick)
     d_n_come = shard_exchange(after(d_n_part, tick).reshape(SHARDS, rows, width))
 
@@ -1102,14 +1126,12 @@
     )
     tick = zsum.play([("cross", "down0")], d_attn_own)
     d_attn = shard_exchange(after(d_attn_own, tick)).reshape(seq, width)
-    tick = zsum.play([("cross", "down1")], d_attn)
-    d_attn = after(d_attn, tick)
 
     d_mixed = dot_nt(d_attn, w_out).astype(bf16)
     d_query, d_key, d_value, d_raw, d_logit = attend_backward(
         scal, queries, keyset, values, raw, logit, inv, ctx, probs, d_mixed, heads
     )
-    tick = zsum.play([("give", "down0"), ("give", "down1"), ("cross", "ff0")], d_logit)
+    tick = zsum.play([("give", "down0"), ("cross", "down1"), ("cross", "ff0")], d_logit)
 
     qk = jnp.concatenate([d_query, d_key], 1)
     vp = jnp.concatenate([d_value, d_raw], 1)
@@ -1120,7 +1142,7 @@
         mixed, lax.dynamic_slice_in_dim(after(d_attn, *p_theirs), (1 - core) * half, half, axis=1)
     )
     g_out_come = core_swap(g_out_theirs)
-    tick = zsum.play([("cross", "ff1")], g_out_theirs)
+    tick = zsum.play([("give", "down1"), ("cross", "ff1")], g_out_theirs)
     keep = after(jnp.where(first_core, qk, vp), tick)
     grad = [
         product_low(normed[:, i * 2 * part : (i + 1) * 2 * part], keep, come[i]) for i in range(2)
@@ -1156,9 +1178,9 @@
     grad_home = after(grad_home, tick)
     zsum.send("first", jnp.concatenate([g_out, grad_home[0]], 0))
     zsum.send("second", grad_home[1:3].reshape(2 * part, 2 * part))
-    tick = zsum.play([("give", "ff0"), ("result", "down1")], grad_home)
+    tick = zsum.play([("give", "ff0")], grad_home)
     last_come = shard_exchange(after(last_part, zsum.own["first"]))
-    tick = zsum.play([("give", "ff1"), ("cross", "first"), ("result", "ff0")], tick)
+    tick = zsum.play([("give", "ff1"), ("result", "down1"), ("cross", "first"), ("result", "ff0")], tick)
     input_grad, output, feed_square = whole(
         last_kernel,
         "last",
@@ -1201,7 +1223,21 @@
     pack_lo = (pack - pack_hi.astype(f32)).astype(bf16)
     pack = jnp.concatenate([pack_hi, pack_lo], 1)
     zsum.send("third", jnp.concatenate([grad_home[SHARDS - 1], pack], 0))
-    tick = zsum.play([("cross", "third"), ("give", "second"), ("result", "first"), ("give", "third")], tick)
+    downs = [zsum.out["down0"], zsum.out["down1"]]
+    others = [core_swap(v) for v in downs]
+    (grad_down,) = whole(
+        down_grads_kernel,
+        "down_grads",
+        2,
+        [struct((ff_part, width), f32)],
+        scal,
+        after(downs[0], tick),
+        downs[1],
+        *others,
+    )
+    tick = zsum.play(
+        [("cross", "third"), ("give", "second"), ("result", "first"), ("give", "third")], grad_down
+    )
     ff_sum = jnp.concatenate([zsum.out["ff0"], zsum.out["ff1"]], 0)
     ff_sum = shard_exchange(ff_sum.reshape(SHARDS, part, 2 * ff_core))
     ff_sum = after(ff_sum, tick)
@@ -1209,7 +1245,7 @@
     tick = zsum.play([("result", "second")], ff_sum)
     ff_grad = struct((part, SHARDS * ff_part), f32)
     grad_gate, grad_up = whole(
-        ff_grads_kernel, "ff_grads", 4, [ff_grad] * 2, scal, ff_sum, after(ff_other[0], tick), ff_other[1]
+        ff_grads_kernel, "ff_grads", 4, [ff_grad] * 2, scal, after(ff_sum, tick), *ff_other
     )
     tick = zsum.play([("result", "third")], grad_gate)
     last = zsum.out["third"]
@@ -1219,10 +1255,6 @@
     sq_input, sq_attn, sq_feed, live_total = (pack[head_count + 2, i] for i in range(4))
     denom = live_total * width
 
-    downs = [zsum.out["down0"], zsum.out["down1"]]
-    (grad_down,) = whole(
-        down_grads_kernel, "down_grads", 2, [struct((ff_part, width), f32)], scal, *downs, *map(core_swap, downs)
-    )
     ours = (zsum.out["first"], zsum.out["second"], last)
     theirs = [core_swap(v) for v in (zsum.out["first"], zsum.out["second"], last[:part])]
     head_grad = struct((part, width), f32)

time: 612 us -> 606 us (level)
  the two profiles are of different devices: /device:TPU:19 before, /device:TPU:0 now
where the time goes in v3:
time: 606 us; the launch traced here: 595 us
  Pallas kernels  192 us (32%)
  waiting for transfers between devices  160 us (26%)
  starting transfers between devices  133 us (22%)
  matrix products  31.4 us (5%)
  local copies, waits for them, and re-layouts  27.7 us (5%)
  blocking collectives  24.9 us (4%)
  other arithmetic  17.8 us (3%)
  between operations  8.46 us (1%)
    pallas_call x13, Pallas kernels, whole(): pl.pallas_call(kernel, in_specs=[pl.BlockSpec(memory_space=pltpu.SMEM)] +...  92 us
    ppermute x21, starting transfers between devices, chip_send(): lax.ppermute(value, 'rep', [(2 * a + c, 2 * b + c) for a, b in pairs for...  83.2 us
    ppermute x21, waiting for transfers between devices, chip_send(): lax.ppermute(value, 'rep', [(2 * a + c, 2 * b + c) for a, b in pairs for...  69.2 us
    ppermute x9, waiting for transfers between devices, shard_swap(): return lax.ppermute(value, 'shard', [(i, i ^ k) for i in range(SHARDS)])  60.4 us
    pallas_call x21, Pallas kernels, blocked(): pl.pallas_call(kernel, grid=(rows // step,), in_specs=[pl.BlockSpec(memor...  53.4 us
    all_to_all x8, starting transfers between devices, shard_exchange(): return lax.all_to_all(blocks, 'shard', 0, 0)  32.6 us
    dot_general x10, matrix products, dot_tn(): lax.dot_general(a, b, (((0,), (0,)), ((), ())), preferred_element_type=f32)  26.2 us
    all_to_all x8, waiting for transfers between devices, shard_exchange(): return lax.all_to_all(blocks, 'shard', 0, 0)  26 us
  transfers between devices with their start and end apart: 55, of which 20 were waited for; matrix products, arithmetic and copies ran while one was open for 8% of the time, Pallas kernels for 26%

profile of v3, /device:TPU:0, one launch (start us, length us, event | category | flops | bytes accessed | tf_op | source)
XLA Modules:
  0.0 594.8 jit_solution(14100528154795325999)
XLA Ops:
  4.1 4.0 collective-permute-start.2
  9.4 3.8 pick_heads.1
  13.8 2.9 collective-permute-start.5
  21.1 4.8 pick_hidden.1
  25.9 27.2 %collective-permute-done.1.refs_2_ = bf16[144,1536]{1,0:T(8,128)(2,1)S(1)} collective-permute-done((bf16[144,1536]{1,0:T(8,128)(2,1)S(1)}, bf16[144,1536]{1,0:T(8,128)(2,1)S(1)}, u32[]{:S(2)}, u32[]{:S(2)}) %collective-permute-start.1) | collective-permute-done | bytes 442400 | tf_op jit(solution)/shard_map/ppermute | solution.py:896
  54.5 3.9 all-to-all-start
  62.5 10.8 %project.1 = (bf16[4,128,1536]{2,1,0:T(8,128)(2,1)}, bf16[512,1536]{1,0:T(8,128)(2,1)}, bf16[512,384]{1,0:T(8,128)(2,1)}, bf16[512,384]{1,0:T(8,128)(2,1)}, bf16...) custom-call(s32[3]{0:T(128)} %pad_add_fusion.scal, ...), custom_call_target="tpu_custom_call" | custom-call | flops 4000000 | tf_op jit(solution)/shard_map/project/pallas_call | solution.py:606
  73.3 19.1 %attend_forward.1 = (bf16[512,384]{1,0:T(8,128)(2,1)}, bf16[3,2,512,512]{3,2,1,0:T(8,128)(2,1)}, bf16[3,2,512,512]{3,2,1,0:T(8,128)(2,1)}, f32[3,512,512]{2,1,0:T(8,128)}) custom-call(s32[3]{0:T(128)} %pad_add_fusion.scal, bf16[512,384]{1,0:T(8,128)(2,1)} %get-tuple-element.111.q_ref.refs_0_, bf16[512,384]{1,0:T(8,128)(2,1)} %get-tuple-element.112.k_ref.refs_1_, ...), custom_call_target="tpu_custom_call" | custom-call | flops 8000000 | tf_op jit(solution)/shard_map/attend_forward/pallas_call | solution.py:571
  94.8 4.7 out_project.1
  99.5 4.5 all-to-all-start.1
  106.5 2.9 collective-permute-start.11
  110.0 23.9 %collective-permute-done.11.c3 = bf16[128,1536]{1,0:T(8,128)(2,1)S(1)} collective-permute-done((bf16[128,1536]{1,0:T(8,128)(2,1)S(1)}, bf16[128,1536]{1,0:T(8,128)(2,1)S(1)}, u32[]{:S(2)}, u32[]{:S(2)}) %collective-permute-start.11) | collective-permute-done | bytes 393248 | tf_op jit(solution)/shard_map/ppermute | solution.py:896
  133.9 7.0 %collective-permute-done.10.c2 = bf16[128,1536]{1,0:T(8,128)(2,1)S(1)} collective-permute-done((bf16[128,1536]{1,0:T(8,128)(2,1)S(1)}, bf16[128,1536]{1,0:T(8,128)(2,1)S(1)}, u32[]{:S(2)}, u32[]{:S(2)}) %collective-permute-start.10) | collective-permute-done | bytes 393248 | tf_op jit(solution)/shard_map/ppermute | solution.py:896
  141.7 3.3 residual_norm.1
  145.0 24.9 %all_to_all.45 = bf16[4,128,1536]{2,1,0:T(8,128)(2,1)} all-to-all(bf16[4,128,1536]{2,1,0:T(8,128)(2,1)} %get-tuple-element.126), channel_id=1, replica_groups=mesh['rep'=8,'shard'=4] {'shard'}, dimensions={0} | all-to-all | bytes 3145728 | tf_op jit(solution)/shard_map/all_to_all | solution.py:888
  169.8 12.8 %feed.1 = (bf16[512,512]{1,0:T(8,128)(2,1)}, bf16[512,512]{1,0:T(8,128)(2,1)}, bf16[512,1024]{1,0:T(8,128)(2,1)}, bf16[512,1024]{1,0:T(8,128)(2,1)}, bf16[512,1536]{1,0:T(8,128)(2,1)}) custom-call(s32[3]{0:T(128)} %pad_add_fusion.scal, bf16[512,1536]{1,0:T(8,128)(2,1)} %bitcast.48, bf16[128,1536]{1,0:T(8,128)(2,1)} %copy-done.14, ...), custom_call_target="tpu_custom_call" | custom-call | flops 6000000 | tf_op jit(solution)/shard_map/feed/pallas_call | solution.py:606
  182.7 3.9 convolution_convert_fusion.1
  186.5 3.6 convolution_convert_fusion
  190.6 9.1 %feed_back.1 = bf16[512,1536]{1,0:T(8,128)(2,1)} custom-call(s32[3]{0:T(128)} %pad_add_fusion.scal, bf16[512,1024]{1,0:T(8,128)(2,1)} %get-tuple-element.138.dgu_a.b, bf16[512,1024]{1,0:T(8,128)(2,1)} %get-tuple-element.132.dgu_b, bf16[4,384,1024]{2,1,0:T(8,128)(2,1)} %copy-done.1, bf16[4,384,1024]{2,1,0:T(8,128)(2,1)} %collective-permute-done.12.theirs), custom_call_target="tpu_custom_call" | custom-call | flops 3000000 | tf_op jit(solution)/shard_map/feed_back/pallas_call | solution.py:606
  202.2 2.9 fusion.1.a
  206.8 3.7 ff0.1.a
  210.5 3.7 ff1.1.a
  214.3 3.6 all-to-all-start.3
  217.8 3.9 collective-permute-start.15
  221.7 15.7 %all-to-all-done.3.come = bf16[4,128,1536]{2,1,0:T(8,128)(2,1)S(1)} async-done(((bf16[4,128,1536]{2,1,0:T(8,128)(2,1)}), bf16[4,128,1536]{2,1,0:T(8,128)(2,1)S(1)}, u32[]{:S(2)}, u32[]{:S(2)}) %all-to-all-start.3) | async-done | bytes 1572896 | tf_op jit(solution)/shard_map/all_to_all | solution.py:888
  238.6 4.1 norm_two_back.1
  246.2 4.6 all-to-all-start.4
  250.8 4.8 collective-permute-start.20
  261.8 7.9 %all-to-all-done.4 = bf16[4,128,1536]{2,1,0:T(8,128)(2,1)} async-done(((bf16[4,128,1536]{2,1,0:T(8,128)(2,1)}), bf16[4,128,1536]{2,1,0:T(8,128)(2,1)}, u32[]{:S(2)}, u32[]{:S(2)}) %all-to-all-start.4) | async-done | bytes 1572896 | tf_op jit(solution)/shard_map/all_to_all | solution.py:888
  269.7 3.5 convolution_convert_fusion.5.refs_8_
  273.2 20.4 %attend_backward.1 = (bf16[512,384]{1,0:T(8,128)(2,1)}, bf16[512,384]{1,0:T(8,128)(2,1)}, bf16[512,384]{1,0:T(8,128)(2,1)}, bf16[512,384]{1,0:T(8,128)(2,1)}, f32[3,1,512]{2,1,0:T(1,128)}) custom-call(s32[3]{0:T(128)} %pad_add_fusion.scal, bf16[512,384]{1,0:T(8,128)(2,1)} %get-tuple-element.111.q_ref.refs_0_, ...), custom_call_target="tpu_custom_call" | custom-call | flops 4000000 | tf_op jit(solution)/shard_map/attend_backward/pallas_call | solution.py:589
  299.6 6.6 %collective-permute-done.17.b = bf16[256,1536]{1,0:T(8,128)(2,1)} collective-permute-done((bf16[256,1536]{1,0:T(8,128)(2,1)}, bf16[256,1536]{1,0:T(8,128)(2,1)}, u32[]{:S(2)}, u32[]{:S(2)}) %collective-permute-start.17) | collective-permute-done | bytes 786464 | tf_op jit(solution)/shard_map/ppermute | solution.py:904
  308.7 3.0 pair.9.a
  311.7 3.1 convolution_convert_fusion.3
  324.0 14.0 %collective-permute-done.16.b = bf16[768,1024]{1,0:T(8,128)(2,1)} collective-permute-done((bf16[768,1024]{1,0:T(8,128)(2,1)S(1)}, bf16[768,1024]{1,0:T(8,128)(2,1)}, u32[]{:S(2)}, u32[]{:S(2)}) %collective-permute-start.16) | collective-permute-done | bytes 1572896 | tf_op jit(solution)/shard_map/ppermute | solution.py:904
  338.0 3.0 pair.10.a
  346.7 4.0 all-to-all-start.5
  355.7 13.5 %input_back.1 = (bf16[4,256,1536]{2,1,0:T(8,128)(2,1)}, f32[1,1536]{1,0:T(1,128)}) custom-call(s32[3]{0:T(128)} %pad_add_fusion.scal, bf16[4,128,1536]{2,1,0:T(8,128)(2,1)} %get-tuple-element.110.tok, bf16[512,384]{1,0:T(8,128)(2,1)} %get-tuple-element.143.dq, bf16[512,384]{1,0:T(8,128)(2,1)} %get-tuple-element.144.dk, ...), custom_call_target="tpu_custom_call" | custom-call | flops 4000000 | tf_op jit(solution)/shard_map/input_back/pallas_call | solution.py:606
  369.2 6.4 %collective-permute-done.24.b = bf16[256,1536]{1,0:T(8,128)(2,1)} collective-permute-done((bf16[256,1536]{1,0:T(8,128)(2,1)S(1)}, bf16[256,1536]{1,0:T(8,128)(2,1)}, u32[]{:S(2)}, u32[]{:S(2)}) %collective-permute-start.24) | collective-permute-done | bytes 786464 | tf_op jit(solution)/shard_map/ppermute | solution.py:904
  381.8 3.9 all-to-all-start.6
  385.8 7.6 %collective-permute-start.27 = (bf16[768,768]{1,0:T(8,128)(2,1)}, bf16[768,768]{1,0:T(8,128)(2,1)}, u32[]{:S(2)}, u32[]{:S(2)}) collective-permute-start(bf16[768,768]{1,0:T(8,128)(2,1)} %pad_maximum_fusion.2.a), channel_id=1, source_target_pairs={{0,8},{4,12},{24,16},{28,20},{1,9},{5,13},{25,17},{29,21},{2,10},{... | collective-permute-start | bytes 3538952 | tf_op jit(solution)/shard_map/ppermute | solution.py:904
  394.7 2.9 total.9.a
  398.9 2.9 total.10.a
  405.5 37.6 %collective-permute-start.34 = (bf16[768,768]{1,0:T(8,128)(2,1)}, bf16[768,768]{1,0:T(8,128)(2,1)}, u32[]{:S(2)}, u32[]{:S(2)}) collective-permute-start(bf16[768,768]{1,0:T(8,128)(2,1)} %bitcast.18.a), channel_id=1, source_target_pairs={{0,8},{4,12},{24,16},{28,20},{1,9},{5,13},{25,17},{29,21},{2,10},{... | collective-permute-start | bytes 3538952 | tf_op jit(solution)/shard_map/ppermute | solution.py:904
  445.4 2.6 pair.11.a
  452.5 2.8 result.9
  457.0 4.3 last.1
  462.6 4.8 collective-permute-done.34.b
  467.4 2.7 concatenate.46
  470.7 4.2 all-to-all-start.7
  474.9 2.5 pair.12.a
  477.5 2.6 total.11.a
  481.3 2.8 result.10
  484.1 3.4 pad_maximum_fusion
  487.5 3.9 all-to-all-start.8
  494.7 4.4 collective-permute-start.31
  502.1 5.0 down_grads.1
  507.1 4.9 collective-permute-done.31.b
  515.6 2.6 total.12.a
  519.4 11.4 %collective-permute-done.38.b = bf16[768,768]{1,0:T(8,128)(2,1)} collective-permute-done((bf16[768,768]{1,0:T(8,128)(2,1)}, bf16[768,768]{1,0:T(8,128)(2,1)}, u32[]{:S(2)}, u32[]{:S(2)}) %collective-permute-start.38) | collective-permute-done | bytes 1179680 | tf_op jit(solution)/shard_map/ppermute | solution.py:904
  530.8 2.5 result.11.refs_0_
  539.9 19.8 %collective-permute-done.41.b = bf16[768,768]{1,0:T(8,128)(2,1)} collective-permute-done((bf16[768,768]{1,0:T(8,128)(2,1)}, bf16[768,768]{1,0:T(8,128)(2,1)}, u32[]{:S(2)}, u32[]{:S(2)}) %collective-permute-start.41) | collective-permute-done | bytes 1179680 | tf_op jit(solution)/shard_map/ppermute | solution.py:904
  564.5 8.4 %ff_grads.1 = (f32[384,4096]{1,0:T(8,128)}, f32[384,4096]{1,0:T(8,128)}) custom-call(s32[3]{0:T(128)} %pad_add_fusion.scal, bf16[4,384,1024]{2,1,0:T(8,128)(2,1)} %copy-done, bf16[2,384,1024]{2,1,0:T(8,128)(2,1)} %copy-done.19, bf16[2,384,1024]{2,1,0:T(8,128)(2,1)} %copy-done.18), custom_call_target="tpu_custom_call" | custom-call | flops 4000000 | tf_op jit(solution)/shard_map/ff_grads/pallas_call | solution.py:606
  583.5 7.5 %head_grads.1 = (f32[384,1536]{1,0:T(8,128)}, f32[384,1536]{1,0:T(8,128)}, f32[384,1536]{1,0:T(8,128)}, f32[384,1536]{1,0:T(8,128)}, f32[384,1536]{1,0:T(8,128)}) custom-call(s32[3]{0:T(128)} %pad_add_fusion.scal, bf16[768,768]{1,0:T(8,128)(2,1)} %result.11.refs_0_, bf16[768,768]{1,0:T(8,128)(2,1)} %result.12.refs_1_, bf16[400,768]{1,0:T(8,128)(2,1)} %result.13.refs_2_, ...), custom_call_target="tpu_custom_call" | custom-call | flops 3000000 | tf_op jit(solution)/shard_map/head_grads/pallas_call | solution.py:606
  (222 shorter events, 119.0 us)
Async XLA Ops:
  4.1 15.0 %copy-start.13 = (bf16[144,1536]{1,0:T(8,128)(2,1)}, bf16[144,1536]{1,0:T(8,128)(2,1)S(1)}, u32[]{:S(2)}) copy-start(bf16[144,1536]{1,0:T(8,128)(2,1)S(1)} %maximum_maximum_fusion.1.refs_0_) | copy-start | bytes 1327108
  4.1 15.0 %collective-permute-start.2 = (bf16[144,1536]{1,0:T(8,128)(2,1)S(1)}, bf16[144,1536]{1,0:T(8,128)(2,1)S(1)}, u32[]{:S(2)}, u32[]{:S(2)}) collective-permute-start(bf16[144,1536]{1,0:T(8,128)(2,1)S(1)} %maximum_maximum_fusion.1.refs_0_), channel_id=1, source_target_pairs={{0,3},{1,2},{2,1},{3,0},{4,7},{5,6},{6,5},{7,4},{8,11},{9,10},{10,... | collective-permute-start | bytes 1327112 | tf_op jit(solution)/shard_map/ppermute | solution.py:896
  13.2 40.6 %collective-permute-start.3 = (bf16[384,768]{1,0:T(8,128)(2,1)}, bf16[384,768]{1,0:T(8,128)(2,1)}, u32[]{:S(2)}, u32[]{:S(2)}) collective-permute-start(bf16[384,768]{1,0:T(8,128)(2,1)} %get-tuple-element.106), channel_id=1, source_target_pairs={{0,1},{1,0},{2,3},{3,2},{4,5},{5,4},{6,7},{7,6},{8,9},{9,8},{10,11... | collective-permute-start | bytes 1769480 | tf_op jit(solution)/shard_map/ppermute | solution.py:896
  13.7 40.0 %collective-permute-start.4 = (bf16[384,768]{1,0:T(8,128)(2,1)}, bf16[384,768]{1,0:T(8,128)(2,1)}, u32[]{:S(2)}, u32[]{:S(2)}) collective-permute-start(bf16[384,768]{1,0:T(8,128)(2,1)} %get-tuple-element.107), channel_id=1, source_target_pairs={{0,2},{1,3},{2,0},{3,1},{4,6},{5,7},{6,4},{7,5},{8,10},{9,11},{10,... | collective-permute-start | bytes 1769480 | tf_op jit(solution)/shard_map/ppermute | solution.py:896
  13.8 40.0 %collective-permute-start.5 = (bf16[384,768]{1,0:T(8,128)(2,1)}, bf16[384,768]{1,0:T(8,128)(2,1)}, u32[]{:S(2)}, u32[]{:S(2)}) collective-permute-start(bf16[384,768]{1,0:T(8,128)(2,1)} %get-tuple-element.108), channel_id=1, source_target_pairs={{0,3},{1,2},{2,1},{3,0},{4,7},{5,6},{6,5},{7,4},{8,11},{9,10},{10,... | collective-permute-start | bytes 1769480 | tf_op jit(solution)/shard_map/ppermute | solution.py:896
  16.7 36.3 %collective-permute-start.1 = (bf16[144,1536]{1,0:T(8,128)(2,1)S(1)}, bf16[144,1536]{1,0:T(8,128)(2,1)S(1)}, u32[]{:S(2)}, u32[]{:S(2)}) collective-permute-start(bf16[144,1536]{1,0:T(8,128)(2,1)S(1)} %maximum_maximum_fusion.1.refs_0_), channel_id=1, source_target_pairs={{0,2},{1,3},{2,0},{3,1},{4,6},{5,7},{6,4},{7,5},{8,10},{9,11},{10,... | collective-permute-start | bytes 1327112 | tf_op jit(solution)/shard_map/ppermute | solution.py:896
  19.1 6.8 %copy-start.31 = (bf16[144,1536]{1,0:T(8,128)(2,1)}, bf16[144,1536]{1,0:T(8,128)(2,1)S(1)}, u32[]{:S(2)}) copy-start(bf16[144,1536]{1,0:T(8,128)(2,1)S(1)} %collective-permute-done.2.refs_3_) | copy-start | bytes 1327108
  19.1 34.3 %collective-permute-start = (bf16[144,1536]{1,0:T(8,128)(2,1)S(1)}, bf16[144,1536]{1,0:T(8,128)(2,1)S(1)}, u32[]{:S(2)}, u32[]{:S(2)}) collective-permute-start(bf16[144,1536]{1,0:T(8,128)(2,1)S(1)} %maximum_maximum_fusion.1.refs_0_), channel_id=1, source_target_pairs={{0,1},{1,0},{2,3},{3,2},{4,5},{5,4},{6,7},{7,6},{8,9},{9,8},{10,11... | collective-permute-start | bytes 1327112 | tf_op jit(solution)/shard_map/ppermute | solution.py:896
  54.5 40.2 %all-to-all-start = ((bf16[4,384,1024]{2,1,0:T(8,128)(2,1)}), bf16[4,384,1024]{2,1,0:T(8,128)(2,1)S(1)}, u32[]{:S(2)}, u32[]{:S(2)}) async-start(bf16[4,384,1024]{2,1,0:T(8,128)(2,1)} %pick_hidden.1), calls=%async_computation | async-start | bytes 6291456 | tf_op jit(solution)/shard_map/all_to_all | solution.py:888
  58.4 2.3 collective-permute-start.6
  58.4 3.2 collective-permute-start.7
  59.0 3.5 collective-permute-start.8
  94.8 4.7 copy-start.1
  99.4 70.4 %collective-permute-start.12 = (bf16[4,384,1024]{2,1,0:T(8,128)(2,1)S(1)}, bf16[4,384,1024]{2,1,0:T(8,128)(2,1)}, u32[]{:S(2)}, u32[]{:S(2)}) collective-permute-start(bf16[4,384,1024]{2,1,0:T(8,128)(2,1)S(1)} %all-to-all-done.ours), channel_id=1, source_target_pairs={{0,4},{4,0},{8,12},{12,8},{16,20},{20,16},{24,28},{28,24},{1,5},{5... | collective-permute-start | bytes 9437192 | tf_op jit(solution)/shard_map/ppermute | solution.py:900
  99.4 5.1 copy-start.9
  99.5 42.2 %all-to-all-start.1 = ((bf16[4,128,1536]{2,1,0:T(8,128)(2,1)}), bf16[4,128,1536]{2,1,0:T(8,128)(2,1)}, u32[]{:S(2)}, u32[]{:S(2)}) async-start(bf16[4,128,1536]{2,1,0:T(8,128)(2,1)} %bitcast.54), calls=%async_computation.1 | async-start | bytes 3145728 | tf_op jit(solution)/shard_map/all_to_all | solution.py:888
  106.5 27.4 %collective-permute-start.11 = (bf16[128,1536]{1,0:T(8,128)(2,1)S(1)}, bf16[128,1536]{1,0:T(8,128)(2,1)S(1)}, u32[]{:S(2)}, u32[]{:S(2)}) collective-permute-start(bf16[128,1536]{1,0:T(8,128)(2,1)S(1)} %get-tuple-element.123.c0), channel_id=1, source_target_pairs={{0,3},{1,2},{2,1},{3,0},{4,7},{5,6},{6,5},{7,4},{8,11},{9,10},{10,... | collective-permute-start | bytes 1179656 | tf_op jit(solution)/shard_map/ppermute | solution.py:896
  109.3 31.6 %collective-permute-start.10 = (bf16[128,1536]{1,0:T(8,128)(2,1)S(1)}, bf16[128,1536]{1,0:T(8,128)(2,1)S(1)}, u32[]{:S(2)}, u32[]{:S(2)}) collective-permute-start(bf16[128,1536]{1,0:T(8,128)(2,1)S(1)} %get-tuple-element.123.c0), channel_id=1, source_target_pairs={{0,2},{1,3},{2,0},{3,1},{4,6},{5,7},{6,4},{7,5},{8,10},{9,11},{10,... | collective-permute-start | bytes 1179656 | tf_op jit(solution)/shard_map/ppermute | solution.py:896
  109.9 31.8 %collective-permute-start.9 = (bf16[128,1536]{1,0:T(8,128)(2,1)S(1)}, bf16[128,1536]{1,0:T(8,128)(2,1)}, u32[]{:S(2)}, u32[]{:S(2)}) collective-permute-start(bf16[128,1536]{1,0:T(8,128)(2,1)S(1)} %get-tuple-element.123.c0), channel_id=1, source_target_pairs={{0,1},{1,0},{2,3},{3,2},{4,5},{5,4},{6,7},{7,6},{8,9},{9,8},{10,11... | collective-permute-start | bytes 1179656 | tf_op jit(solution)/shard_map/ppermute | solution.py:896
  133.9 35.9 %copy-start.34 = (bf16[128,1536]{1,0:T(8,128)(2,1)}, bf16[128,1536]{1,0:T(8,128)(2,1)S(1)}, u32[]{:S(2)}) copy-start(bf16[128,1536]{1,0:T(8,128)(2,1)S(1)} %collective-permute-done.11.c3) | copy-start | bytes 1179652
  190.1 15.0 %collective-permute-start.14 = (bf16[1536,1024]{1,0:T(8,128)(2,1)}, bf16[1536,1024]{1,0:T(8,128)(2,1)S(1)}, u32[]{:S(2)}, u32[]{:S(2)}) collective-permute-start(bf16[1536,1024]{1,0:T(8,128)(2,1)} %convolution_convert_fusion), channel_id=1, source_target_pairs={{0,4},{4,0},{8,12},{12,8},{16,20},{20,16},{24,28},{28,24},{1,5},{5... | collective-permute-start | bytes 9437192 | tf_op jit(solution)/shard_map/ppermute | solution.py:900
  190.1 9.6 %collective-permute-start.13 = (bf16[512,1536]{1,0:T(8,128)(2,1)}, bf16[512,1536]{1,0:T(8,128)(2,1)}, u32[]{:S(2)}, u32[]{:S(2)}) collective-permute-start(bf16[512,1536]{1,0:T(8,128)(2,1)} %convolution_convert_fusion.1), channel_id=1, source_target_pairs={{0,4},{4,0},{8,12},{12,8},{16,20},{20,16},{24,28},{28,24},{1,5},{5... | collective-permute-start | bytes 4718600 | tf_op jit(solution)/shard_map/ppermute | solution.py:900
  202.2 15.6 %copy-start.23 = (bf16[256,1536]{1,0:T(8,128)(2,1)}, bf16[256,1536]{1,0:T(8,128)(2,1)S(1)}, u32[]{:S(2)}) copy-start(bf16[256,1536]{1,0:T(8,128)(2,1)S(1)} %fusion.a) | copy-start | bytes 2359300
  214.3 23.2 %all-to-all-start.3 = ((bf16[4,128,1536]{2,1,0:T(8,128)(2,1)}), bf16[4,128,1536]{2,1,0:T(8,128)(2,1)S(1)}, u32[]{:S(2)}, u32[]{:S(2)}) async-start(bf16[4,128,1536]{2,1,0:T(8,128)(2,1)} %bitcast.6), calls=%async_computation.3 | async-start | bytes 3145728 | tf_op jit(solution)/shard_map/all_to_all | solution.py:888
  217.8 24.9 %collective-permute-start.15 = (bf16[256,1536]{1,0:T(8,128)(2,1)S(1)}, bf16[256,1536]{1,0:T(8,128)(2,1)S(1)}, u32[]{:S(2)}, u32[]{:S(2)}) collective-permute-start(bf16[256,1536]{1,0:T(8,128)(2,1)S(1)} %fusion.a), channel_id=1, source_target_pairs={{0,8},{4,12},{24,16},{28,20},{1,9},{5,13},{25,17},{29,21},{2,10},{... | collective-permute-start | bytes 2359304 | tf_op jit(solution)/shard_map/ppermute | solution.py:904
  246.1 11.6 %copy-start.6 = (bf16[768,1024]{1,0:T(8,128)(2,1)S(1)}, bf16[768,1024]{1,0:T(8,128)(2,1)}, u32[]{:S(2)}) copy-start(bf16[768,1024]{1,0:T(8,128)(2,1)} %ff1.1.a) | copy-start | bytes 4718596
  246.2 23.5 %all-to-all-start.4 = ((bf16[4,128,1536]{2,1,0:T(8,128)(2,1)}), bf16[4,128,1536]{2,1,0:T(8,128)(2,1)}, u32[]{:S(2)}, u32[]{:S(2)}) async-start(bf16[4,128,1536]{2,1,0:T(8,128)(2,1)} %get-tuple-element.142), calls=%async_computation.4 | async-start | bytes 3145728 | tf_op jit(solution)/shard_map/all_to_all | solution.py:888
  250.8 57.9 %collective-permute-start.20 = (bf16[768,1024]{1,0:T(8,128)(2,1)S(1)}, bf16[768,1024]{1,0:T(8,128)(2,1)}, u32[]{:S(2)}, u32[]{:S(2)}) collective-permute-start(bf16[768,1024]{1,0:T(8,128)(2,1)S(1)} %copy-done.7), channel_id=1, source_target_pairs={{0,8},{4,12},{24,16},{28,20},{1,9},{5,13},{25,17},{29,21},{2,10},{... | collective-permute-start | bytes 4718600 | tf_op jit(solution)/shard_map/ppermute | solution.py:904
  255.6 50.6 %collective-permute-start.17 = (bf16[256,1536]{1,0:T(8,128)(2,1)}, bf16[256,1536]{1,0:T(8,128)(2,1)}, u32[]{:S(2)}, u32[]{:S(2)}) collective-permute-start(bf16[256,1536]{1,0:T(8,128)(2,1)} %fusion.1.a), channel_id=1, source_target_pairs={{0,8},{4,12},{24,16},{28,20},{1,9},{5,13},{25,17},{29,21},{2,10},{... | collective-permute-start | bytes 2359304 | tf_op jit(solution)/shard_map/ppermute | solution.py:904
  257.8 80.2 %collective-permute-start.16 = (bf16[768,1024]{1,0:T(8,128)(2,1)S(1)}, bf16[768,1024]{1,0:T(8,128)(2,1)}, u32[]{:S(2)}, u32[]{:S(2)}) collective-permute-start(bf16[768,1024]{1,0:T(8,128)(2,1)S(1)} %copy-done.6), channel_id=1, source_target_pairs={{0,8},{4,12},{24,16},{28,20},{1,9},{5,13},{25,17},{29,21},{2,10},{... | collective-permute-start | bytes 4718600 | tf_op jit(solution)/shard_map/ppermute | solution.py:904
  260.2 37.0 %collective-permute-start.18 = (bf16[256,1536]{1,0:T(8,128)(2,1)}, bf16[256,1536]{1,0:T(8,128)(2,1)}, u32[]{:S(2)}, u32[]{:S(2)}) collective-permute-start(bf16[256,1536]{1,0:T(8,128)(2,1)} %pair.7.a), channel_id=1, source_target_pairs={{8,16},{12,20},{16,8},{20,12},{9,17},{13,21},{17,9},{21,13},{10,18... | collective-permute-start | bytes 2359304 | tf_op jit(solution)/shard_map/ppermute | solution.py:904
  314.8 26.1 %collective-permute-start.21 = (bf16[768,768]{1,0:T(8,128)(2,1)}, bf16[768,768]{1,0:T(8,128)(2,1)}, u32[]{:S(2)}, u32[]{:S(2)}) collective-permute-start(bf16[768,768]{1,0:T(8,128)(2,1)} %convolution_convert_fusion.3), channel_id=1, source_target_pairs={{0,4},{4,0},{8,12},{12,8},{16,20},{20,16},{24,28},{28,24},{1,5},{5... | collective-permute-start | bytes 3538952 | tf_op jit(solution)/shard_map/ppermute | solution.py:900
  316.7 26.4 %collective-permute-start.22 = (bf16[768,768]{1,0:T(8,128)(2,1)}, bf16[768,768]{1,0:T(8,128)(2,1)}, u32[]{:S(2)}, u32[]{:S(2)}) collective-permute-start(bf16[768,768]{1,0:T(8,128)(2,1)} %convolution_convert_fusion.2), channel_id=1, source_target_pairs={{0,4},{4,0},{8,12},{12,8},{16,20},{20,16},{24,28},{28,24},{1,5},{5... | collective-permute-start | bytes 3538952 | tf_op jit(solution)/shard_map/ppermute | solution.py:900
  317.2 3.4 collective-permute-start.19
  324.0 17.0 %copy-start.17 = (bf16[512,1536]{1,0:T(8,128)(2,1)S(1)}, bf16[512,1536]{1,0:T(8,128)(2,1)}, u32[]{:S(2)}) copy-start(bf16[512,1536]{1,0:T(8,128)(2,1)} %get-tuple-element.148) | copy-start | bytes 4718596
  346.7 33.0 %all-to-all-start.5 = ((bf16[4,384,768]{2,1,0:T(8,128)(2,1)}), bf16[4,384,768]{2,1,0:T(8,128)(2,1)S(1)}, u32[]{:S(2)}, u32[]{:S(2)}) async-start(bf16[4,384,768]{2,1,0:T(8,128)(2,1)} %bitcast.53), calls=%async_computation.5 | async-start | bytes 4718592 | tf_op jit(solution)/shard_map/all_to_all | solution.py:888
  350.7 24.9 %collective-permute-start.24 = (bf16[256,1536]{1,0:T(8,128)(2,1)S(1)}, bf16[256,1536]{1,0:T(8,128)(2,1)}, u32[]{:S(2)}, u32[]{:S(2)}) collective-permute-start(bf16[256,1536]{1,0:T(8,128)(2,1)S(1)} %copy-done.11), channel_id=1, source_target_pairs={{8,0},{12,4},{16,24},{20,28},{9,1},{13,5},{17,25},{21,29},{10,2},{... | collective-permute-start | bytes 2359304 | tf_op jit(solution)/shard_map/ppermute | solution.py:904
  352.0 25.9 %collective-permute-start.23 = (bf16[384,768]{1,0:T(8,128)(2,1)}, bf16[384,768]{1,0:T(8,128)(2,1)}, u32[]{:S(2)}, u32[]{:S(2)}) collective-permute-start(bf16[384,768]{1,0:T(8,128)(2,1)} %convolution_convert_fusion.4), channel_id=1, source_target_pairs={{0,4},{4,0},{8,12},{12,8},{16,20},{20,16},{24,28},{28,24},{1,5},{5... | collective-permute-start | bytes 1769480 | tf_op jit(solution)/shard_map/ppermute | solution.py:900
  352.1 42.6 %collective-permute-start.25 = (bf16[768,1024]{1,0:T(8,128)(2,1)}, bf16[768,1024]{1,0:T(8,128)(2,1)}, u32[]{:S(2)}, u32[]{:S(2)}) collective-permute-start(bf16[768,1024]{1,0:T(8,128)(2,1)} %pair.9.a), channel_id=1, source_target_pairs={{8,16},{12,20},{16,8},{20,12},{9,17},{13,21},{17,9},{21,13},{10,18... | collective-permute-start | bytes 4718600 | tf_op jit(solution)/shard_map/ppermute | solution.py:904
  353.9 45.0 %collective-permute-start.29 = (bf16[768,1024]{1,0:T(8,128)(2,1)}, bf16[768,1024]{1,0:T(8,128)(2,1)}, u32[]{:S(2)}, u32[]{:S(2)}) collective-permute-start(bf16[768,1024]{1,0:T(8,128)(2,1)} %pair.10.a), channel_id=1, source_target_pairs={{8,16},{12,20},{16,8},{20,12},{9,17},{13,21},{17,9},{21,13},{10,18... | collective-permute-start | bytes 4718600 | tf_op jit(solution)/shard_map/ppermute | solution.py:904
  381.8 73.5 %all-to-all-start.6 = ((bf16[4,256,1536]{2,1,0:T(8,128)(2,1)}), bf16[4,256,1536]{2,1,0:T(8,128)(2,1)S(1)}, u32[]{:S(2)}, u32[]{:S(2)}) async-start(bf16[4,256,1536]{2,1,0:T(8,128)(2,1)} %get-tuple-element.164), calls=%async_computation.6 | async-start | bytes 6291456 | tf_op jit(solution)/shard_map/all_to_all | solution.py:888
  385.8 59.6 %collective-permute-start.27 = (bf16[768,768]{1,0:T(8,128)(2,1)}, bf16[768,768]{1,0:T(8,128)(2,1)}, u32[]{:S(2)}, u32[]{:S(2)}) collective-permute-start(bf16[768,768]{1,0:T(8,128)(2,1)} %pad_maximum_fusion.2.a), channel_id=1, source_target_pairs={{0,8},{4,12},{24,16},{28,20},{1,9},{5,13},{25,17},{29,21},{2,10},{... | collective-permute-start | bytes 3538952 | tf_op jit(solution)/shard_map/ppermute | solution.py:904
  393.4 49.7 %collective-permute-start.28 = (bf16[256,1536]{1,0:T(8,128)(2,1)}, bf16[256,1536]{1,0:T(8,128)(2,1)}, u32[]{:S(2)}, u32[]{:S(2)}) collective-permute-start(bf16[256,1536]{1,0:T(8,128)(2,1)} %total.8.a), channel_id=1, source_target_pairs={{8,0},{12,4},{16,24},{20,28},{9,1},{13,5},{17,25},{21,29},{10,2},{... | collective-permute-start | bytes 2359304 | tf_op jit(solution)/shard_map/ppermute | solution.py:904
  397.6 54.9 %collective-permute-start.26 = (bf16[768,1024]{1,0:T(8,128)(2,1)}, bf16[768,1024]{1,0:T(8,128)(2,1)}, u32[]{:S(2)}, u32[]{:S(2)}) collective-permute-start(bf16[768,1024]{1,0:T(8,128)(2,1)} %total.9.a), channel_id=1, source_target_pairs={{8,0},{12,4},{16,24},{20,28},{9,1},{13,5},{17,25},{21,29},{10,2},{... | collective-permute-start | bytes 4718600 | tf_op jit(solution)/shard_map/ppermute | solution.py:904
  401.8 79.5 %collective-permute-start.32 = (bf16[768,1024]{1,0:T(8,128)(2,1)}, bf16[768,1024]{1,0:T(8,128)(2,1)}, u32[]{:S(2)}, u32[]{:S(2)}) collective-permute-start(bf16[768,1024]{1,0:T(8,128)(2,1)} %total.10.a), channel_id=1, source_target_pairs={{8,0},{12,4},{16,24},{20,28},{9,1},{13,5},{17,25},{21,29},{10,2},{... | collective-permute-start | bytes 4718600 | tf_op jit(solution)/shard_map/ppermute | solution.py:904
  405.5 62.0 %collective-permute-start.34 = (bf16[768,768]{1,0:T(8,128)(2,1)}, bf16[768,768]{1,0:T(8,128)(2,1)}, u32[]{:S(2)}, u32[]{:S(2)}) collective-permute-start(bf16[768,768]{1,0:T(8,128)(2,1)} %bitcast.18.a), channel_id=1, source_target_pairs={{0,8},{4,12},{24,16},{28,20},{1,9},{5,13},{25,17},{29,21},{2,10},{... | collective-permute-start | bytes 3538952 | tf_op jit(solution)/shard_map/ppermute | solution.py:904
  445.4 5.3 copy-start.37
  448.0 29.5 %collective-permute-start.33 = (bf16[768,768]{1,0:T(8,128)(2,1)}, bf16[768,768]{1,0:T(8,128)(2,1)}, u32[]{:S(2)}, u32[]{:S(2)}) collective-permute-start(bf16[768,768]{1,0:T(8,128)(2,1)} %pair.11.a), channel_id=1, source_target_pairs={{8,16},{12,20},{16,8},{20,12},{9,17},{13,21},{17,9},{21,13},{10,18... | collective-permute-start | bytes 3538952 | tf_op jit(solution)/shard_map/ppermute | solution.py:904
  470.7 16.7 %all-to-all-start.7 = ((f32[4,6,384]{2,1,0:T(8,128)}), f32[4,6,384]{2,1,0:T(8,128)S(1)}, u32[]{:S(2)}, u32[]{:S(2)}) async-start(f32[4,6,384]{2,1,0:T(8,128)} %pad_maximum_fusion.4), calls=%async_computation.7 | async-start | bytes 98304 | tf_op jit(solution)/shard_map/all_to_all | solution.py:888
  487.5 47.9 %all-to-all-start.8 = ((bf16[4,384,1024]{2,1,0:T(8,128)(2,1)}), bf16[4,384,1024]{2,1,0:T(8,128)(2,1)S(1)}, u32[]{:S(2)}, u32[]{:S(2)}) async-start(bf16[4,384,1024]{2,1,0:T(8,128)(2,1)} %bitcast.52), calls=%async_computation.8 | async-start | bytes 6291456 | tf_op jit(solution)/shard_map/all_to_all | solution.py:888
  491.5 1.2 collective-permute-start.30
  491.5 10.6 %collective-permute-start.35 = (bf16[256,1536]{1,0:T(8,128)(2,1)}, bf16[256,1536]{1,0:T(8,128)(2,1)}, u32[]{:S(2)}, u32[]{:S(2)}) collective-permute-start(bf16[256,1536]{1,0:T(8,128)(2,1)} %result.7.a0), channel_id=1, source_target_pairs={{0,4},{4,0},{8,12},{12,8},{16,20},{20,16},{24,28},{28,24},{1,5},{5... | collective-permute-start | bytes 2359304 | tf_op jit(solution)/shard_map/ppermute | solution.py:900
  492.0 10.1 %collective-permute-start.36 = (bf16[256,1536]{1,0:T(8,128)(2,1)}, bf16[256,1536]{1,0:T(8,128)(2,1)}, u32[]{:S(2)}, u32[]{:S(2)}) collective-permute-start(bf16[256,1536]{1,0:T(8,128)(2,1)} %result.8.a1), channel_id=1, source_target_pairs={{0,4},{4,0},{8,12},{12,8},{16,20},{20,16},{24,28},{28,24},{1,5},{5... | collective-permute-start | bytes 2359304 | tf_op jit(solution)/shard_map/ppermute | solution.py:900
  494.7 17.4 %collective-permute-start.31 = (bf16[400,768]{1,0:T(8,128)(2,1)}, bf16[400,768]{1,0:T(8,128)(2,1)}, u32[]{:S(2)}, u32[]{:S(2)}) collective-permute-start(bf16[400,768]{1,0:T(8,128)(2,1)} %maximum_maximum_fusion.a), channel_id=1, source_target_pairs={{0,8},{4,12},{24,16},{28,20},{1,9},{5,13},{25,17},{29,21},{2,10},{... | collective-permute-start | bytes 1843208 | tf_op jit(solution)/shard_map/ppermute | solution.py:904
  499.2 16.4 %collective-permute-start.39 = (bf16[768,768]{1,0:T(8,128)(2,1)}, bf16[768,768]{1,0:T(8,128)(2,1)}, u32[]{:S(2)}, u32[]{:S(2)}) collective-permute-start(bf16[768,768]{1,0:T(8,128)(2,1)} %pair.12.a), channel_id=1, source_target_pairs={{8,16},{12,20},{16,8},{20,12},{9,17},{13,21},{17,9},{21,13},{10,18... | collective-permute-start | bytes 3538952 | tf_op jit(solution)/shard_map/ppermute | solution.py:904
  500.8 30.0 %collective-permute-start.38 = (bf16[768,768]{1,0:T(8,128)(2,1)}, bf16[768,768]{1,0:T(8,128)(2,1)}, u32[]{:S(2)}, u32[]{:S(2)}) collective-permute-start(bf16[768,768]{1,0:T(8,128)(2,1)} %total.11.a), channel_id=1, source_target_pairs={{8,0},{12,4},{16,24},{20,28},{9,1},{13,5},{17,25},{21,29},{10,2},{... | collective-permute-start | bytes 3538952 | tf_op jit(solution)/shard_map/ppermute | solution.py:904
  514.1 19.2 %collective-permute-start.37 = (bf16[400,768]{1,0:T(8,128)(2,1)}, bf16[400,768]{1,0:T(8,128)(2,1)}, u32[]{:S(2)}, u32[]{:S(2)}) collective-permute-start(bf16[400,768]{1,0:T(8,128)(2,1)} %pair.13.a), channel_id=1, source_target_pairs={{8,16},{12,20},{16,8},{20,12},{9,17},{13,21},{17,9},{21,13},{10,18... | collective-permute-start | bytes 1843208 | tf_op jit(solution)/shard_map/ppermute | solution.py:904
  518.1 41.6 %collective-permute-start.41 = (bf16[768,768]{1,0:T(8,128)(2,1)}, bf16[768,768]{1,0:T(8,128)(2,1)}, u32[]{:S(2)}, u32[]{:S(2)}) collective-permute-start(bf16[768,768]{1,0:T(8,128)(2,1)} %total.12.a), channel_id=1, source_target_pairs={{8,0},{12,4},{16,24},{20,28},{9,1},{13,5},{17,25},{21,29},{10,2},{... | collective-permute-start | bytes 3538952 | tf_op jit(solution)/shard_map/ppermute | solution.py:904
  538.0 24.2 %collective-permute-start.43 = (bf16[2,384,1024]{2,1,0:T(8,128)(2,1)}, bf16[2,384,1024]{2,1,0:T(8,128)(2,1)S(1)}, u32[]{:S(2)}, u32[]{:S(2)}) collective-permute-start(bf16[2,384,1024]{2,1,0:T(8,128)(2,1)} %get-tuple-element.200), channel_id=1, source_target_pairs={{0,4},{4,0},{8,12},{12,8},{16,20},{20,16},{24,28},{28,24},{1,5},{5... | collective-permute-start | bytes 4718600 | tf_op jit(solution)/shard_map/ppermute | solution.py:900
  538.0 24.2 %collective-permute-start.42 = (bf16[2,384,1024]{2,1,0:T(8,128)(2,1)}, bf16[2,384,1024]{2,1,0:T(8,128)(2,1)S(1)}, u32[]{:S(2)}, u32[]{:S(2)}) collective-permute-start(bf16[2,384,1024]{2,1,0:T(8,128)(2,1)} %get-tuple-element.201), channel_id=1, source_target_pairs={{0,4},{4,0},{8,12},{12,8},{16,20},{20,16},{24,28},{28,24},{1,5},{5... | collective-permute-start | bytes 4718600 | tf_op jit(solution)/shard_map/ppermute | solution.py:900
  538.5 34.4 %collective-permute-start.40 = (bf16[400,768]{1,0:T(8,128)(2,1)}, bf16[400,768]{1,0:T(8,128)(2,1)S(1)}, u32[]{:S(2)}, u32[]{:S(2)}) collective-permute-start(bf16[400,768]{1,0:T(8,128)(2,1)} %total.13.a), channel_id=1, source_target_pairs={{8,0},{12,4},{16,24},{20,28},{9,1},{13,5},{17,25},{21,29},{10,2},{... | collective-permute-start | bytes 1843208 | tf_op jit(solution)/shard_map/ppermute | solution.py:904
  539.8 42.9 %collective-permute-start.44 = (bf16[768,768]{1,0:T(8,128)(2,1)}, bf16[768,768]{1,0:T(8,128)(2,1)}, u32[]{:S(2)}, u32[]{:S(2)}) collective-permute-start(bf16[768,768]{1,0:T(8,128)(2,1)} %result.11.refs_0_), channel_id=1, source_target_pairs={{0,4},{4,0},{8,12},{12,8},{16,20},{20,16},{24,28},{28,24},{1,5},{5... | collective-permute-start | bytes 3538952 | tf_op jit(solution)/shard_map/ppermute | solution.py:900
  562.2 20.5 %collective-permute-start.45 = (bf16[768,768]{1,0:T(8,128)(2,1)}, bf16[768,768]{1,0:T(8,128)(2,1)}, u32[]{:S(2)}, u32[]{:S(2)}) collective-permute-start(bf16[768,768]{1,0:T(8,128)(2,1)} %result.12.refs_1_), channel_id=1, source_target_pairs={{0,4},{4,0},{8,12},{12,8},{16,20},{20,16},{24,28},{28,24},{1,5},{5... | collective-permute-start | bytes 3538952 | tf_op jit(solution)/shard_map/ppermute | solution.py:900
  576.9 5.8 collective-permute-start.46
  (33 other events, 81.7 us)

commit v4 on v3

--- a/solution.py
+++ b/solution.py
@@ -716,11 +716,26 @@
         dgu[:, half:] = (d_hid * act).astype(bf16)
 
 
-def feed_back_kernel(scal, dgu_a, dgu_b, ours, theirs, out):
-    part = ours.shape[1]
-    for k in range(4):
-        d_n = dot_nt(dgu_a[...], ours[k]) + dot_nt(dgu_b[...], theirs[k])
-        out[:, k * part : (k + 1) * part] = d_n.astype(bf16)
+def feed_back_kernel(dgu_a, dgu_b, ours, theirs, out):
+    d_n = dot_nt(dgu_a[...], ours[0]) + dot_nt(dgu_b[...], theirs[0])
+    out[...] = d_n.astype(bf16)
+
+
+def feed_back(dgu_a, dgu_b, ours, theirs):
+    count, part, cols = ours.shape
+    rows = dgu_a.shape[0]
+    held = pl.BlockSpec((rows, cols), lambda k: (0, 0))
+    block = pl.BlockSpec((1, part, cols), lambda k: (k, 0, 0))
+    return pl.pallas_call(
+        feed_back_kernel,
+        grid=(count,),
+        in_specs=[held, held, block, block],
+        out_specs=pl.BlockSpec((rows, part), lambda k: (0, k)),
+        out_shape=struct((rows, count * part), bf16),
+        compiler_params=grant(),
+        cost_estimate=cost(3),
+        name="feed_back",
+    )(dgu_a, dgu_b, ours, theirs)
 
 
 def norm_two_kernel(scal, stream_ref, cot, gain, come, d_stream_ref, d_attn_ref, gain_ref):
@@ -809,15 +824,35 @@
             outs[3][:, at] = high[:, part:]
 
 
-def ff_grads_kernel(scal, ours, theirs_low, theirs_high, gate, up):
+def ff_grads_kernel(scal, ours, low, high, gate, up):
     first = scal[1] == 0
     half = ours.shape[2] // 2
-    for k in range(4):
-        a, b = ours[k], (theirs_low, theirs_high)[k // 2][k % 2]
-        for i, v in enumerate((jnp.where(first, a, b), jnp.where(first, b, a))):
-            at = slice((2 * k + i) * half, (2 * k + i + 1) * half)
-            gate[:, at] = v[:, :half].astype(f32)
-            up[:, at] = v[:, half:].astype(f32)
+    a, b = ours[0], jnp.where(pl.program_id(0) < 2, low[0], high[0])
+    for i, v in enumerate((jnp.where(first, a, b), jnp.where(first, b, a))):
+        at = slice(i * half, (i + 1) * half)
+        gate[:, at] = v[:, :half].astype(f32)
+        up[:, at] = v[:, half:].astype(f32)
+
+
+def ff_grads(scal, ours, low, high):
+    count, part, cols = ours.shape
+    shape = (1, part, cols)
+    out = pl.BlockSpec((part, cols), lambda k: (0, k))
+    return pl.pallas_call(
+        ff_grads_kernel,
+        grid=(count,),
+        in_specs=[
+            pl.BlockSpec(memory_space=pltpu.SMEM),
+            pl.BlockSpec(shape, lambda k: (k, 0, 0)),
+            pl.BlockSpec(shape, lambda k: (jnp.minimum(k, 1), 0, 0)),
+            pl.BlockSpec(shape, lambda k: (jnp.maximum(k - 2, 0), 0, 0)),
+        ],
+        out_specs=[out, out],
+        out_shape=[struct((part, count * cols), f32)] * 2,
+        compiler_params=grant(),
+        cost_estimate=cost(4),
+        name="ff_grads",
+    )(scal, ours, low, high)
 
 
 def product_kernel(a, b, c, out):
@@ -1091,17 +1126,7 @@
     down_come = core_swap(down_theirs)
     ff_theirs_grad = product_low(n_two, after(dgu_b, down_theirs))
     ff_come = core_swap(ff_theirs_grad)
-    (d_n_part,) = whole(
-        feed_back_kernel,
-        "feed_back",
-        3,
-        [wide],
-        scal,
-        after(dgu_a, ff_theirs_grad),
-        dgu_b,
-        ff_ours,
-        ff_theirs,
-    )
+    d_n_part = feed_back(after(dgu_a, ff_theirs_grad), dgu_b, ff_ours, ff_theirs)
     tick = d_n_part
     for i in range(2):
         at = slice(i * (ff_core // 2), (i + 1) * (ff_core // 2))
@@ -1243,10 +1268,7 @@
     ff_sum = after(ff_sum, tick)
     ff_other = [core_swap(ff_sum[:2]), core_swap(ff_sum[2:])]
     tick = zsum.play([("result", "second")], ff_sum)
-    ff_grad = struct((part, SHARDS * ff_part), f32)
-    grad_gate, grad_up = whole(
-        ff_grads_kernel, "ff_grads", 4, [ff_grad] * 2, scal, after(ff_sum, tick), *ff_other
-    )
+    grad_gate, grad_up = ff_grads(scal, after(ff_sum, tick), *ff_other)
     tick = zsum.play([("result", "third")], grad_gate)
     last = zsum.out["third"]
     pack = last[part:, :part].astype(f32) + last[part:, part:].astype(f32)

time: 606 us -> 604 us (level)
    pallas_call x13 -> x11, Pallas kernels: 92 us -> 74.5 us  [whole(): pl.pallas_call(kernel, in_specs=[pl.BlockSpec(memory_space=pltpu.SMEM)] +...]
    pallas_call x0 -> x2, Pallas kernels: none -> 16.1 us  [the longest x1 8.19 us: feed_back(): pl.pallas_call(feed_back_kernel, grid=(count,), in_specs=[held, held, blo...]
where the time goes in v4:
time: 604 us; the launch traced here: 593 us
  Pallas kernels  191 us (32%)
  waiting for transfers between devices  160 us (26%)
  starting transfers between devices  133 us (22%)
  matrix products  31.4 us (5%)
  local copies, waits for them, and re-layouts  27.7 us (5%)
  blocking collectives  24.4 us (4%)
  other arithmetic  17.8 us (3%)
  between operations  8.46 us (1%)
    ppermute x21, starting transfers between devices, chip_send(): lax.ppermute(value, 'rep', [(2 * a + c, 2 * b + c) for a, b in pairs for...  83.2 us
    pallas_call x11, Pallas kernels, whole(): pl.pallas_call(kernel, in_specs=[pl.BlockSpec(memory_space=pltpu.SMEM)] +...  74.5 us
    ppermute x21, waiting for transfers between devices, chip_send(): lax.ppermute(value, 'rep', [(2 * a + c, 2 * b + c) for a, b in pairs for...  69.2 us
    ppermute x9, waiting for transfers between devices, shard_swap(): return lax.ppermute(value, 'shard', [(i, i ^ k) for i in range(SHARDS)])  60.4 us
    pallas_call x21, Pallas kernels, blocked(): pl.pallas_call(kernel, grid=(rows // step,), in_specs=[pl.BlockSpec(memor...  53.4 us
    all_to_all x8, starting transfers between devices, shard_exchange(): return lax.all_to_all(blocks, 'shard', 0, 0)  33 us
    dot_general x10, matrix products, dot_tn(): lax.dot_general(a, b, (((0,), (0,)), ((), ())), preferred_element_type=f32)  26.2 us
    all_to_all x8, waiting for transfers between devices, shard_exchange(): return lax.all_to_all(blocks, 'shard', 0, 0)  26 us
  transfers between devices with their start and end apart: 55, of which 20 were waited for; matrix products, arithmetic and copies ran while one was open for 8% of the time, Pallas kernels for 26%

profile of v4, /device:TPU:0, one launch (start us, length us, event | category | flops | bytes accessed | tf_op | source)
XLA Modules:
  0.0 593.4 jit_solution(2842356281173392910)
XLA Ops:
  4.1 4.0 collective-permute-start.2
  9.4 3.8 pick_heads.1
  13.8 2.9 collective-permute-start.5
  21.1 4.8 pick_hidden.1
  25.9 27.2 %collective-permute-done.1.refs_2_ = bf16[144,1536]{1,0:T(8,128)(2,1)S(1)} collective-permute-done((bf16[144,1536]{1,0:T(8,128)(2,1)S(1)}, bf16[144,1536]{1,0:T(8,128)(2,1)S(1)}, u32[]{:S(2)}, u32[]{:S(2)}) %collective-permute-start.1) | collective-permute-done | bytes 442400 | tf_op jit(solution)/shard_map/ppermute | solution.py:931
  54.5 3.9 all-to-all-start
  62.5 10.8 %project.1 = (bf16[4,128,1536]{2,1,0:T(8,128)(2,1)}, bf16[512,1536]{1,0:T(8,128)(2,1)}, bf16[512,384]{1,0:T(8,128)(2,1)}, bf16[512,384]{1,0:T(8,128)(2,1)}, bf16...) custom-call(s32[3]{0:T(128)} %pad_add_fusion.scal, ...), custom_call_target="tpu_custom_call" | custom-call | flops 4000000 | tf_op jit(solution)/shard_map/project/pallas_call | solution.py:606
  73.3 19.1 %attend_forward.1 = (bf16[512,384]{1,0:T(8,128)(2,1)}, bf16[3,2,512,512]{3,2,1,0:T(8,128)(2,1)}, bf16[3,2,512,512]{3,2,1,0:T(8,128)(2,1)}, f32[3,512,512]{2,1,0:T(8,128)}) custom-call(s32[3]{0:T(128)} %pad_add_fusion.scal, bf16[512,384]{1,0:T(8,128)(2,1)} %get-tuple-element.111.q_ref.refs_0_, bf16[512,384]{1,0:T(8,128)(2,1)} %get-tuple-element.112.k_ref.refs_1_, ...), custom_call_target="tpu_custom_call" | custom-call | flops 8000000 | tf_op jit(solution)/shard_map/attend_forward/pallas_call | solution.py:571
  94.8 4.7 out_project.1
  99.5 5.0 all-to-all-start.1
  106.9 2.9 collective-permute-start.11
  110.4 23.9 %collective-permute-done.11.c3 = bf16[128,1536]{1,0:T(8,128)(2,1)S(1)} collective-permute-done((bf16[128,1536]{1,0:T(8,128)(2,1)S(1)}, bf16[128,1536]{1,0:T(8,128)(2,1)S(1)}, u32[]{:S(2)}, u32[]{:S(2)}) %collective-permute-start.11) | collective-permute-done | bytes 393248 | tf_op jit(solution)/shard_map/ppermute | solution.py:931
  134.3 7.1 %collective-permute-done.10.c2 = bf16[128,1536]{1,0:T(8,128)(2,1)S(1)} collective-permute-done((bf16[128,1536]{1,0:T(8,128)(2,1)S(1)}, bf16[128,1536]{1,0:T(8,128)(2,1)S(1)}, u32[]{:S(2)}, u32[]{:S(2)}) %collective-permute-start.10) | collective-permute-done | bytes 393248 | tf_op jit(solution)/shard_map/ppermute | solution.py:931
  142.1 3.3 residual_norm.1
  145.4 24.4 %all_to_all.45 = bf16[4,128,1536]{2,1,0:T(8,128)(2,1)} all-to-all(bf16[4,128,1536]{2,1,0:T(8,128)(2,1)} %get-tuple-element.126), channel_id=1, replica_groups=mesh['rep'=8,'shard'=4] {'shard'}, dimensions={0} | all-to-all | bytes 3145728 | tf_op jit(solution)/shard_map/all_to_all | solution.py:923
  169.8 12.8 %feed.1 = (bf16[512,512]{1,0:T(8,128)(2,1)}, bf16[512,512]{1,0:T(8,128)(2,1)}, bf16[512,1024]{1,0:T(8,128)(2,1)}, bf16[512,1024]{1,0:T(8,128)(2,1)}, bf16[512,1536]{1,0:T(8,128)(2,1)}) custom-call(s32[3]{0:T(128)} %pad_add_fusion.scal, bf16[512,1536]{1,0:T(8,128)(2,1)} %bitcast.48, bf16[128,1536]{1,0:T(8,128)(2,1)} %copy-done.14, ...), custom_call_target="tpu_custom_call" | custom-call | flops 6000000 | tf_op jit(solution)/shard_map/feed/pallas_call | solution.py:606
  182.7 3.9 convolution_convert_fusion.1
  186.5 3.6 convolution_convert_fusion
  190.7 8.2 %feed_back.1 = bf16[512,1536]{1,0:T(8,128)(2,1)} custom-call(bf16[512,1024]{1,0:T(8,128)(2,1)} %get-tuple-element.138.dgu_a.b, bf16[512,1024]{1,0:T(8,128)(2,1)} %get-tuple-element.132.dgu_b, bf16[4,384,1024]{2,1,0:T(8,128)(2,1)} %copy-done.1, bf16[4,384,1024]{2,1,0:T(8,128)(2,1)} %collective-permute-done.12.theirs), custom_call_target="tpu_custom_call" | custom-call | flops 3000000 | tf_op jit(solution)/shard_map/feed_back/pallas_call | solution.py:729
  201.3 2.9 fusion.1.a
  205.9 3.7 ff0.1.a
  209.6 3.7 ff1.1.a
  213.3 3.6 all-to-all-start.3
  216.9 3.9 collective-permute-start.15
  220.8 15.7 %all-to-all-done.3.come = bf16[4,128,1536]{2,1,0:T(8,128)(2,1)S(1)} async-done(((bf16[4,128,1536]{2,1,0:T(8,128)(2,1)}), bf16[4,128,1536]{2,1,0:T(8,128)(2,1)S(1)}, u32[]{:S(2)}, u32[]{:S(2)}) %all-to-all-start.3) | async-done | bytes 1572896 | tf_op jit(solution)/shard_map/all_to_all | solution.py:923
  237.7 4.1 norm_two_back.1
  245.2 4.6 all-to-all-start.4
  249.9 4.8 collective-permute-start.20
  260.8 7.9 %all-to-all-done.4 = bf16[4,128,1536]{2,1,0:T(8,128)(2,1)} async-done(((bf16[4,128,1536]{2,1,0:T(8,128)(2,1)}), bf16[4,128,1536]{2,1,0:T(8,128)(2,1)}, u32[]{:S(2)}, u32[]{:S(2)}) %all-to-all-start.4) | async-done | bytes 1572896 | tf_op jit(solution)/shard_map/all_to_all | solution.py:923
  268.8 3.5 convolution_convert_fusion.5.refs_8_
  272.3 20.4 %attend_backward.1 = (bf16[512,384]{1,0:T(8,128)(2,1)}, bf16[512,384]{1,0:T(8,128)(2,1)}, bf16[512,384]{1,0:T(8,128)(2,1)}, bf16[512,384]{1,0:T(8,128)(2,1)}, f32[3,1,512]{2,1,0:T(1,128)}) custom-call(s32[3]{0:T(128)} %pad_add_fusion.scal, bf16[512,384]{1,0:T(8,128)(2,1)} %get-tuple-element.111.q_ref.refs_0_, ...), custom_call_target="tpu_custom_call" | custom-call | flops 4000000 | tf_op jit(solution)/shard_map/attend_backward/pallas_call | solution.py:589
  298.7 6.6 %collective-permute-done.17.b = bf16[256,1536]{1,0:T(8,128)(2,1)} collective-permute-done((bf16[256,1536]{1,0:T(8,128)(2,1)}, bf16[256,1536]{1,0:T(8,128)(2,1)}, u32[]{:S(2)}, u32[]{:S(2)}) %collective-permute-start.17) | collective-permute-done | bytes 786464 | tf_op jit(solution)/shard_map/ppermute | solution.py:939
  307.8 3.0 pair.9.a
  310.8 3.1 convolution_convert_fusion.3
  323.1 14.0 %collective-permute-done.16.b = bf16[768,1024]{1,0:T(8,128)(2,1)} collective-permute-done((bf16[768,1024]{1,0:T(8,128)(2,1)S(1)}, bf16[768,1024]{1,0:T(8,128)(2,1)}, u32[]{:S(2)}, u32[]{:S(2)}) %collective-permute-start.16) | collective-permute-done | bytes 1572896 | tf_op jit(solution)/shard_map/ppermute | solution.py:939
  337.1 3.0 pair.10.a
  345.8 4.0 all-to-all-start.5
  354.8 13.5 %input_back.1 = (bf16[4,256,1536]{2,1,0:T(8,128)(2,1)}, f32[1,1536]{1,0:T(1,128)}) custom-call(s32[3]{0:T(128)} %pad_add_fusion.scal, bf16[4,128,1536]{2,1,0:T(8,128)(2,1)} %get-tuple-element.110.tok, bf16[512,384]{1,0:T(8,128)(2,1)} %get-tuple-element.143.dq, bf16[512,384]{1,0:T(8,128)(2,1)} %get-tuple-element.144.dk, ...), custom_call_target="tpu_custom_call" | custom-call | flops 4000000 | tf_op jit(solution)/shard_map/input_back/pallas_call | solution.py:606
  368.3 6.4 %collective-permute-done.24.b = bf16[256,1536]{1,0:T(8,128)(2,1)} collective-permute-done((bf16[256,1536]{1,0:T(8,128)(2,1)S(1)}, bf16[256,1536]{1,0:T(8,128)(2,1)}, u32[]{:S(2)}, u32[]{:S(2)}) %collective-permute-start.24) | collective-permute-done | bytes 786464 | tf_op jit(solution)/shard_map/ppermute | solution.py:939
  380.9 3.9 all-to-all-start.6
  384.9 7.6 %collective-permute-start.27 = (bf16[768,768]{1,0:T(8,128)(2,1)}, bf16[768,768]{1,0:T(8,128)(2,1)}, u32[]{:S(2)}, u32[]{:S(2)}) collective-permute-start(bf16[768,768]{1,0:T(8,128)(2,1)} %pad_maximum_fusion.2.a), channel_id=1, source_target_pairs={{0,8},{4,12},{24,16},{28,20},{1,9},{5,13},{25,17},{29,21},{2,10},{... | collective-permute-start | bytes 3538952 | tf_op jit(solution)/shard_map/ppermute | solution.py:939
  393.7 2.9 total.9.a
  398.0 2.9 total.10.a
  404.5 37.6 %collective-permute-start.34 = (bf16[768,768]{1,0:T(8,128)(2,1)}, bf16[768,768]{1,0:T(8,128)(2,1)}, u32[]{:S(2)}, u32[]{:S(2)}) collective-permute-start(bf16[768,768]{1,0:T(8,128)(2,1)} %bitcast.18.a), channel_id=1, source_target_pairs={{0,8},{4,12},{24,16},{28,20},{1,9},{5,13},{25,17},{29,21},{2,10},{... | collective-permute-start | bytes 3538952 | tf_op jit(solution)/shard_map/ppermute | solution.py:939
  444.5 2.6 pair.11.a
  451.5 2.8 result.9
  456.0 4.3 last.1
  461.7 4.8 collective-permute-done.34.b
  466.5 2.7 concatenate.46
  469.8 4.2 all-to-all-start.7
  474.0 2.5 pair.12.a
  476.6 2.6 total.11.a
  480.3 2.8 result.10
  483.2 3.4 pad_maximum_fusion
  486.5 3.9 all-to-all-start.8
  493.8 4.4 collective-permute-start.31
  501.2 5.0 down_grads.1
  506.2 4.9 collective-permute-done.31.b
  514.7 2.6 total.12.a
  518.5 11.4 %collective-permute-done.38.b = bf16[768,768]{1,0:T(8,128)(2,1)} collective-permute-done((bf16[768,768]{1,0:T(8,128)(2,1)}, bf16[768,768]{1,0:T(8,128)(2,1)}, u32[]{:S(2)}, u32[]{:S(2)}) %collective-permute-start.38) | collective-permute-done | bytes 1179680 | tf_op jit(solution)/shard_map/ppermute | solution.py:939
  529.9 2.5 result.11.refs_0_
  539.0 19.8 %collective-permute-done.41.b = bf16[768,768]{1,0:T(8,128)(2,1)} collective-permute-done((bf16[768,768]{1,0:T(8,128)(2,1)}, bf16[768,768]{1,0:T(8,128)(2,1)}, u32[]{:S(2)}, u32[]{:S(2)}) %collective-permute-start.41) | collective-permute-done | bytes 1179680 | tf_op jit(solution)/shard_map/ppermute | solution.py:939
  563.6 7.9 %ff_grads.1 = (f32[384,4096]{1,0:T(8,128)}, f32[384,4096]{1,0:T(8,128)}) custom-call(s32[3]{0:T(128)} %pad_add_fusion.scal, bf16[4,384,1024]{2,1,0:T(8,128)(2,1)} %copy-done, bf16[2,384,1024]{2,1,0:T(8,128)(2,1)} %copy-done.19, bf16[2,384,1024]{2,1,0:T(8,128)(2,1)} %copy-done.18), custom_call_target="tpu_custom_call" | custom-call | flops 4000000 | tf_op jit(solution)/shard_map/ff_grads/pallas_call | solution.py:841
  582.1 7.5 %head_grads.1 = (f32[384,1536]{1,0:T(8,128)}, f32[384,1536]{1,0:T(8,128)}, f32[384,1536]{1,0:T(8,128)}, f32[384,1536]{1,0:T(8,128)}, f32[384,1536]{1,0:T(8,128)}) custom-call(s32[3]{0:T(128)} %pad_add_fusion.scal, bf16[768,768]{1,0:T(8,128)(2,1)} %result.11.refs_0_, bf16[768,768]{1,0:T(8,128)(2,1)} %result.12.refs_1_, bf16[400,768]{1,0:T(8,128)(2,1)} %result.13.refs_2_, ...), custom_call_target="tpu_custom_call" | custom-call | flops 3000000 | tf_op jit(solution)/shard_map/head_grads/pallas_call | solution.py:606
  (222 shorter events, 119.0 us)
Async XLA Ops:
  4.1 15.0 %copy-start.13 = (bf16[144,1536]{1,0:T(8,128)(2,1)}, bf16[144,1536]{1,0:T(8,128)(2,1)S(1)}, u32[]{:S(2)}) copy-start(bf16[144,1536]{1,0:T(8,128)(2,1)S(1)} %maximum_maximum_fusion.1.refs_0_) | copy-start | bytes 1327108
  4.1 15.0 %collective-permute-start.2 = (bf16[144,1536]{1,0:T(8,128)(2,1)S(1)}, bf16[144,1536]{1,0:T(8,128)(2,1)S(1)}, u32[]{:S(2)}, u32[]{:S(2)}) collective-permute-start(bf16[144,1536]{1,0:T(8,128)(2,1)S(1)} %maximum_maximum_fusion.1.refs_0_), channel_id=1, source_target_pairs={{0,3},{1,2},{2,1},{3,0},{4,7},{5,6},{6,5},{7,4},{8,11},{9,10},{10,... | collective-permute-start | bytes 1327112 | tf_op jit(solution)/shard_map/ppermute | solution.py:931
  13.2 40.6 %collective-permute-start.3 = (bf16[384,768]{1,0:T(8,128)(2,1)}, bf16[384,768]{1,0:T(8,128)(2,1)}, u32[]{:S(2)}, u32[]{:S(2)}) collective-permute-start(bf16[384,768]{1,0:T(8,128)(2,1)} %get-tuple-element.106), channel_id=1, source_target_pairs={{0,1},{1,0},{2,3},{3,2},{4,5},{5,4},{6,7},{7,6},{8,9},{9,8},{10,11... | collective-permute-start | bytes 1769480 | tf_op jit(solution)/shard_map/ppermute | solution.py:931
  13.7 40.0 %collective-permute-start.4 = (bf16[384,768]{1,0:T(8,128)(2,1)}, bf16[384,768]{1,0:T(8,128)(2,1)}, u32[]{:S(2)}, u32[]{:S(2)}) collective-permute-start(bf16[384,768]{1,0:T(8,128)(2,1)} %get-tuple-element.107), channel_id=1, source_target_pairs={{0,2},{1,3},{2,0},{3,1},{4,6},{5,7},{6,4},{7,5},{8,10},{9,11},{10,... | collective-permute-start | bytes 1769480 | tf_op jit(solution)/shard_map/ppermute | solution.py:931
  13.8 40.0 %collective-permute-start.5 = (bf16[384,768]{1,0:T(8,128)(2,1)}, bf16[384,768]{1,0:T(8,128)(2,1)}, u32[]{:S(2)}, u32[]{:S(2)}) collective-permute-start(bf16[384,768]{1,0:T(8,128)(2,1)} %get-tuple-element.108), channel_id=1, source_target_pairs={{0,3},{1,2},{2,1},{3,0},{4,7},{5,6},{6,5},{7,4},{8,11},{9,10},{10,... | collective-permute-start | bytes 1769480 | tf_op jit(solution)/shard_map/ppermute | solution.py:931
  16.7 36.3 %collective-permute-start.1 = (bf16[144,1536]{1,0:T(8,128)(2,1)S(1)}, bf16[144,1536]{1,0:T(8,128)(2,1)S(1)}, u32[]{:S(2)}, u32[]{:S(2)}) collective-permute-start(bf16[144,1536]{1,0:T(8,128)(2,1)S(1)} %maximum_maximum_fusion.1.refs_0_), channel_id=1, source_target_pairs={{0,2},{1,3},{2,0},{3,1},{4,6},{5,7},{6,4},{7,5},{8,10},{9,11},{10,... | collective-permute-start | bytes 1327112 | tf_op jit(solution)/shard_map/ppermute | solution.py:931
  19.1 6.8 %copy-start.31 = (bf16[144,1536]{1,0:T(8,128)(2,1)}, bf16[144,1536]{1,0:T(8,128)(2,1)S(1)}, u32[]{:S(2)}) copy-start(bf16[144,1536]{1,0:T(8,128)(2,1)S(1)} %collective-permute-done.2.refs_3_) | copy-start | bytes 1327108
  19.1 34.3 %collective-permute-start = (bf16[144,1536]{1,0:T(8,128)(2,1)S(1)}, bf16[144,1536]{1,0:T(8,128)(2,1)S(1)}, u32[]{:S(2)}, u32[]{:S(2)}) collective-permute-start(bf16[144,1536]{1,0:T(8,128)(2,1)S(1)} %maximum_maximum_fusion.1.refs_0_), channel_id=1, source_target_pairs={{0,1},{1,0},{2,3},{3,2},{4,5},{5,4},{6,7},{7,6},{8,9},{9,8},{10,11... | collective-permute-start | bytes 1327112 | tf_op jit(solution)/shard_map/ppermute | solution.py:931
  54.5 40.2 %all-to-all-start = ((bf16[4,384,1024]{2,1,0:T(8,128)(2,1)}), bf16[4,384,1024]{2,1,0:T(8,128)(2,1)S(1)}, u32[]{:S(2)}, u32[]{:S(2)}) async-start(bf16[4,384,1024]{2,1,0:T(8,128)(2,1)} %pick_hidden.1), calls=%async_computation | async-start | bytes 6291456 | tf_op jit(solution)/shard_map/all_to_all | solution.py:923
  58.4 2.3 collective-permute-start.6
  58.4 3.2 collective-permute-start.7
  59.0 3.5 collective-permute-start.8
  94.8 4.7 copy-start.1
  99.4 70.4 %collective-permute-start.12 = (bf16[4,384,1024]{2,1,0:T(8,128)(2,1)S(1)}, bf16[4,384,1024]{2,1,0:T(8,128)(2,1)}, u32[]{:S(2)}, u32[]{:S(2)}) collective-permute-start(bf16[4,384,1024]{2,1,0:T(8,128)(2,1)S(1)} %all-to-all-done.ours), channel_id=1, source_target_pairs={{0,4},{4,0},{8,12},{12,8},{16,20},{20,16},{24,28},{28,24},{1,5},{5... | collective-permute-start | bytes 9437192 | tf_op jit(solution)/shard_map/ppermute | solution.py:935
  99.4 5.6 copy-start.9
  99.5 42.7 %all-to-all-start.1 = ((bf16[4,128,1536]{2,1,0:T(8,128)(2,1)}), bf16[4,128,1536]{2,1,0:T(8,128)(2,1)}, u32[]{:S(2)}, u32[]{:S(2)}) async-start(bf16[4,128,1536]{2,1,0:T(8,128)(2,1)} %bitcast.54), calls=%async_computation.1 | async-start | bytes 3145728 | tf_op jit(solution)/shard_map/all_to_all | solution.py:923
  106.9 27.4 %collective-permute-start.11 = (bf16[128,1536]{1,0:T(8,128)(2,1)S(1)}, bf16[128,1536]{1,0:T(8,128)(2,1)S(1)}, u32[]{:S(2)}, u32[]{:S(2)}) collective-permute-start(bf16[128,1536]{1,0:T(8,128)(2,1)S(1)} %get-tuple-element.123.c0), channel_id=1, source_target_pairs={{0,3},{1,2},{2,1},{3,0},{4,7},{5,6},{6,5},{7,4},{8,11},{9,10},{10,... | collective-permute-start | bytes 1179656 | tf_op jit(solution)/shard_map/ppermute | solution.py:931
  109.8 31.6 %collective-permute-start.10 = (bf16[128,1536]{1,0:T(8,128)(2,1)S(1)}, bf16[128,1536]{1,0:T(8,128)(2,1)S(1)}, u32[]{:S(2)}, u32[]{:S(2)}) collective-permute-start(bf16[128,1536]{1,0:T(8,128)(2,1)S(1)} %get-tuple-element.123.c0), channel_id=1, source_target_pairs={{0,2},{1,3},{2,0},{3,1},{4,6},{5,7},{6,4},{7,5},{8,10},{9,11},{10,... | collective-permute-start | bytes 1179656 | tf_op jit(solution)/shard_map/ppermute | solution.py:931
  110.4 31.8 %collective-permute-start.9 = (bf16[128,1536]{1,0:T(8,128)(2,1)S(1)}, bf16[128,1536]{1,0:T(8,128)(2,1)}, u32[]{:S(2)}, u32[]{:S(2)}) collective-permute-start(bf16[128,1536]{1,0:T(8,128)(2,1)S(1)} %get-tuple-element.123.c0), channel_id=1, source_target_pairs={{0,1},{1,0},{2,3},{3,2},{4,5},{5,4},{6,7},{7,6},{8,9},{9,8},{10,11... | collective-permute-start | bytes 1179656 | tf_op jit(solution)/shard_map/ppermute | solution.py:931
  134.3 35.5 %copy-start.34 = (bf16[128,1536]{1,0:T(8,128)(2,1)}, bf16[128,1536]{1,0:T(8,128)(2,1)S(1)}, u32[]{:S(2)}) copy-start(bf16[128,1536]{1,0:T(8,128)(2,1)S(1)} %collective-permute-done.11.c3) | copy-start | bytes 1179652
  190.2 14.1 %collective-permute-start.14 = (bf16[1536,1024]{1,0:T(8,128)(2,1)}, bf16[1536,1024]{1,0:T(8,128)(2,1)S(1)}, u32[]{:S(2)}, u32[]{:S(2)}) collective-permute-start(bf16[1536,1024]{1,0:T(8,128)(2,1)} %convolution_convert_fusion), channel_id=1, source_target_pairs={{0,4},{4,0},{8,12},{12,8},{16,20},{20,16},{24,28},{28,24},{1,5},{5... | collective-permute-start | bytes 9437192 | tf_op jit(solution)/shard_map/ppermute | solution.py:935
  190.2 8.7 %collective-permute-start.13 = (bf16[512,1536]{1,0:T(8,128)(2,1)}, bf16[512,1536]{1,0:T(8,128)(2,1)}, u32[]{:S(2)}, u32[]{:S(2)}) collective-permute-start(bf16[512,1536]{1,0:T(8,128)(2,1)} %convolution_convert_fusion.1), channel_id=1, source_target_pairs={{0,4},{4,0},{8,12},{12,8},{16,20},{20,16},{24,28},{28,24},{1,5},{5... | collective-permute-start | bytes 4718600 | tf_op jit(solution)/shard_map/ppermute | solution.py:935
  201.3 15.6 %copy-start.23 = (bf16[256,1536]{1,0:T(8,128)(2,1)}, bf16[256,1536]{1,0:T(8,128)(2,1)S(1)}, u32[]{:S(2)}) copy-start(bf16[256,1536]{1,0:T(8,128)(2,1)S(1)} %fusion.a) | copy-start | bytes 2359300
  213.3 23.2 %all-to-all-start.3 = ((bf16[4,128,1536]{2,1,0:T(8,128)(2,1)}), bf16[4,128,1536]{2,1,0:T(8,128)(2,1)S(1)}, u32[]{:S(2)}, u32[]{:S(2)}) async-start(bf16[4,128,1536]{2,1,0:T(8,128)(2,1)} %bitcast.6), calls=%async_computation.3 | async-start | bytes 3145728 | tf_op jit(solution)/shard_map/all_to_all | solution.py:923
  216.9 24.9 %collective-permute-start.15 = (bf16[256,1536]{1,0:T(8,128)(2,1)S(1)}, bf16[256,1536]{1,0:T(8,128)(2,1)S(1)}, u32[]{:S(2)}, u32[]{:S(2)}) collective-permute-start(bf16[256,1536]{1,0:T(8,128)(2,1)S(1)} %fusion.a), channel_id=1, source_target_pairs={{0,8},{4,12},{24,16},{28,20},{1,9},{5,13},{25,17},{29,21},{2,10},{... | collective-permute-start | bytes 2359304 | tf_op jit(solution)/shard_map/ppermute | solution.py:939
  245.2 11.6 %copy-start.6 = (bf16[768,1024]{1,0:T(8,128)(2,1)S(1)}, bf16[768,1024]{1,0:T(8,128)(2,1)}, u32[]{:S(2)}) copy-start(bf16[768,1024]{1,0:T(8,128)(2,1)} %ff1.1.a) | copy-start | bytes 4718596
  245.2 23.5 %all-to-all-start.4 = ((bf16[4,128,1536]{2,1,0:T(8,128)(2,1)}), bf16[4,128,1536]{2,1,0:T(8,128)(2,1)}, u32[]{:S(2)}, u32[]{:S(2)}) async-start(bf16[4,128,1536]{2,1,0:T(8,128)(2,1)} %get-tuple-element.142), calls=%async_computation.4 | async-start | bytes 3145728 | tf_op jit(solution)/shard_map/all_to_all | solution.py:923
  249.9 57.9 %collective-permute-start.20 = (bf16[768,1024]{1,0:T(8,128)(2,1)S(1)}, bf16[768,1024]{1,0:T(8,128)(2,1)}, u32[]{:S(2)}, u32[]{:S(2)}) collective-permute-start(bf16[768,1024]{1,0:T(8,128)(2,1)S(1)} %copy-done.7), channel_id=1, source_target_pairs={{0,8},{4,12},{24,16},{28,20},{1,9},{5,13},{25,17},{29,21},{2,10},{... | collective-permute-start | bytes 4718600 | tf_op jit(solution)/shard_map/ppermute | solution.py:939
  254.7 50.6 %collective-permute-start.17 = (bf16[256,1536]{1,0:T(8,128)(2,1)}, bf16[256,1536]{1,0:T(8,128)(2,1)}, u32[]{:S(2)}, u32[]{:S(2)}) collective-permute-start(bf16[256,1536]{1,0:T(8,128)(2,1)} %fusion.1.a), channel_id=1, source_target_pairs={{0,8},{4,12},{24,16},{28,20},{1,9},{5,13},{25,17},{29,21},{2,10},{... | collective-permute-start | bytes 2359304 | tf_op jit(solution)/shard_map/ppermute | solution.py:939
  256.9 80.2 %collective-permute-start.16 = (bf16[768,1024]{1,0:T(8,128)(2,1)S(1)}, bf16[768,1024]{1,0:T(8,128)(2,1)}, u32[]{:S(2)}, u32[]{:S(2)}) collective-permute-start(bf16[768,1024]{1,0:T(8,128)(2,1)S(1)} %copy-done.6), channel_id=1, source_target_pairs={{0,8},{4,12},{24,16},{28,20},{1,9},{5,13},{25,17},{29,21},{2,10},{... | collective-permute-start | bytes 4718600 | tf_op jit(solution)/shard_map/ppermute | solution.py:939
  259.3 37.0 %collective-permute-start.18 = (bf16[256,1536]{1,0:T(8,128)(2,1)}, bf16[256,1536]{1,0:T(8,128)(2,1)}, u32[]{:S(2)}, u32[]{:S(2)}) collective-permute-start(bf16[256,1536]{1,0:T(8,128)(2,1)} %pair.7.a), channel_id=1, source_target_pairs={{8,16},{12,20},{16,8},{20,12},{9,17},{13,21},{17,9},{21,13},{10,18... | collective-permute-start | bytes 2359304 | tf_op jit(solution)/shard_map/ppermute | solution.py:939
  313.9 26.1 %collective-permute-start.21 = (bf16[768,768]{1,0:T(8,128)(2,1)}, bf16[768,768]{1,0:T(8,128)(2,1)}, u32[]{:S(2)}, u32[]{:S(2)}) collective-permute-start(bf16[768,768]{1,0:T(8,128)(2,1)} %convolution_convert_fusion.3), channel_id=1, source_target_pairs={{0,4},{4,0},{8,12},{12,8},{16,20},{20,16},{24,28},{28,24},{1,5},{5... | collective-permute-start | bytes 3538952 | tf_op jit(solution)/shard_map/ppermute | solution.py:935
  315.8 26.4 %collective-permute-start.22 = (bf16[768,768]{1,0:T(8,128)(2,1)}, bf16[768,768]{1,0:T(8,128)(2,1)}, u32[]{:S(2)}, u32[]{:S(2)}) collective-permute-start(bf16[768,768]{1,0:T(8,128)(2,1)} %convolution_convert_fusion.2), channel_id=1, source_target_pairs={{0,4},{4,0},{8,12},{12,8},{16,20},{20,16},{24,28},{28,24},{1,5},{5... | collective-permute-start | bytes 3538952 | tf_op jit(solution)/shard_map/ppermute | solution.py:935
  316.3 3.4 collective-permute-start.19
  323.1 17.0 %copy-start.17 = (bf16[512,1536]{1,0:T(8,128)(2,1)S(1)}, bf16[512,1536]{1,0:T(8,128)(2,1)}, u32[]{:S(2)}) copy-start(bf16[512,1536]{1,0:T(8,128)(2,1)} %get-tuple-element.148) | copy-start | bytes 4718596
  345.8 33.0 %all-to-all-start.5 = ((bf16[4,384,768]{2,1,0:T(8,128)(2,1)}), bf16[4,384,768]{2,1,0:T(8,128)(2,1)S(1)}, u32[]{:S(2)}, u32[]{:S(2)}) async-start(bf16[4,384,768]{2,1,0:T(8,128)(2,1)} %bitcast.53), calls=%async_computation.5 | async-start | bytes 4718592 | tf_op jit(solution)/shard_map/all_to_all | solution.py:923
  349.8 24.9 %collective-permute-start.24 = (bf16[256,1536]{1,0:T(8,128)(2,1)S(1)}, bf16[256,1536]{1,0:T(8,128)(2,1)}, u32[]{:S(2)}, u32[]{:S(2)}) collective-permute-start(bf16[256,1536]{1,0:T(8,128)(2,1)S(1)} %copy-done.11), channel_id=1, source_target_pairs={{8,0},{12,4},{16,24},{20,28},{9,1},{13,5},{17,25},{21,29},{10,2},{... | collective-permute-start | bytes 2359304 | tf_op jit(solution)/shard_map/ppermute | solution.py:939
  351.1 25.9 %collective-permute-start.23 = (bf16[384,768]{1,0:T(8,128)(2,1)}, bf16[384,768]{1,0:T(8,128)(2,1)}, u32[]{:S(2)}, u32[]{:S(2)}) collective-permute-start(bf16[384,768]{1,0:T(8,128)(2,1)} %convolution_convert_fusion.4), channel_id=1, source_target_pairs={{0,4},{4,0},{8,12},{12,8},{16,20},{20,16},{24,28},{28,24},{1,5},{5... | collective-permute-start | bytes 1769480 | tf_op jit(solution)/shard_map/ppermute | solution.py:935
  351.1 42.6 %collective-permute-start.25 = (bf16[768,1024]{1,0:T(8,128)(2,1)}, bf16[768,1024]{1,0:T(8,128)(2,1)}, u32[]{:S(2)}, u32[]{:S(2)}) collective-permute-start(bf16[768,1024]{1,0:T(8,128)(2,1)} %pair.9.a), channel_id=1, source_target_pairs={{8,16},{12,20},{16,8},{20,12},{9,17},{13,21},{17,9},{21,13},{10,18... | collective-permute-start | bytes 4718600 | tf_op jit(solution)/shard_map/ppermute | solution.py:939
  353.0 45.0 %collective-permute-start.29 = (bf16[768,1024]{1,0:T(8,128)(2,1)}, bf16[768,1024]{1,0:T(8,128)(2,1)}, u32[]{:S(2)}, u32[]{:S(2)}) collective-permute-start(bf16[768,1024]{1,0:T(8,128)(2,1)} %pair.10.a), channel_id=1, source_target_pairs={{8,16},{12,20},{16,8},{20,12},{9,17},{13,21},{17,9},{21,13},{10,18... | collective-permute-start | bytes 4718600 | tf_op jit(solution)/shard_map/ppermute | solution.py:939
  380.9 73.5 %all-to-all-start.6 = ((bf16[4,256,1536]{2,1,0:T(8,128)(2,1)}), bf16[4,256,1536]{2,1,0:T(8,128)(2,1)S(1)}, u32[]{:S(2)}, u32[]{:S(2)}) async-start(bf16[4,256,1536]{2,1,0:T(8,128)(2,1)} %get-tuple-element.164), calls=%async_computation.6 | async-start | bytes 6291456 | tf_op jit(solution)/shard_map/all_to_all | solution.py:923
  384.9 59.6 %collective-permute-start.27 = (bf16[768,768]{1,0:T(8,128)(2,1)}, bf16[768,768]{1,0:T(8,128)(2,1)}, u32[]{:S(2)}, u32[]{:S(2)}) collective-permute-start(bf16[768,768]{1,0:T(8,128)(2,1)} %pad_maximum_fusion.2.a), channel_id=1, source_target_pairs={{0,8},{4,12},{24,16},{28,20},{1,9},{5,13},{25,17},{29,21},{2,10},{... | collective-permute-start | bytes 3538952 | tf_op jit(solution)/shard_map/ppermute | solution.py:939
  392.4 49.7 %collective-permute-start.28 = (bf16[256,1536]{1,0:T(8,128)(2,1)}, bf16[256,1536]{1,0:T(8,128)(2,1)}, u32[]{:S(2)}, u32[]{:S(2)}) collective-permute-start(bf16[256,1536]{1,0:T(8,128)(2,1)} %total.8.a), channel_id=1, source_target_pairs={{8,0},{12,4},{16,24},{20,28},{9,1},{13,5},{17,25},{21,29},{10,2},{... | collective-permute-start | bytes 2359304 | tf_op jit(solution)/shard_map/ppermute | solution.py:939
  396.7 54.9 %collective-permute-start.26 = (bf16[768,1024]{1,0:T(8,128)(2,1)}, bf16[768,1024]{1,0:T(8,128)(2,1)}, u32[]{:S(2)}, u32[]{:S(2)}) collective-permute-start(bf16[768,1024]{1,0:T(8,128)(2,1)} %total.9.a), channel_id=1, source_target_pairs={{8,0},{12,4},{16,24},{20,28},{9,1},{13,5},{17,25},{21,29},{10,2},{... | collective-permute-start | bytes 4718600 | tf_op jit(solution)/shard_map/ppermute | solution.py:939
  400.9 79.5 %collective-permute-start.32 = (bf16[768,1024]{1,0:T(8,128)(2,1)}, bf16[768,1024]{1,0:T(8,128)(2,1)}, u32[]{:S(2)}, u32[]{:S(2)}) collective-permute-start(bf16[768,1024]{1,0:T(8,128)(2,1)} %total.10.a), channel_id=1, source_target_pairs={{8,0},{12,4},{16,24},{20,28},{9,1},{13,5},{17,25},{21,29},{10,2},{... | collective-permute-start | bytes 4718600 | tf_op jit(solution)/shard_map/ppermute | solution.py:939
  404.5 62.0 %collective-permute-start.34 = (bf16[768,768]{1,0:T(8,128)(2,1)}, bf16[768,768]{1,0:T(8,128)(2,1)}, u32[]{:S(2)}, u32[]{:S(2)}) collective-permute-start(bf16[768,768]{1,0:T(8,128)(2,1)} %bitcast.18.a), channel_id=1, source_target_pairs={{0,8},{4,12},{24,16},{28,20},{1,9},{5,13},{25,17},{29,21},{2,10},{... | collective-permute-start | bytes 3538952 | tf_op jit(solution)/shard_map/ppermute | solution.py:939
  444.5 5.3 copy-start.37
  447.1 29.5 %collective-permute-start.33 = (bf16[768,768]{1,0:T(8,128)(2,1)}, bf16[768,768]{1,0:T(8,128)(2,1)}, u32[]{:S(2)}, u32[]{:S(2)}) collective-permute-start(bf16[768,768]{1,0:T(8,128)(2,1)} %pair.11.a), channel_id=1, source_target_pairs={{8,16},{12,20},{16,8},{20,12},{9,17},{13,21},{17,9},{21,13},{10,18... | collective-permute-start | bytes 3538952 | tf_op jit(solution)/shard_map/ppermute | solution.py:939
  469.8 16.7 %all-to-all-start.7 = ((f32[4,6,384]{2,1,0:T(8,128)}), f32[4,6,384]{2,1,0:T(8,128)S(1)}, u32[]{:S(2)}, u32[]{:S(2)}) async-start(f32[4,6,384]{2,1,0:T(8,128)} %pad_maximum_fusion.4), calls=%async_computation.7 | async-start | bytes 98304 | tf_op jit(solution)/shard_map/all_to_all | solution.py:923
  486.5 47.9 %all-to-all-start.8 = ((bf16[4,384,1024]{2,1,0:T(8,128)(2,1)}), bf16[4,384,1024]{2,1,0:T(8,128)(2,1)S(1)}, u32[]{:S(2)}, u32[]{:S(2)}) async-start(bf16[4,384,1024]{2,1,0:T(8,128)(2,1)} %bitcast.52), calls=%async_computation.8 | async-start | bytes 6291456 | tf_op jit(solution)/shard_map/all_to_all | solution.py:923
  490.6 1.2 collective-permute-start.30
  490.6 10.6 %collective-permute-start.35 = (bf16[256,1536]{1,0:T(8,128)(2,1)}, bf16[256,1536]{1,0:T(8,128)(2,1)}, u32[]{:S(2)}, u32[]{:S(2)}) collective-permute-start(bf16[256,1536]{1,0:T(8,128)(2,1)} %result.7.a0), channel_id=1, source_target_pairs={{0,4},{4,0},{8,12},{12,8},{16,20},{20,16},{24,28},{28,24},{1,5},{5... | collective-permute-start | bytes 2359304 | tf_op jit(solution)/shard_map/ppermute | solution.py:935
  491.1 10.1 %collective-permute-start.36 = (bf16[256,1536]{1,0:T(8,128)(2,1)}, bf16[256,1536]{1,0:T(8,128)(2,1)}, u32[]{:S(2)}, u32[]{:S(2)}) collective-permute-start(bf16[256,1536]{1,0:T(8,128)(2,1)} %result.8.a1), channel_id=1, source_target_pairs={{0,4},{4,0},{8,12},{12,8},{16,20},{20,16},{24,28},{28,24},{1,5},{5... | collective-permute-start | bytes 2359304 | tf_op jit(solution)/shard_map/ppermute | solution.py:935
  493.8 17.4 %collective-permute-start.31 = (bf16[400,768]{1,0:T(8,128)(2,1)}, bf16[400,768]{1,0:T(8,128)(2,1)}, u32[]{:S(2)}, u32[]{:S(2)}) collective-permute-start(bf16[400,768]{1,0:T(8,128)(2,1)} %maximum_maximum_fusion.a), channel_id=1, source_target_pairs={{0,8},{4,12},{24,16},{28,20},{1,9},{5,13},{25,17},{29,21},{2,10},{... | collective-permute-start | bytes 1843208 | tf_op jit(solution)/shard_map/ppermute | solution.py:939
  498.2 16.4 %collective-permute-start.39 = (bf16[768,768]{1,0:T(8,128)(2,1)}, bf16[768,768]{1,0:T(8,128)(2,1)}, u32[]{:S(2)}, u32[]{:S(2)}) collective-permute-start(bf16[768,768]{1,0:T(8,128)(2,1)} %pair.12.a), channel_id=1, source_target_pairs={{8,16},{12,20},{16,8},{20,12},{9,17},{13,21},{17,9},{21,13},{10,18... | collective-permute-start | bytes 3538952 | tf_op jit(solution)/shard_map/ppermute | solution.py:939
  499.9 30.0 %collective-permute-start.38 = (bf16[768,768]{1,0:T(8,128)(2,1)}, bf16[768,768]{1,0:T(8,128)(2,1)}, u32[]{:S(2)}, u32[]{:S(2)}) collective-permute-start(bf16[768,768]{1,0:T(8,128)(2,1)} %total.11.a), channel_id=1, source_target_pairs={{8,0},{12,4},{16,24},{20,28},{9,1},{13,5},{17,25},{21,29},{10,2},{... | collective-permute-start | bytes 3538952 | tf_op jit(solution)/shard_map/ppermute | solution.py:939
  513.2 19.2 %collective-permute-start.37 = (bf16[400,768]{1,0:T(8,128)(2,1)}, bf16[400,768]{1,0:T(8,128)(2,1)}, u32[]{:S(2)}, u32[]{:S(2)}) collective-permute-start(bf16[400,768]{1,0:T(8,128)(2,1)} %pair.13.a), channel_id=1, source_target_pairs={{8,16},{12,20},{16,8},{20,12},{9,17},{13,21},{17,9},{21,13},{10,18... | collective-permute-start | bytes 1843208 | tf_op jit(solution)/shard_map/ppermute | solution.py:939
  517.2 41.6 %collective-permute-start.41 = (bf16[768,768]{1,0:T(8,128)(2,1)}, bf16[768,768]{1,0:T(8,128)(2,1)}, u32[]{:S(2)}, u32[]{:S(2)}) collective-permute-start(bf16[768,768]{1,0:T(8,128)(2,1)} %total.12.a), channel_id=1, source_target_pairs={{8,0},{12,4},{16,24},{20,28},{9,1},{13,5},{17,25},{21,29},{10,2},{... | collective-permute-start | bytes 3538952 | tf_op jit(solution)/shard_map/ppermute | solution.py:939
  537.1 24.2 %collective-permute-start.43 = (bf16[2,384,1024]{2,1,0:T(8,128)(2,1)}, bf16[2,384,1024]{2,1,0:T(8,128)(2,1)S(1)}, u32[]{:S(2)}, u32[]{:S(2)}) collective-permute-start(bf16[2,384,1024]{2,1,0:T(8,128)(2,1)} %get-tuple-element.200), channel_id=1, source_target_pairs={{0,4},{4,0},{8,12},{12,8},{16,20},{20,16},{24,28},{28,24},{1,5},{5... | collective-permute-start | bytes 4718600 | tf_op jit(solution)/shard_map/ppermute | solution.py:935
  537.1 24.2 %collective-permute-start.42 = (bf16[2,384,1024]{2,1,0:T(8,128)(2,1)}, bf16[2,384,1024]{2,1,0:T(8,128)(2,1)S(1)}, u32[]{:S(2)}, u32[]{:S(2)}) collective-permute-start(bf16[2,384,1024]{2,1,0:T(8,128)(2,1)} %get-tuple-element.201), channel_id=1, source_target_pairs={{0,4},{4,0},{8,12},{12,8},{16,20},{20,16},{24,28},{28,24},{1,5},{5... | collective-permute-start | bytes 4718600 | tf_op jit(solution)/shard_map/ppermute | solution.py:935
  537.6 33.9 %collective-permute-start.40 = (bf16[400,768]{1,0:T(8,128)(2,1)}, bf16[400,768]{1,0:T(8,128)(2,1)S(1)}, u32[]{:S(2)}, u32[]{:S(2)}) collective-permute-start(bf16[400,768]{1,0:T(8,128)(2,1)} %total.13.a), channel_id=1, source_target_pairs={{8,0},{12,4},{16,24},{20,28},{9,1},{13,5},{17,25},{21,29},{10,2},{... | collective-permute-start | bytes 1843208 | tf_op jit(solution)/shard_map/ppermute | solution.py:939
  538.9 42.4 %collective-permute-start.44 = (bf16[768,768]{1,0:T(8,128)(2,1)}, bf16[768,768]{1,0:T(8,128)(2,1)}, u32[]{:S(2)}, u32[]{:S(2)}) collective-permute-start(bf16[768,768]{1,0:T(8,128)(2,1)} %result.11.refs_0_), channel_id=1, source_target_pairs={{0,4},{4,0},{8,12},{12,8},{16,20},{20,16},{24,28},{28,24},{1,5},{5... | collective-permute-start | bytes 3538952 | tf_op jit(solution)/shard_map/ppermute | solution.py:935
  561.3 20.0 %collective-permute-start.45 = (bf16[768,768]{1,0:T(8,128)(2,1)}, bf16[768,768]{1,0:T(8,128)(2,1)}, u32[]{:S(2)}, u32[]{:S(2)}) collective-permute-start(bf16[768,768]{1,0:T(8,128)(2,1)} %result.12.refs_1_), channel_id=1, source_target_pairs={{0,4},{4,0},{8,12},{12,8},{16,20},{20,16},{24,28},{28,24},{1,5},{5... | collective-permute-start | bytes 3538952 | tf_op jit(solution)/shard_map/ppermute | solution.py:935
  575.4 5.8 collective-permute-start.46
  (33 other events, 81.7 us)

commit v5 on v4

--- a/solution.py
+++ b/solution.py
@@ -806,22 +806,44 @@
 
 
 def head_grads_kernel(scal, *refs):
-    ours, theirs, outs = refs[:3], refs[3:6], refs[6:]
+    ours, theirs, outs = refs[:5], refs[5:10], refs[10:]
     first = scal[1] == 0
-    part, width = outs[0].shape
+    part = ours[0].shape[1] // 2
     for k in range(5):
-        at = slice((k % 2) * part, (k % 2 + 1) * part)
-        a, b = ours[k // 2][at, :], theirs[k // 2][at, :]
+        a, b = ours[k][...], theirs[k][...]
         low, high = jnp.where(first, a, b).astype(f32), jnp.where(first, b, a).astype(f32)
         if k == 0:
-            outs[4][:, : width // 2] = low
-            outs[4][:, width // 2 :] = high
+            outs[4][:, : 2 * part] = low
+            outs[4][:, 2 * part :] = high
         else:
             at = slice((k - 1) * part, k * part)
             outs[0][:, at] = low[:, :part]
             outs[1][:, at] = low[:, part:]
             outs[2][:, at] = high[:, :part]
             outs[3][:, at] = high[:, part:]
+
+
+def head_grads(scal, ours, theirs, rows):
+    cols = ours[0].shape[1]
+    steps = rows // 128
+    low = pl.BlockSpec((128, cols), lambda i: (i, 0))
+    high = pl.BlockSpec((128, cols), lambda i: (steps + i, 0))
+    out = pl.BlockSpec((128, 2 * cols), lambda i: (i, 0))
+
+    def five(group):
+        first, second, third = group
+        return (first, first, second, second, third)
+
+    return pl.pallas_call(
+        head_grads_kernel,
+        grid=(steps,),
+        in_specs=[pl.BlockSpec(memory_space=pltpu.SMEM)] + [low, high, low, high, low] * 2,
+        out_specs=[out] * 5,
+        out_shape=[struct((rows, 2 * cols), f32)] * 5,
+        compiler_params=grant(),
+        cost_estimate=cost(3),
+        name="head_grads",
+    )(scal, *five(ours), *five(theirs))
 
 
 def ff_grads_kernel(scal, ours, low, high, gate, up):
@@ -1279,10 +1301,7 @@
 
     ours = (zsum.out["first"], zsum.out["second"], last)
     theirs = [core_swap(v) for v in (zsum.out["first"], zsum.out["second"], last[:part])]
-    head_grad = struct((part, width), f32)
-    grad_query, grad_key, grad_value, grad_path, grad_out = whole(
-        head_grads_kernel, "head_grads", 3, [head_grad] * 5, scal, *ours, *theirs
-    )
+    grad_query, grad_key, grad_value, grad_path, grad_out = head_grads(scal, ours, theirs, part)
     return (
         output,
         input_grad,

time: 604 us -> 603 us (level)
    pallas_call x11 -> x10, Pallas kernels: 74.5 us -> 67 us  [whole(): pl.pallas_call(kernel, in_specs=[pl.BlockSpec(memory_space=pltpu.SMEM)] +...]
    pallas_call x0 -> x1, Pallas kernels: none -> 7.11 us  [head_grads(): pl.pallas_call(head_grads_kernel, grid=(steps,), in_specs=[pl.BlockSpec(m...]
where the time goes in v5:
time: 603 us; the launch traced here: 593 us
  Pallas kernels  191 us (32%)
  waiting for transfers between devices  160 us (27%)
  starting transfers between devices  133 us (22%)
  matrix products  31.4 us (5%)
  local copies, waits for them, and re-layouts  27.1 us (4%)
  blocking collectives  24.4 us (4%)
  other arithmetic  17.8 us (3%)
  between operations  8.47 us (1%)
    ppermute x21, starting transfers between devices, chip_send(): lax.ppermute(value, 'rep', [(2 * a + c, 2 * b + c) for a, b in pairs for...  83.2 us
    ppermute x21, waiting for transfers between devices, chip_send(): lax.ppermute(value, 'rep', [(2 * a + c, 2 * b + c) for a, b in pairs for...  69.2 us
    pallas_call x10, Pallas kernels, whole(): pl.pallas_call(kernel, in_specs=[pl.BlockSpec(memory_space=pltpu.SMEM)] +...  67 us
    ppermute x9, waiting for transfers between devices, shard_swap(): return lax.ppermute(value, 'shard', [(i, i ^ k) for i in range(SHARDS)])  60.4 us
    pallas_call x21, Pallas kernels, blocked(): pl.pallas_call(kernel, grid=(rows // step,), in_specs=[pl.BlockSpec(memor...  53.4 us
    all_to_all x8, starting transfers between devices, shard_exchange(): return lax.all_to_all(blocks, 'shard', 0, 0)  33 us
    dot_general x10, matrix products, dot_tn(): lax.dot_general(a, b, (((0,), (0,)), ((), ())), preferred_element_type=f32)  26.2 us
    all_to_all x8, waiting for transfers between devices, shard_exchange(): return lax.all_to_all(blocks, 'shard', 0, 0)  26 us
  transfers between devices with their start and end apart: 55, of which 20 were waited for; matrix products, arithmetic and copies ran while one was open for 8% of the time, Pallas kernels for 26%

profile of v5, /device:TPU:0, one launch (start us, length us, event | category | flops | bytes accessed | tf_op | source)
XLA Modules:
  0.0 592.5 jit_solution(13982842688614208846)
XLA Ops:
  4.1 4.0 collective-permute-start.2
  9.4 3.8 pick_heads.1
  13.8 2.9 collective-permute-start.5
  21.1 4.8 pick_hidden.1
  25.9 27.2 %collective-permute-done.1.refs_2_ = bf16[144,1536]{1,0:T(8,128)(2,1)S(1)} collective-permute-done((bf16[144,1536]{1,0:T(8,128)(2,1)S(1)}, bf16[144,1536]{1,0:T(8,128)(2,1)S(1)}, u32[]{:S(2)}, u32[]{:S(2)}) %collective-permute-start.1) | collective-permute-done | bytes 442400 | tf_op jit(solution)/shard_map/ppermute | solution.py:953
  54.5 3.9 all-to-all-start
  62.5 10.8 %project.1 = (bf16[4,128,1536]{2,1,0:T(8,128)(2,1)}, bf16[512,1536]{1,0:T(8,128)(2,1)}, bf16[512,384]{1,0:T(8,128)(2,1)}, bf16[512,384]{1,0:T(8,128)(2,1)}, bf16...) custom-call(s32[3]{0:T(128)} %pad_add_fusion.scal, ...), custom_call_target="tpu_custom_call" | custom-call | flops 4000000 | tf_op jit(solution)/shard_map/project/pallas_call | solution.py:606
  73.3 19.1 %attend_forward.1 = (bf16[512,384]{1,0:T(8,128)(2,1)}, bf16[3,2,512,512]{3,2,1,0:T(8,128)(2,1)}, bf16[3,2,512,512]{3,2,1,0:T(8,128)(2,1)}, f32[3,512,512]{2,1,0:T(8,128)}) custom-call(s32[3]{0:T(128)} %pad_add_fusion.scal, bf16[512,384]{1,0:T(8,128)(2,1)} %get-tuple-element.111.q_ref.refs_0_, bf16[512,384]{1,0:T(8,128)(2,1)} %get-tuple-element.112.k_ref.refs_1_, ...), custom_call_target="tpu_custom_call" | custom-call | flops 8000000 | tf_op jit(solution)/shard_map/attend_forward/pallas_call | solution.py:571
  94.8 4.7 out_project.1
  99.5 5.0 all-to-all-start.1
  106.9 2.9 collective-permute-start.11
  110.4 23.9 %collective-permute-done.11.c3 = bf16[128,1536]{1,0:T(8,128)(2,1)S(1)} collective-permute-done((bf16[128,1536]{1,0:T(8,128)(2,1)S(1)}, bf16[128,1536]{1,0:T(8,128)(2,1)S(1)}, u32[]{:S(2)}, u32[]{:S(2)}) %collective-permute-start.11) | collective-permute-done | bytes 393248 | tf_op jit(solution)/shard_map/ppermute | solution.py:953
  134.3 7.1 %collective-permute-done.10.c2 = bf16[128,1536]{1,0:T(8,128)(2,1)S(1)} collective-permute-done((bf16[128,1536]{1,0:T(8,128)(2,1)S(1)}, bf16[128,1536]{1,0:T(8,128)(2,1)S(1)}, u32[]{:S(2)}, u32[]{:S(2)}) %collective-permute-start.10) | collective-permute-done | bytes 393248 | tf_op jit(solution)/shard_map/ppermute | solution.py:953
  142.1 3.3 residual_norm.1
  145.4 24.4 %all_to_all.45 = bf16[4,128,1536]{2,1,0:T(8,128)(2,1)} all-to-all(bf16[4,128,1536]{2,1,0:T(8,128)(2,1)} %get-tuple-element.126), channel_id=1, replica_groups=mesh['rep'=8,'shard'=4] {'shard'}, dimensions={0} | all-to-all | bytes 3145728 | tf_op jit(solution)/shard_map/all_to_all | solution.py:945
  169.8 12.8 %feed.1 = (bf16[512,512]{1,0:T(8,128)(2,1)}, bf16[512,512]{1,0:T(8,128)(2,1)}, bf16[512,1024]{1,0:T(8,128)(2,1)}, bf16[512,1024]{1,0:T(8,128)(2,1)}, bf16[512,1536]{1,0:T(8,128)(2,1)}) custom-call(s32[3]{0:T(128)} %pad_add_fusion.scal, bf16[512,1536]{1,0:T(8,128)(2,1)} %bitcast.48, bf16[128,1536]{1,0:T(8,128)(2,1)} %copy-done.16, ...), custom_call_target="tpu_custom_call" | custom-call | flops 6000000 | tf_op jit(solution)/shard_map/feed/pallas_call | solution.py:606
  182.7 3.9 convolution_convert_fusion.1
  186.5 3.6 convolution_convert_fusion
  190.7 8.2 %feed_back.1 = bf16[512,1536]{1,0:T(8,128)(2,1)} custom-call(bf16[512,1024]{1,0:T(8,128)(2,1)} %get-tuple-element.138.dgu_a.b, bf16[512,1024]{1,0:T(8,128)(2,1)} %get-tuple-element.132.dgu_b, bf16[4,384,1024]{2,1,0:T(8,128)(2,1)} %copy-done.1, bf16[4,384,1024]{2,1,0:T(8,128)(2,1)} %collective-permute-done.12.theirs), custom_call_target="tpu_custom_call" | custom-call | flops 3000000 | tf_op jit(solution)/shard_map/feed_back/pallas_call | solution.py:729
  201.3 2.9 fusion.1.a
  205.9 3.7 ff0.1.a
  209.6 3.7 ff1.1.a
  213.3 3.6 all-to-all-start.3
  216.9 3.9 collective-permute-start.15
  220.8 15.7 %all-to-all-done.3.come = bf16[4,128,1536]{2,1,0:T(8,128)(2,1)S(1)} async-done(((bf16[4,128,1536]{2,1,0:T(8,128)(2,1)}), bf16[4,128,1536]{2,1,0:T(8,128)(2,1)S(1)}, u32[]{:S(2)}, u32[]{:S(2)}) %all-to-all-start.3) | async-done | bytes 1572896 | tf_op jit(solution)/shard_map/all_to_all | solution.py:945
  237.7 4.1 norm_two_back.1
  245.2 4.6 all-to-all-start.4
  249.9 4.8 collective-permute-start.20
  260.8 7.9 %all-to-all-done.4 = bf16[4,128,1536]{2,1,0:T(8,128)(2,1)} async-done(((bf16[4,128,1536]{2,1,0:T(8,128)(2,1)}), bf16[4,128,1536]{2,1,0:T(8,128)(2,1)}, u32[]{:S(2)}, u32[]{:S(2)}) %all-to-all-start.4) | async-done | bytes 1572896 | tf_op jit(solution)/shard_map/all_to_all | solution.py:945
  268.8 3.5 convolution_convert_fusion.5.refs_8_
  272.3 20.4 %attend_backward.1 = (bf16[512,384]{1,0:T(8,128)(2,1)}, bf16[512,384]{1,0:T(8,128)(2,1)}, bf16[512,384]{1,0:T(8,128)(2,1)}, bf16[512,384]{1,0:T(8,128)(2,1)}, f32[3,1,512]{2,1,0:T(1,128)}) custom-call(s32[3]{0:T(128)} %pad_add_fusion.scal, bf16[512,384]{1,0:T(8,128)(2,1)} %get-tuple-element.111.q_ref.refs_0_, ...), custom_call_target="tpu_custom_call" | custom-call | flops 4000000 | tf_op jit(solution)/shard_map/attend_backward/pallas_call | solution.py:589
  298.7 6.6 %collective-permute-done.17.b = bf16[256,1536]{1,0:T(8,128)(2,1)} collective-permute-done((bf16[256,1536]{1,0:T(8,128)(2,1)}, bf16[256,1536]{1,0:T(8,128)(2,1)}, u32[]{:S(2)}, u32[]{:S(2)}) %collective-permute-start.17) | collective-permute-done | bytes 786464 | tf_op jit(solution)/shard_map/ppermute | solution.py:961
  307.8 3.0 pair.9.a
  310.8 3.1 convolution_convert_fusion.3
  323.1 14.0 %collective-permute-done.16.b = bf16[768,1024]{1,0:T(8,128)(2,1)} collective-permute-done((bf16[768,1024]{1,0:T(8,128)(2,1)S(1)}, bf16[768,1024]{1,0:T(8,128)(2,1)}, u32[]{:S(2)}, u32[]{:S(2)}) %collective-permute-start.16) | collective-permute-done | bytes 1572896 | tf_op jit(solution)/shard_map/ppermute | solution.py:961
  337.1 3.0 pair.10.a
  345.8 4.0 all-to-all-start.5
  354.8 13.5 %input_back.1 = (bf16[4,256,1536]{2,1,0:T(8,128)(2,1)}, f32[1,1536]{1,0:T(1,128)}) custom-call(s32[3]{0:T(128)} %pad_add_fusion.scal, bf16[4,128,1536]{2,1,0:T(8,128)(2,1)} %get-tuple-element.110.tok, bf16[512,384]{1,0:T(8,128)(2,1)} %get-tuple-element.143.dq, bf16[512,384]{1,0:T(8,128)(2,1)} %get-tuple-element.144.dk, ...), custom_call_target="tpu_custom_call" | custom-call | flops 4000000 | tf_op jit(solution)/shard_map/input_back/pallas_call | solution.py:606
  368.3 6.4 %collective-permute-done.24.b = bf16[256,1536]{1,0:T(8,128)(2,1)} collective-permute-done((bf16[256,1536]{1,0:T(8,128)(2,1)S(1)}, bf16[256,1536]{1,0:T(8,128)(2,1)}, u32[]{:S(2)}, u32[]{:S(2)}) %collective-permute-start.24) | collective-permute-done | bytes 786464 | tf_op jit(solution)/shard_map/ppermute | solution.py:961
  380.9 3.9 all-to-all-start.6
  384.9 7.6 %collective-permute-start.27 = (bf16[768,768]{1,0:T(8,128)(2,1)}, bf16[768,768]{1,0:T(8,128)(2,1)}, u32[]{:S(2)}, u32[]{:S(2)}) collective-permute-start(bf16[768,768]{1,0:T(8,128)(2,1)} %pad_maximum_fusion.2.a), channel_id=1, source_target_pairs={{0,8},{4,12},{24,16},{28,20},{1,9},{5,13},{25,17},{29,21},{2,10},{... | collective-permute-start | bytes 3538952 | tf_op jit(solution)/shard_map/ppermute | solution.py:961
  393.7 2.9 total.9.a
  398.0 2.9 total.10.a
  404.5 37.6 %collective-permute-start.34 = (bf16[768,768]{1,0:T(8,128)(2,1)}, bf16[768,768]{1,0:T(8,128)(2,1)}, u32[]{:S(2)}, u32[]{:S(2)}) collective-permute-start(bf16[768,768]{1,0:T(8,128)(2,1)} %bitcast.18.a), channel_id=1, source_target_pairs={{0,8},{4,12},{24,16},{28,20},{1,9},{5,13},{25,17},{29,21},{2,10},{... | collective-permute-start | bytes 3538952 | tf_op jit(solution)/shard_map/ppermute | solution.py:961
  444.5 2.6 pair.11.a
  451.5 2.8 result.9
  456.0 4.3 last.1
  461.7 4.8 collective-permute-done.34.b
  466.5 2.7 concatenate.46
  469.8 4.2 all-to-all-start.7
  474.0 2.5 pair.12.a
  476.6 2.6 total.11.a
  480.3 2.8 result.10
  483.2 3.4 pad_maximum_fusion
  486.5 3.9 all-to-all-start.8
  493.8 4.4 collective-permute-start.31
  501.2 5.0 down_grads.1
  506.2 4.9 collective-permute-done.31.b
  514.7 2.6 total.12.a
  518.5 11.4 %collective-permute-done.38.b = bf16[768,768]{1,0:T(8,128)(2,1)} collective-permute-done((bf16[768,768]{1,0:T(8,128)(2,1)}, bf16[768,768]{1,0:T(8,128)(2,1)}, u32[]{:S(2)}, u32[]{:S(2)}) %collective-permute-start.38) | collective-permute-done | bytes 1179680 | tf_op jit(solution)/shard_map/ppermute | solution.py:961
  538.9 19.9 %collective-permute-done.41.b = bf16[768,768]{1,0:T(8,128)(2,1)} collective-permute-done((bf16[768,768]{1,0:T(8,128)(2,1)}, bf16[768,768]{1,0:T(8,128)(2,1)}, u32[]{:S(2)}, u32[]{:S(2)}) %collective-permute-start.41) | collective-permute-done | bytes 1179680 | tf_op jit(solution)/shard_map/ppermute | solution.py:961
  558.8 2.5 result.12.refs_2_.refs_3_
  562.5 7.9 %ff_grads.1 = (f32[384,4096]{1,0:T(8,128)}, f32[384,4096]{1,0:T(8,128)}) custom-call(s32[3]{0:T(128)} %pad_add_fusion.scal, bf16[4,384,1024]{2,1,0:T(8,128)(2,1)} %copy-done, bf16[2,384,1024]{2,1,0:T(8,128)(2,1)} %collective-permute-done.42.low, bf16[2,384,1024]{2,1,0:T(8,128)(2,1)} %copy-done.20), custom_call_target="tpu_custom_call" | custom-call | flops 4000000 | tf_op jit(solution)/shard_map/ff_grads/pallas_call | solution.py:863
  581.6 7.1 %head_grads.1 = (f32[384,1536]{1,0:T(8,128)}, f32[384,1536]{1,0:T(8,128)}, f32[384,1536]{1,0:T(8,128)}, f32[384,1536]{1,0:T(8,128)}, f32[384,1536]{1,0:T(8,128)}) custom-call(s32[3]{0:T(128)} %pad_add_fusion.scal, bf16[768,768]{1,0:T(8,128)(2,1)} %result.11.refs_0_.refs_1_, bf16[768,768]{1,0:T(8,128)(2,1)} %result.11.refs_0_.refs_1_, ...), custom_call_target="tpu_custom_call" | custom-call | flops 3000000 | tf_op jit(solution)/shard_map/head_grads/pallas_call | solution.py:837
  (222 shorter events, 118.4 us)
Async XLA Ops:
  4.1 15.0 %copy-start.15 = (bf16[144,1536]{1,0:T(8,128)(2,1)}, bf16[144,1536]{1,0:T(8,128)(2,1)S(1)}, u32[]{:S(2)}) copy-start(bf16[144,1536]{1,0:T(8,128)(2,1)S(1)} %maximum_maximum_fusion.1.refs_0_) | copy-start | bytes 1327108
  4.1 15.0 %collective-permute-start.2 = (bf16[144,1536]{1,0:T(8,128)(2,1)S(1)}, bf16[144,1536]{1,0:T(8,128)(2,1)S(1)}, u32[]{:S(2)}, u32[]{:S(2)}) collective-permute-start(bf16[144,1536]{1,0:T(8,128)(2,1)S(1)} %maximum_maximum_fusion.1.refs_0_), channel_id=1, source_target_pairs={{0,3},{1,2},{2,1},{3,0},{4,7},{5,6},{6,5},{7,4},{8,11},{9,10},{10,... | collective-permute-start | bytes 1327112 | tf_op jit(solution)/shard_map/ppermute | solution.py:953
  13.2 40.6 %collective-permute-start.3 = (bf16[384,768]{1,0:T(8,128)(2,1)}, bf16[384,768]{1,0:T(8,128)(2,1)}, u32[]{:S(2)}, u32[]{:S(2)}) collective-permute-start(bf16[384,768]{1,0:T(8,128)(2,1)} %get-tuple-element.106), channel_id=1, source_target_pairs={{0,1},{1,0},{2,3},{3,2},{4,5},{5,4},{6,7},{7,6},{8,9},{9,8},{10,11... | collective-permute-start | bytes 1769480 | tf_op jit(solution)/shard_map/ppermute | solution.py:953
  13.7 40.0 %collective-permute-start.4 = (bf16[384,768]{1,0:T(8,128)(2,1)}, bf16[384,768]{1,0:T(8,128)(2,1)}, u32[]{:S(2)}, u32[]{:S(2)}) collective-permute-start(bf16[384,768]{1,0:T(8,128)(2,1)} %get-tuple-element.107), channel_id=1, source_target_pairs={{0,2},{1,3},{2,0},{3,1},{4,6},{5,7},{6,4},{7,5},{8,10},{9,11},{10,... | collective-permute-start | bytes 1769480 | tf_op jit(solution)/shard_map/ppermute | solution.py:953
  13.8 40.0 %collective-permute-start.5 = (bf16[384,768]{1,0:T(8,128)(2,1)}, bf16[384,768]{1,0:T(8,128)(2,1)}, u32[]{:S(2)}, u32[]{:S(2)}) collective-permute-start(bf16[384,768]{1,0:T(8,128)(2,1)} %get-tuple-element.108), channel_id=1, source_target_pairs={{0,3},{1,2},{2,1},{3,0},{4,7},{5,6},{6,5},{7,4},{8,11},{9,10},{10,... | collective-permute-start | bytes 1769480 | tf_op jit(solution)/shard_map/ppermute | solution.py:953
  16.7 36.3 %collective-permute-start.1 = (bf16[144,1536]{1,0:T(8,128)(2,1)S(1)}, bf16[144,1536]{1,0:T(8,128)(2,1)S(1)}, u32[]{:S(2)}, u32[]{:S(2)}) collective-permute-start(bf16[144,1536]{1,0:T(8,128)(2,1)S(1)} %maximum_maximum_fusion.1.refs_0_), channel_id=1, source_target_pairs={{0,2},{1,3},{2,0},{3,1},{4,6},{5,7},{6,4},{7,5},{8,10},{9,11},{10,... | collective-permute-start | bytes 1327112 | tf_op jit(solution)/shard_map/ppermute | solution.py:953
  19.1 6.8 %copy-start.31 = (bf16[144,1536]{1,0:T(8,128)(2,1)}, bf16[144,1536]{1,0:T(8,128)(2,1)S(1)}, u32[]{:S(2)}) copy-start(bf16[144,1536]{1,0:T(8,128)(2,1)S(1)} %collective-permute-done.2.refs_3_) | copy-start | bytes 1327108
  19.1 34.3 %collective-permute-start = (bf16[144,1536]{1,0:T(8,128)(2,1)S(1)}, bf16[144,1536]{1,0:T(8,128)(2,1)S(1)}, u32[]{:S(2)}, u32[]{:S(2)}) collective-permute-start(bf16[144,1536]{1,0:T(8,128)(2,1)S(1)} %maximum_maximum_fusion.1.refs_0_), channel_id=1, source_target_pairs={{0,1},{1,0},{2,3},{3,2},{4,5},{5,4},{6,7},{7,6},{8,9},{9,8},{10,11... | collective-permute-start | bytes 1327112 | tf_op jit(solution)/shard_map/ppermute | solution.py:953
  54.5 40.2 %all-to-all-start = ((bf16[4,384,1024]{2,1,0:T(8,128)(2,1)}), bf16[4,384,1024]{2,1,0:T(8,128)(2,1)S(1)}, u32[]{:S(2)}, u32[]{:S(2)}) async-start(bf16[4,384,1024]{2,1,0:T(8,128)(2,1)} %pick_hidden.1), calls=%async_computation | async-start | bytes 6291456 | tf_op jit(solution)/shard_map/all_to_all | solution.py:945
  58.4 2.3 collective-permute-start.6
  58.4 3.2 collective-permute-start.7
  59.0 3.5 collective-permute-start.8
  94.8 4.7 copy-start.1
  99.4 70.4 %collective-permute-start.12 = (bf16[4,384,1024]{2,1,0:T(8,128)(2,1)S(1)}, bf16[4,384,1024]{2,1,0:T(8,128)(2,1)}, u32[]{:S(2)}, u32[]{:S(2)}) collective-permute-start(bf16[4,384,1024]{2,1,0:T(8,128)(2,1)S(1)} %all-to-all-done.ours), channel_id=1, source_target_pairs={{0,4},{4,0},{8,12},{12,8},{16,20},{20,16},{24,28},{28,24},{1,5},{5... | collective-permute-start | bytes 9437192 | tf_op jit(solution)/shard_map/ppermute | solution.py:957
  99.4 5.6 copy-start.9
  99.5 42.7 %all-to-all-start.1 = ((bf16[4,128,1536]{2,1,0:T(8,128)(2,1)}), bf16[4,128,1536]{2,1,0:T(8,128)(2,1)}, u32[]{:S(2)}, u32[]{:S(2)}) async-start(bf16[4,128,1536]{2,1,0:T(8,128)(2,1)} %bitcast.54), calls=%async_computation.1 | async-start | bytes 3145728 | tf_op jit(solution)/shard_map/all_to_all | solution.py:945
  106.9 27.4 %collective-permute-start.11 = (bf16[128,1536]{1,0:T(8,128)(2,1)S(1)}, bf16[128,1536]{1,0:T(8,128)(2,1)S(1)}, u32[]{:S(2)}, u32[]{:S(2)}) collective-permute-start(bf16[128,1536]{1,0:T(8,128)(2,1)S(1)} %get-tuple-element.123.c0), channel_id=1, source_target_pairs={{0,3},{1,2},{2,1},{3,0},{4,7},{5,6},{6,5},{7,4},{8,11},{9,10},{10,... | collective-permute-start | bytes 1179656 | tf_op jit(solution)/shard_map/ppermute | solution.py:953
  109.8 31.6 %collective-permute-start.10 = (bf16[128,1536]{1,0:T(8,128)(2,1)S(1)}, bf16[128,1536]{1,0:T(8,128)(2,1)S(1)}, u32[]{:S(2)}, u32[]{:S(2)}) collective-permute-start(bf16[128,1536]{1,0:T(8,128)(2,1)S(1)} %get-tuple-element.123.c0), channel_id=1, source_target_pairs={{0,2},{1,3},{2,0},{3,1},{4,6},{5,7},{6,4},{7,5},{8,10},{9,11},{10,... | collective-permute-start | bytes 1179656 | tf_op jit(solution)/shard_map/ppermute | solution.py:953
  110.4 31.8 %collective-permute-start.9 = (bf16[128,1536]{1,0:T(8,128)(2,1)S(1)}, bf16[128,1536]{1,0:T(8,128)(2,1)}, u32[]{:S(2)}, u32[]{:S(2)}) collective-permute-start(bf16[128,1536]{1,0:T(8,128)(2,1)S(1)} %get-tuple-element.123.c0), channel_id=1, source_target_pairs={{0,1},{1,0},{2,3},{3,2},{4,5},{5,4},{6,7},{7,6},{8,9},{9,8},{10,11... | collective-permute-start | bytes 1179656 | tf_op jit(solution)/shard_map/ppermute | solution.py:953
  134.3 35.5 %copy-start.34 = (bf16[128,1536]{1,0:T(8,128)(2,1)}, bf16[128,1536]{1,0:T(8,128)(2,1)S(1)}, u32[]{:S(2)}) copy-start(bf16[128,1536]{1,0:T(8,128)(2,1)S(1)} %collective-permute-done.11.c3) | copy-start | bytes 1179652
  190.2 14.1 %collective-permute-start.14 = (bf16[1536,1024]{1,0:T(8,128)(2,1)}, bf16[1536,1024]{1,0:T(8,128)(2,1)S(1)}, u32[]{:S(2)}, u32[]{:S(2)}) collective-permute-start(bf16[1536,1024]{1,0:T(8,128)(2,1)} %convolution_convert_fusion), channel_id=1, source_target_pairs={{0,4},{4,0},{8,12},{12,8},{16,20},{20,16},{24,28},{28,24},{1,5},{5... | collective-permute-start | bytes 9437192 | tf_op jit(solution)/shard_map/ppermute | solution.py:957
  190.2 8.7 %collective-permute-start.13 = (bf16[512,1536]{1,0:T(8,128)(2,1)}, bf16[512,1536]{1,0:T(8,128)(2,1)}, u32[]{:S(2)}, u32[]{:S(2)}) collective-permute-start(bf16[512,1536]{1,0:T(8,128)(2,1)} %convolution_convert_fusion.1), channel_id=1, source_target_pairs={{0,4},{4,0},{8,12},{12,8},{16,20},{20,16},{24,28},{28,24},{1,5},{5... | collective-permute-start | bytes 4718600 | tf_op jit(solution)/shard_map/ppermute | solution.py:957
  201.3 15.6 %copy-start.24 = (bf16[256,1536]{1,0:T(8,128)(2,1)}, bf16[256,1536]{1,0:T(8,128)(2,1)S(1)}, u32[]{:S(2)}) copy-start(bf16[256,1536]{1,0:T(8,128)(2,1)S(1)} %fusion.a) | copy-start | bytes 2359300
  213.3 23.2 %all-to-all-start.3 = ((bf16[4,128,1536]{2,1,0:T(8,128)(2,1)}), bf16[4,128,1536]{2,1,0:T(8,128)(2,1)S(1)}, u32[]{:S(2)}, u32[]{:S(2)}) async-start(bf16[4,128,1536]{2,1,0:T(8,128)(2,1)} %bitcast.6), calls=%async_computation.3 | async-start | bytes 3145728 | tf_op jit(solution)/shard_map/all_to_all | solution.py:945
  216.9 24.9 %collective-permute-start.15 = (bf16[256,1536]{1,0:T(8,128)(2,1)S(1)}, bf16[256,1536]{1,0:T(8,128)(2,1)S(1)}, u32[]{:S(2)}, u32[]{:S(2)}) collective-permute-start(bf16[256,1536]{1,0:T(8,128)(2,1)S(1)} %fusion.a), channel_id=1, source_target_pairs={{0,8},{4,12},{24,16},{28,20},{1,9},{5,13},{25,17},{29,21},{2,10},{... | collective-permute-start | bytes 2359304 | tf_op jit(solution)/shard_map/ppermute | solution.py:961
  245.2 11.6 %copy-start.6 = (bf16[768,1024]{1,0:T(8,128)(2,1)S(1)}, bf16[768,1024]{1,0:T(8,128)(2,1)}, u32[]{:S(2)}) copy-start(bf16[768,1024]{1,0:T(8,128)(2,1)} %ff1.1.a) | copy-start | bytes 4718596
  245.2 23.5 %all-to-all-start.4 = ((bf16[4,128,1536]{2,1,0:T(8,128)(2,1)}), bf16[4,128,1536]{2,1,0:T(8,128)(2,1)}, u32[]{:S(2)}, u32[]{:S(2)}) async-start(bf16[4,128,1536]{2,1,0:T(8,128)(2,1)} %get-tuple-element.142), calls=%async_computation.4 | async-start | bytes 3145728 | tf_op jit(solution)/shard_map/all_to_all | solution.py:945
  249.9 57.9 %collective-permute-start.20 = (bf16[768,1024]{1,0:T(8,128)(2,1)S(1)}, bf16[768,1024]{1,0:T(8,128)(2,1)}, u32[]{:S(2)}, u32[]{:S(2)}) collective-permute-start(bf16[768,1024]{1,0:T(8,128)(2,1)S(1)} %copy-done.7), channel_id=1, source_target_pairs={{0,8},{4,12},{24,16},{28,20},{1,9},{5,13},{25,17},{29,21},{2,10},{... | collective-permute-start | bytes 4718600 | tf_op jit(solution)/shard_map/ppermute | solution.py:961
  254.7 50.6 %collective-permute-start.17 = (bf16[256,1536]{1,0:T(8,128)(2,1)}, bf16[256,1536]{1,0:T(8,128)(2,1)}, u32[]{:S(2)}, u32[]{:S(2)}) collective-permute-start(bf16[256,1536]{1,0:T(8,128)(2,1)} %fusion.1.a), channel_id=1, source_target_pairs={{0,8},{4,12},{24,16},{28,20},{1,9},{5,13},{25,17},{29,21},{2,10},{... | collective-permute-start | bytes 2359304 | tf_op jit(solution)/shard_map/ppermute | solution.py:961
  256.9 80.2 %collective-permute-start.16 = (bf16[768,1024]{1,0:T(8,128)(2,1)S(1)}, bf16[768,1024]{1,0:T(8,128)(2,1)}, u32[]{:S(2)}, u32[]{:S(2)}) collective-permute-start(bf16[768,1024]{1,0:T(8,128)(2,1)S(1)} %copy-done.6), channel_id=1, source_target_pairs={{0,8},{4,12},{24,16},{28,20},{1,9},{5,13},{25,17},{29,21},{2,10},{... | collective-permute-start | bytes 4718600 | tf_op jit(solution)/shard_map/ppermute | solution.py:961
  259.3 37.0 %collective-permute-start.18 = (bf16[256,1536]{1,0:T(8,128)(2,1)}, bf16[256,1536]{1,0:T(8,128)(2,1)}, u32[]{:S(2)}, u32[]{:S(2)}) collective-permute-start(bf16[256,1536]{1,0:T(8,128)(2,1)} %pair.7.a), channel_id=1, source_target_pairs={{8,16},{12,20},{16,8},{20,12},{9,17},{13,21},{17,9},{21,13},{10,18... | collective-permute-start | bytes 2359304 | tf_op jit(solution)/shard_map/ppermute | solution.py:961
  313.9 26.1 %collective-permute-start.21 = (bf16[768,768]{1,0:T(8,128)(2,1)}, bf16[768,768]{1,0:T(8,128)(2,1)}, u32[]{:S(2)}, u32[]{:S(2)}) collective-permute-start(bf16[768,768]{1,0:T(8,128)(2,1)} %convolution_convert_fusion.3), channel_id=1, source_target_pairs={{0,4},{4,0},{8,12},{12,8},{16,20},{20,16},{24,28},{28,24},{1,5},{5... | collective-permute-start | bytes 3538952 | tf_op jit(solution)/shard_map/ppermute | solution.py:957
  315.8 26.4 %collective-permute-start.22 = (bf16[768,768]{1,0:T(8,128)(2,1)}, bf16[768,768]{1,0:T(8,128)(2,1)}, u32[]{:S(2)}, u32[]{:S(2)}) collective-permute-start(bf16[768,768]{1,0:T(8,128)(2,1)} %convolution_convert_fusion.2), channel_id=1, source_target_pairs={{0,4},{4,0},{8,12},{12,8},{16,20},{20,16},{24,28},{28,24},{1,5},{5... | collective-permute-start | bytes 3538952 | tf_op jit(solution)/shard_map/ppermute | solution.py:957
  316.3 3.4 collective-permute-start.19
  323.1 17.0 %copy-start.19 = (bf16[512,1536]{1,0:T(8,128)(2,1)S(1)}, bf16[512,1536]{1,0:T(8,128)(2,1)}, u32[]{:S(2)}) copy-start(bf16[512,1536]{1,0:T(8,128)(2,1)} %get-tuple-element.148) | copy-start | bytes 4718596
  345.8 33.0 %all-to-all-start.5 = ((bf16[4,384,768]{2,1,0:T(8,128)(2,1)}), bf16[4,384,768]{2,1,0:T(8,128)(2,1)S(1)}, u32[]{:S(2)}, u32[]{:S(2)}) async-start(bf16[4,384,768]{2,1,0:T(8,128)(2,1)} %bitcast.53), calls=%async_computation.5 | async-start | bytes 4718592 | tf_op jit(solution)/shard_map/all_to_all | solution.py:945
  349.8 24.9 %collective-permute-start.24 = (bf16[256,1536]{1,0:T(8,128)(2,1)S(1)}, bf16[256,1536]{1,0:T(8,128)(2,1)}, u32[]{:S(2)}, u32[]{:S(2)}) collective-permute-start(bf16[256,1536]{1,0:T(8,128)(2,1)S(1)} %copy-done.13), channel_id=1, source_target_pairs={{8,0},{12,4},{16,24},{20,28},{9,1},{13,5},{17,25},{21,29},{10,2},{... | collective-permute-start | bytes 2359304 | tf_op jit(solution)/shard_map/ppermute | solution.py:961
  351.1 25.9 %collective-permute-start.23 = (bf16[384,768]{1,0:T(8,128)(2,1)}, bf16[384,768]{1,0:T(8,128)(2,1)}, u32[]{:S(2)}, u32[]{:S(2)}) collective-permute-start(bf16[384,768]{1,0:T(8,128)(2,1)} %convolution_convert_fusion.4), channel_id=1, source_target_pairs={{0,4},{4,0},{8,12},{12,8},{16,20},{20,16},{24,28},{28,24},{1,5},{5... | collective-permute-start | bytes 1769480 | tf_op jit(solution)/shard_map/ppermute | solution.py:957
  351.1 42.6 %collective-permute-start.25 = (bf16[768,1024]{1,0:T(8,128)(2,1)}, bf16[768,1024]{1,0:T(8,128)(2,1)}, u32[]{:S(2)}, u32[]{:S(2)}) collective-permute-start(bf16[768,1024]{1,0:T(8,128)(2,1)} %pair.9.a), channel_id=1, source_target_pairs={{8,16},{12,20},{16,8},{20,12},{9,17},{13,21},{17,9},{21,13},{10,18... | collective-permute-start | bytes 4718600 | tf_op jit(solution)/shard_map/ppermute | solution.py:961
  353.0 45.0 %collective-permute-start.29 = (bf16[768,1024]{1,0:T(8,128)(2,1)}, bf16[768,1024]{1,0:T(8,128)(2,1)}, u32[]{:S(2)}, u32[]{:S(2)}) collective-permute-start(bf16[768,1024]{1,0:T(8,128)(2,1)} %pair.10.a), channel_id=1, source_target_pairs={{8,16},{12,20},{16,8},{20,12},{9,17},{13,21},{17,9},{21,13},{10,18... | collective-permute-start | bytes 4718600 | tf_op jit(solution)/shard_map/ppermute | solution.py:961
  380.9 73.5 %all-to-all-start.6 = ((bf16[4,256,1536]{2,1,0:T(8,128)(2,1)}), bf16[4,256,1536]{2,1,0:T(8,128)(2,1)S(1)}, u32[]{:S(2)}, u32[]{:S(2)}) async-start(bf16[4,256,1536]{2,1,0:T(8,128)(2,1)} %get-tuple-element.164), calls=%async_computation.6 | async-start | bytes 6291456 | tf_op jit(solution)/shard_map/all_to_all | solution.py:945
  384.9 59.6 %collective-permute-start.27 = (bf16[768,768]{1,0:T(8,128)(2,1)}, bf16[768,768]{1,0:T(8,128)(2,1)}, u32[]{:S(2)}, u32[]{:S(2)}) collective-permute-start(bf16[768,768]{1,0:T(8,128)(2,1)} %pad_maximum_fusion.2.a), channel_id=1, source_target_pairs={{0,8},{4,12},{24,16},{28,20},{1,9},{5,13},{25,17},{29,21},{2,10},{... | collective-permute-start | bytes 3538952 | tf_op jit(solution)/shard_map/ppermute | solution.py:961
  392.4 49.7 %collective-permute-start.28 = (bf16[256,1536]{1,0:T(8,128)(2,1)}, bf16[256,1536]{1,0:T(8,128)(2,1)}, u32[]{:S(2)}, u32[]{:S(2)}) collective-permute-start(bf16[256,1536]{1,0:T(8,128)(2,1)} %total.8.a), channel_id=1, source_target_pairs={{8,0},{12,4},{16,24},{20,28},{9,1},{13,5},{17,25},{21,29},{10,2},{... | collective-permute-start | bytes 2359304 | tf_op jit(solution)/shard_map/ppermute | solution.py:961
  396.7 54.9 %collective-permute-start.26 = (bf16[768,1024]{1,0:T(8,128)(2,1)}, bf16[768,1024]{1,0:T(8,128)(2,1)}, u32[]{:S(2)}, u32[]{:S(2)}) collective-permute-start(bf16[768,1024]{1,0:T(8,128)(2,1)} %total.9.a), channel_id=1, source_target_pairs={{8,0},{12,4},{16,24},{20,28},{9,1},{13,5},{17,25},{21,29},{10,2},{... | collective-permute-start | bytes 4718600 | tf_op jit(solution)/shard_map/ppermute | solution.py:961
  400.9 79.5 %collective-permute-start.32 = (bf16[768,1024]{1,0:T(8,128)(2,1)}, bf16[768,1024]{1,0:T(8,128)(2,1)}, u32[]{:S(2)}, u32[]{:S(2)}) collective-permute-start(bf16[768,1024]{1,0:T(8,128)(2,1)} %total.10.a), channel_id=1, source_target_pairs={{8,0},{12,4},{16,24},{20,28},{9,1},{13,5},{17,25},{21,29},{10,2},{... | collective-permute-start | bytes 4718600 | tf_op jit(solution)/shard_map/ppermute | solution.py:961
  404.5 62.0 %collective-permute-start.34 = (bf16[768,768]{1,0:T(8,128)(2,1)}, bf16[768,768]{1,0:T(8,128)(2,1)}, u32[]{:S(2)}, u32[]{:S(2)}) collective-permute-start(bf16[768,768]{1,0:T(8,128)(2,1)} %bitcast.18.a), channel_id=1, source_target_pairs={{0,8},{4,12},{24,16},{28,20},{1,9},{5,13},{25,17},{29,21},{2,10},{... | collective-permute-start | bytes 3538952 | tf_op jit(solution)/shard_map/ppermute | solution.py:961
  444.5 5.3 copy-start.37
  447.1 29.5 %collective-permute-start.33 = (bf16[768,768]{1,0:T(8,128)(2,1)}, bf16[768,768]{1,0:T(8,128)(2,1)}, u32[]{:S(2)}, u32[]{:S(2)}) collective-permute-start(bf16[768,768]{1,0:T(8,128)(2,1)} %pair.11.a), channel_id=1, source_target_pairs={{8,16},{12,20},{16,8},{20,12},{9,17},{13,21},{17,9},{21,13},{10,18... | collective-permute-start | bytes 3538952 | tf_op jit(solution)/shard_map/ppermute | solution.py:961
  469.8 16.7 %all-to-all-start.7 = ((f32[4,6,384]{2,1,0:T(8,128)}), f32[4,6,384]{2,1,0:T(8,128)S(1)}, u32[]{:S(2)}, u32[]{:S(2)}) async-start(f32[4,6,384]{2,1,0:T(8,128)} %pad_maximum_fusion.4), calls=%async_computation.7 | async-start | bytes 98304 | tf_op jit(solution)/shard_map/all_to_all | solution.py:945
  486.5 47.9 %all-to-all-start.8 = ((bf16[4,384,1024]{2,1,0:T(8,128)(2,1)}), bf16[4,384,1024]{2,1,0:T(8,128)(2,1)S(1)}, u32[]{:S(2)}, u32[]{:S(2)}) async-start(bf16[4,384,1024]{2,1,0:T(8,128)(2,1)} %bitcast.52), calls=%async_computation.8 | async-start | bytes 6291456 | tf_op jit(solution)/shard_map/all_to_all | solution.py:945
  490.6 1.2 collective-permute-start.30
  490.6 10.6 %collective-permute-start.35 = (bf16[256,1536]{1,0:T(8,128)(2,1)}, bf16[256,1536]{1,0:T(8,128)(2,1)}, u32[]{:S(2)}, u32[]{:S(2)}) collective-permute-start(bf16[256,1536]{1,0:T(8,128)(2,1)} %result.7.a0), channel_id=1, source_target_pairs={{0,4},{4,0},{8,12},{12,8},{16,20},{20,16},{24,28},{28,24},{1,5},{5... | collective-permute-start | bytes 2359304 | tf_op jit(solution)/shard_map/ppermute | solution.py:957
  491.1 10.1 %collective-permute-start.36 = (bf16[256,1536]{1,0:T(8,128)(2,1)}, bf16[256,1536]{1,0:T(8,128)(2,1)}, u32[]{:S(2)}, u32[]{:S(2)}) collective-permute-start(bf16[256,1536]{1,0:T(8,128)(2,1)} %result.8.a1), channel_id=1, source_target_pairs={{0,4},{4,0},{8,12},{12,8},{16,20},{20,16},{24,28},{28,24},{1,5},{5... | collective-permute-start | bytes 2359304 | tf_op jit(solution)/shard_map/ppermute | solution.py:957
  493.8 17.4 %collective-permute-start.31 = (bf16[400,768]{1,0:T(8,128)(2,1)}, bf16[400,768]{1,0:T(8,128)(2,1)}, u32[]{:S(2)}, u32[]{:S(2)}) collective-permute-start(bf16[400,768]{1,0:T(8,128)(2,1)} %maximum_maximum_fusion.a), channel_id=1, source_target_pairs={{0,8},{4,12},{24,16},{28,20},{1,9},{5,13},{25,17},{29,21},{2,10},{... | collective-permute-start | bytes 1843208 | tf_op jit(solution)/shard_map/ppermute | solution.py:961
  498.2 16.4 %collective-permute-start.39 = (bf16[768,768]{1,0:T(8,128)(2,1)}, bf16[768,768]{1,0:T(8,128)(2,1)}, u32[]{:S(2)}, u32[]{:S(2)}) collective-permute-start(bf16[768,768]{1,0:T(8,128)(2,1)} %pair.12.a), channel_id=1, source_target_pairs={{8,16},{12,20},{16,8},{20,12},{9,17},{13,21},{17,9},{21,13},{10,18... | collective-permute-start | bytes 3538952 | tf_op jit(solution)/shard_map/ppermute | solution.py:961
  499.9 30.0 %collective-permute-start.38 = (bf16[768,768]{1,0:T(8,128)(2,1)}, bf16[768,768]{1,0:T(8,128)(2,1)}, u32[]{:S(2)}, u32[]{:S(2)}) collective-permute-start(bf16[768,768]{1,0:T(8,128)(2,1)} %total.11.a), channel_id=1, source_target_pairs={{8,0},{12,4},{16,24},{20,28},{9,1},{13,5},{17,25},{21,29},{10,2},{... | collective-permute-start | bytes 3538952 | tf_op jit(solution)/shard_map/ppermute | solution.py:961
  513.2 19.2 %collective-permute-start.37 = (bf16[400,768]{1,0:T(8,128)(2,1)}, bf16[400,768]{1,0:T(8,128)(2,1)}, u32[]{:S(2)}, u32[]{:S(2)}) collective-permute-start(bf16[400,768]{1,0:T(8,128)(2,1)} %pair.13.a), channel_id=1, source_target_pairs={{8,16},{12,20},{16,8},{20,12},{9,17},{13,21},{17,9},{21,13},{10,18... | collective-permute-start | bytes 1843208 | tf_op jit(solution)/shard_map/ppermute | solution.py:961
  517.2 41.6 %collective-permute-start.41 = (bf16[768,768]{1,0:T(8,128)(2,1)}, bf16[768,768]{1,0:T(8,128)(2,1)}, u32[]{:S(2)}, u32[]{:S(2)}) collective-permute-start(bf16[768,768]{1,0:T(8,128)(2,1)} %total.12.a), channel_id=1, source_target_pairs={{8,0},{12,4},{16,24},{20,28},{9,1},{13,5},{17,25},{21,29},{10,2},{... | collective-permute-start | bytes 3538952 | tf_op jit(solution)/shard_map/ppermute | solution.py:961
  537.0 24.3 %collective-permute-start.43 = (bf16[2,384,1024]{2,1,0:T(8,128)(2,1)}, bf16[2,384,1024]{2,1,0:T(8,128)(2,1)S(1)}, u32[]{:S(2)}, u32[]{:S(2)}) collective-permute-start(bf16[2,384,1024]{2,1,0:T(8,128)(2,1)} %get-tuple-element.200), channel_id=1, source_target_pairs={{0,4},{4,0},{8,12},{12,8},{16,20},{20,16},{24,28},{28,24},{1,5},{5... | collective-permute-start | bytes 4718600 | tf_op jit(solution)/shard_map/ppermute | solution.py:957
  537.0 24.3 %collective-permute-start.42 = (bf16[2,384,1024]{2,1,0:T(8,128)(2,1)}, bf16[2,384,1024]{2,1,0:T(8,128)(2,1)}, u32[]{:S(2)}, u32[]{:S(2)}) collective-permute-start(bf16[2,384,1024]{2,1,0:T(8,128)(2,1)} %get-tuple-element.201), channel_id=1, source_target_pairs={{0,4},{4,0},{8,12},{12,8},{16,20},{20,16},{24,28},{28,24},{1,5},{5... | collective-permute-start | bytes 4718600 | tf_op jit(solution)/shard_map/ppermute | solution.py:957
  537.6 32.8 %collective-permute-start.40 = (bf16[400,768]{1,0:T(8,128)(2,1)}, bf16[400,768]{1,0:T(8,128)(2,1)}, u32[]{:S(2)}, u32[]{:S(2)}) collective-permute-start(bf16[400,768]{1,0:T(8,128)(2,1)} %total.13.a), channel_id=1, source_target_pairs={{8,0},{12,4},{16,24},{20,28},{9,1},{13,5},{17,25},{21,29},{10,2},{... | collective-permute-start | bytes 1843208 | tf_op jit(solution)/shard_map/ppermute | solution.py:961
  538.8 40.5 %collective-permute-start.44 = (bf16[768,768]{1,0:T(8,128)(2,1)}, bf16[768,768]{1,0:T(8,128)(2,1)S(1)}, u32[]{:S(2)}, u32[]{:S(2)}) collective-permute-start(bf16[768,768]{1,0:T(8,128)(2,1)} %result.11.refs_0_.refs_1_), channel_id=1, source_target_pairs={{0,4},{4,0},{8,12},{12,8},{16,20},{20,16},{24,28},{28,24},{1,5},{5... | collective-permute-start | bytes 3538952 | tf_op jit(solution)/shard_map/ppermute | solution.py:957
  561.4 18.0 %collective-permute-start.45 = (bf16[768,768]{1,0:T(8,128)(2,1)}, bf16[768,768]{1,0:T(8,128)(2,1)S(1)}, u32[]{:S(2)}, u32[]{:S(2)}) collective-permute-start(bf16[768,768]{1,0:T(8,128)(2,1)} %result.12.refs_2_.refs_3_), channel_id=1, source_target_pairs={{0,4},{4,0},{8,12},{12,8},{16,20},{20,16},{24,28},{28,24},{1,5},{5... | collective-permute-start | bytes 3538952 | tf_op jit(solution)/shard_map/ppermute | solution.py:957
  573.5 5.9 collective-permute-start.46
  (33 other events, 82.2 us)
